TPU v7x, 32 devices: a whole 2x2x4 slice. The times are simulated.
32 devices in a mesh: frames: 8 (over z, x), heads: 4 (over y, core).
Axes of the slice: x: 2, y: 2, z: 4, core: 2. Of those that a mesh axis runs over, the one named last changes fastest.
Arguments:
- frames: bfloat16 [8192, 1024], P('frames', 'heads'), may hold values from -6 to 6
- latents: bfloat16 [512, 1024], replicated, may hold values from -6 to 6
- cross_query: bfloat16 [2, 1024, 1024], P(None, None, 'heads'), may hold values from -0.1875 to 0.1875
- cross_key: bfloat16 [2, 1024, 1024], P(None, None, 'heads'), may hold values from -0.1875 to 0.1875
- cross_value: bfloat16 [2, 1024, 1024], P(None, None, 'heads'), may hold values from -0.1875 to 0.1875
- cross_out: bfloat16 [2, 1024, 1024], P(None, 'heads'), may hold values from -0.1875 to 0.1875
- self_query: bfloat16 [2, 1024, 1024], P(None, None, 'heads'), may hold values from -0.1875 to 0.1875
- self_key: bfloat16 [2, 1024, 1024], P(None, None, 'heads'), may hold values from -0.1875 to 0.1875
- self_value: bfloat16 [2, 1024, 1024], P(None, None, 'heads'), may hold values from -0.1875 to 0.1875
- self_out: bfloat16 [2, 1024, 1024], P(None, 'heads'), may hold values from -0.1875 to 0.1875
- mlp_in: bfloat16 [2, 1024, 4096], P(None, None, 'heads'), may hold values from -0.1875 to 0.1875
- mlp_out: bfloat16 [2, 4096, 1024], P(None, 'heads'), may hold values from -0.09375 to 0.09375
Outputs:
- encoded: float32 [512, 1024], P('frames')
- midway: float32 [512, 1024], P(None, 'heads')
All inputs are finite; a program needn't handle non-finite values.
Results may differ from a plain program's by a relative error of at most 0.007.
Values may be sent and summed in bfloat16 or wider, within the bound.
No kernel may reach another device: no remote copies, remote signals or barrier semaphores. Data moves between devices by JAX's collectives and lax.ppermute only.
A program may use at most 64 MiB of HBM per device.

v0:
```python
import functools

import jax
import jax.numpy as jnp
from jax import lax
from jax.experimental import pallas as pl
from jax.experimental.pallas import tpu as pltpu
from jax.sharding import PartitionSpec as P

HEAD_DIM = 64
STATS = 4
VMEM_BYTES = 10 << 20
LOAD_BYTES = 51 << 20
CHUNKS = 2
WIDEST = 8
epsilon = 1e-05
f32, bf16 = jnp.float32, jnp.bfloat16


def shifted(value, axis, step):
    count = lax.axis_size(axis)
    return lax.ppermute(value, axis, [(i, (i + step) % count) for i in range(count)])


def origin(count, widest, k, me):
    return k if count > widest else lax.rem(me - k + count, count)


def gathered_blocks(value, axis):
    count = lax.axis_size(axis)
    if count > WIDEST:
        pieces = lax.all_gather(value, axis)
        return [pieces[k] for k in range(count)]
    return [value] + [shifted(value, axis, k) for k in range(1, count)]


def line_of(count):
    return [list(range(x, count, 2)) for x in range(2)]


def line_shift(value, step):
    count = lax.axis_size("frames")
    return lax.ppermute(value, "frames", [(i, (i + 2 * step) % count) for i in range(count)])


def line_gather(value):
    count = lax.axis_size("frames")
    if count > WIDEST:
        pieces = lax.all_gather(value, "frames", axis_index_groups=line_of(count))
        return [pieces[k] for k in range(count // 2)]
    return [value] + [line_shift(value, k) for k in range(1, count // 2)]


def line_return(blocks):
    count = lax.axis_size("frames")
    if count > WIDEST:
        groups = line_of(count)
        pieces = lax.all_to_all(jnp.stack(blocks), "frames", 0, 0, axis_index_groups=groups)
        return [pieces[k] for k in range(count // 2)]
    return [blocks[0]] + [line_shift(blocks[k], -k) for k in range(1, count // 2)]


def pair_swap(value):
    count = lax.axis_size("frames")
    return lax.ppermute(value, "frames", [(i, i ^ 1) for i in range(count)])


def pass_on(blocks, alongside):
    count = lax.axis_size("heads")
    blocks, alongside = lax.optimization_barrier((blocks, alongside))
    swap = [(i, i ^ 1) for i in range(count)]
    return blocks + [lax.ppermute(block, "heads", swap) for block in blocks], alongside


def whole_call(body, results, *operands, cost=None, unplaced=(), scalars=(), after=(), scratch=(), limit=None):
    space = pl.BlockSpec(memory_space=pltpu.VMEM)
    specs = [pl.BlockSpec(memory_space=pltpu.HBM)] * len(unplaced) + [space] * len(operands)
    specs += [pl.BlockSpec(memory_space=pltpu.SMEM)] * len(scalars) + [space] * len(after)
    scalars = [jnp.asarray(index, jnp.int32).reshape(1, 1) for index in scalars]
    return pl.pallas_call(
        body,
        out_shape=results,
        in_specs=specs,
        out_specs=jax.tree.map(lambda _: space, results),
        scratch_shapes=scratch,
        compiler_params=pltpu.CompilerParams(vmem_limit_bytes=limit or VMEM_BYTES),
        cost_estimate=cost,
    )(*unplaced, *operands, *scalars, *after)


def shaped(shape, dtype):
    return jax.ShapeDtypeStruct(shape, dtype)


def normed(vector):
    centre = vector - jnp.mean(vector, axis=-1, keepdims=True)
    spread_sq = jnp.mean(centre * centre, axis=-1, keepdims=True)
    return (centre * lax.rsqrt(spread_sq + epsilon)).astype(bf16)


def product(left_side, weight):
    return jnp.dot(left_side, weight, preferred_element_type=f32)


def contracted(left_side, right_side, left_dim, right_dim, precision=None):
    return lax.dot_general(
        left_side,
        right_side,
        (((left_dim,), (right_dim,)), ((), ())),
        precision=precision,
        preferred_element_type=f32,
    )


def chunk_kernel(chunk, count, first_half, carried, *refs):
    queries, key_w, value_w = refs[:3]
    blocks, owners, refs = refs[3 : 3 + count], refs[3 + count : 3 + 2 * count], refs[3 + 2 * count :]
    carry, outs = (refs[:2], refs[2:]) if carried else (None, refs)
    out, keys, values = outs[:3]
    rows, width = out.shape[0], blocks[0].shape[1]
    served = queries.at[pl.ds(first_half, queries.shape[0] - first_half), :]
    tile = min(rows, 32)
    for start in range(0, rows, tile):
        pieces = []
        for block in blocks:
            first = start + (chunk * rows if block.shape[0] > rows else 0)
            pieces.append(block[first : first + tile, :].astype(f32))
        mean = jnp.sum(sum(pieces), axis=1, keepdims=True) / (width * count)
        pieces = [piece - mean for piece in pieces]
        total = jnp.sum(sum(piece * piece for piece in pieces), axis=1, keepdims=True)
        scale = lax.rsqrt(total / (width * count) + epsilon)
        for piece, owner in zip(pieces, owners):
            lanes = pl.ds(pl.multiple_of(owner[0, 0] * width, width), width)
            out[start : start + tile, lanes] = (piece * scale).astype(bf16)
    keys[...] = product(out[...], key_w[...]).astype(bf16)
    values[...] = product(out[...], value_w[...]).astype(bf16).T
    for found in weighed(served, [keys], [values], carry, first_half):
        if first_half:
            store_terms(outs[3], *found)
        else:
            store_carry(outs[3], outs[4], *found)


def own_kernel(queries, keys, values, carry_out, carry_stats, out, stats):
    served = queries.at[pl.ds(0, out.shape[1]), :]
    for found in weighed(served, [keys], [values], (carry_out, carry_stats), 0):
        store_carry(out, stats, *found)


def key_value_kernel(p, *refs):
    row_refs, (key_w, value_w, keys, values) = refs[:-4], refs[-4:]
    start = 0
    for rows in row_refs:
        end = start + rows.shape[0]
        keys[start:end, :] = product(rows[...], key_w[p]).astype(bf16)
        values[:, start:end] = product(rows[...], value_w[p]).astype(bf16).T
        start = end


def latents_kernel(scale, count, frames_hbm, key_hbm, value_hbm, latents_hbm, query_hbm, me, *refs):
    state, queries, own, key_w, value_w, latents, query_w, rows_normed, sems = refs
    moves = [
        (latents_hbm, latents),
        (query_hbm.at[0], query_w),
        (frames_hbm, own),
        (key_hbm.at[0], key_w),
        (value_hbm.at[0], value_w),
    ]
    loads = [pltpu.make_async_copy(*move, sems.at[i]) for i, move in enumerate(moves)]
    for load in loads:
        load.start()
    rows = state.shape[0]
    line, side = me[0, 0] // 2, lax.rem(me[0, 0], 2)
    loads[0].wait()
    for j in range(count):
        k = j % (count // 2)
        index = 2 * origin(count // 2, WIDEST // 2, k, line) + (side if j == k else 1 - side)
        value = latents[pl.ds(pl.multiple_of(index * rows, rows), rows), :].astype(f32)
        rows_normed[j * rows : (j + 1) * rows, :] = normed(value)
    state[...] = latents[pl.ds(pl.multiple_of(me[0, 0] * rows, rows), rows), :].astype(f32)
    loads[1].wait()
    queries[...] = (product(rows_normed[...], query_w[...]) * scale).astype(bf16)
    for load in loads[2:]:
        load.wait()


def split_terms(value):
    high = value.astype(bf16).astype(f32)
    return high, (value - high).astype(bf16).astype(f32)


def weighed(queries, key_refs, value_refs, carry, carry_start):
    columns = key_refs[0].shape[1]
    latents = queries.shape[0]
    heads = columns // HEAD_DIM
    chunk = min(latents, 256)
    span = min(columns, 128)
    lane_head = lax.broadcasted_iota(jnp.int32, (chunk, span), 1) // HEAD_DIM

    def scores_of(start, h):
        lanes = slice(h * HEAD_DIM // span * span, (h * HEAD_DIM // span + 1) * span)
        some = queries[start : start + chunk, lanes]
        mine = lane_head == h % (span // HEAD_DIM)
        one = jnp.where(mine, some, jnp.zeros_like(some))
        return [contracted(keys[:, lanes], one, 1, 1) for keys in key_refs]

    order = [(start, h) for start in range(0, latents, chunk) for h in range(heads)]
    coming = scores_of(*order[0])
    for start in range(0, latents, chunk):
        pieces, tops, sums = [], [], []
        for h in range(heads):
            scores, following = coming, order.index((start, h)) + 1
            if following < len(order):
                coming = scores_of(*order[following])
            top = functools.reduce(
                jnp.maximum, [jnp.max(part, axis=0, keepdims=True) for part in scores]
            )
            own = slice(h * HEAD_DIM, (h + 1) * HEAD_DIM)
            place = slice(carry_start + start, carry_start + start + chunk)
            if carry is not None:
                before = carry[1][h : h + 1, place]
                top = jnp.maximum(top, before)
            high, low = split_terms(top)
            top = high + low
            terms = [jnp.exp(part - top) for part in scores]
            total = sum(jnp.sum(part, axis=0, keepdims=True) for part in terms)
            piece = sum(product(v[own, :], part.astype(bf16)) for v, part in zip(value_refs, terms))
            if carry is not None:
                factor = jnp.exp(before - top)
                total += factor * carry[1][heads + h : heads + h + 1, place]
                piece += factor * carry[0][own, place]
            pieces.append(piece)
            tops.append(top)
            sums.append(total)
        yield start, pieces, tops, sums


def store_carry(out, stats, start, pieces, tops, sums):
    for h, rows in enumerate(tops + sums):
        stats[h : h + 1, start : start + rows.shape[1]] = rows
    for h, piece in enumerate(pieces):
        out[h * HEAD_DIM : (h + 1) * HEAD_DIM, start : start + piece.shape[1]] = piece


def split_stats(tops, sums, count):
    tops, sums = [split_terms(top) for top in tops], [split_terms(total) for total in sums]
    rows = [pair[0] for pair in tops] + [pair[1] for pair in tops]
    rows += [pair[0] for pair in sums] + [pair[1] for pair in sums]
    rows += [jnp.zeros_like(rows[0])] * (count - len(rows))
    return jnp.concatenate(rows, axis=0)


def joined_stats(stats, heads):
    return stats[:heads] + stats[heads : 2 * heads], stats[2 * heads : 3 * heads] + stats[3 * heads : 4 * heads]


def store_terms(out, start, pieces, tops, sums):
    place = slice(start, start + pieces[0].shape[1])
    columns = len(pieces) * HEAD_DIM
    out[:columns, place] = jnp.concatenate(pieces, axis=0).astype(bf16)
    out[columns:, place] = split_stats(tops, sums, out.shape[0] - columns).astype(bf16)


def store_packed(outs, rows, start, pieces, tops, sums):
    columns = len(pieces) * HEAD_DIM
    turned = jnp.concatenate(pieces, axis=0).T.astype(bf16)
    stats = split_stats(tops, sums, outs[0].shape[0] - rows)
    for j in range(turned.shape[0] // rows):
        out = outs[start // rows + j]
        out[:rows, :] = turned[j * rows : (j + 1) * rows, :]
        piece = stats[:, j * rows : (j + 1) * rows]
        piece = jnp.concatenate([piece, jnp.zeros((piece.shape[0], columns - rows), f32)], axis=1)
        out[rows:, :] = piece.astype(bf16)


def fold_kernel(rows, carry_out, carry_stats, other, *outs):
    columns, _ = carry_out.shape
    heads = columns // HEAD_DIM
    tops, sums = carry_stats[:heads, :], carry_stats[heads:, :]
    other_tops, other_sums = joined_stats(other[columns:, :].astype(f32), heads)
    highest = jnp.maximum(tops, other_tops)
    factor, other_factor = jnp.exp(tops - highest), jnp.exp(other_tops - highest)
    total = factor * sums + other_factor * other_sums
    pieces = []
    for h in range(heads):
        own = slice(h * HEAD_DIM, (h + 1) * HEAD_DIM)
        piece = factor[h : h + 1] * carry_out[own, :]
        pieces.append(piece + other_factor[h : h + 1] * other[own, :].astype(f32))
    tops = [highest[h : h + 1] for h in range(heads)]
    sums = [total[h : h + 1] for h in range(heads)]
    store_packed(outs, rows, 0, pieces, tops, sums)


def partial_kernel(query_count, rows, *refs):
    query_refs, refs = refs[:query_count], refs[query_count:]
    key_refs, value_refs, outs, share = refs[:2], refs[2:4], refs[4:-1], refs[-1]
    columns = key_refs[0].shape[1]
    queries = jnp.concatenate([ref[:, :columns] for ref in query_refs], axis=0)
    for k, ref in enumerate(query_refs):
        share[k * rows : (k + 1) * rows, :] = ref[:, columns:]
    for found in weighed(queries, key_refs, value_refs, None, 0):
        store_packed(outs, rows, *found)


def merge_kernel(p, *refs):
    parts, weight, out = refs[:-2], refs[-2], refs[-1]
    shards, columns = len(parts), parts[0].shape[1]
    heads = columns // HEAD_DIM
    rows = out.shape[0]
    tops, sums = [], []
    for s in range(shards):
        top, total = joined_stats(parts[s][rows:, :].astype(f32)[:, :rows], heads)
        tops.append(top)
        sums.append(total)
    highest = functools.reduce(jnp.maximum, tops)
    factors = [jnp.exp(top - highest) for top in tops]
    total = sum(factor * one for factor, one in zip(factors, sums))
    factors = jnp.concatenate([factor / total for factor in factors], axis=0)
    shape = (shards * heads, shards * columns)
    row = lax.broadcasted_iota(jnp.int32, shape, 0)
    lane = lax.broadcasted_iota(jnp.int32, shape, 1)
    spreader = (lane // HEAD_DIM == row).astype(f32)
    factors = contracted(factors, spreader, 0, 0, lax.Precision.HIGHEST)
    context = jnp.zeros((rows, columns), f32)
    for s in range(shards):
        context += factors[:, s * columns : (s + 1) * columns] * parts[s][:rows, :].astype(f32)
    out[...] = product(context.astype(bf16), weight[p]).astype(bf16)


def updated(state, parts):
    return state[...] + sum(parts[h].astype(f32) for h in range(parts.shape[0]))


def project_kernel(p, scale, state, parts, query_w, key_w, value_w, new_state, query, both):
    value = updated(state, parts)
    new_state[...] = value
    value = normed(value)
    columns = query_w.shape[2]
    query[...] = (product(value, query_w[p]) * scale).astype(bf16)
    both[:, :columns] = product(value, key_w[p]).astype(bf16)
    both[:, columns:] = product(value, value_w[p]).astype(bf16)


def attend_kernel(p, query, *refs):
    blocks, weight, out = refs[:-2], refs[-2], refs[-1]
    rows, columns = query.shape
    heads = columns // HEAD_DIM
    lane_head = lax.broadcasted_iota(jnp.int32, (rows, columns), 1) // HEAD_DIM
    some = query[...]
    stacked = [jnp.where(lane_head == h, some, jnp.zeros_like(some)) for h in range(heads)]
    stacked = jnp.concatenate(stacked, axis=0)
    scores = [contracted(block[:, :columns], stacked, 1, 1) for block in blocks]
    top = functools.reduce(jnp.maximum, scores)
    top = jnp.max(top, axis=0, keepdims=True)
    terms = [jnp.exp(part - top) for part in scores]
    total = jnp.sum(sum(terms), axis=0, keepdims=True)
    share = jnp.concatenate([(part / total).astype(bf16) for part in terms], axis=0)
    values = jnp.concatenate([block[:, columns:] for block in blocks], axis=0)
    made = contracted(share, values, 0, 0)
    context = jnp.zeros((rows, columns), f32)
    for h in range(heads):
        context = jnp.where(lane_head == h, made[h * rows : (h + 1) * rows, :], context)
    out[...] = product(context.astype(bf16), weight[p]).astype(bf16)


def mlp_kernel(p, state, parts, in_w, out_w, new_state, out):
    value = updated(state, parts)
    new_state[...] = value
    hidden = product(normed(value), in_w[p])
    hidden = 0.5 * hidden * (1.0 + lax.erf(hidden * 0.5**0.5))
    out[...] = product(hidden.astype(bf16), out_w[p]).astype(bf16)


def query_kernel(p, scale, state, parts, query_w, index, new_state, message):
    value = updated(state, parts)
    new_state[...] = value
    columns = query_w.shape[2]
    message[:, :columns] = (product(normed(value), query_w[p]) * scale).astype(bf16)
    own = new_state[:, pl.ds(pl.multiple_of(index[0, 0] * columns, columns), columns)]
    message[:, columns:] = own.astype(bf16)


def final_kernel(count, state, parts, share, other_share, me, new_state, midway):
    new_state[...] = updated(state, parts)
    rows = new_state.shape[0]
    line, side = me[0, 0] // 2, lax.rem(me[0, 0], 2)
    for k in range(count // 2):
        place_of = 2 * origin(count // 2, WIDEST // 2, k, line)
        for block, at in ((share, place_of + side), (other_share, place_of + 1 - side)):
            start = pl.multiple_of(at * rows, rows)
            midway[pl.ds(start, rows), :] = block[k * rows : (k + 1) * rows, :].astype(f32)


def local(
    frames,
    latents,
    cross_query,
    cross_key,
    cross_value,
    cross_out,
    self_query,
    self_key,
    self_value,
    self_out,
    mlp_in,
    mlp_out,
):
    scale = 1.0 / HEAD_DIM**0.5
    passes, width, columns = cross_query.shape
    shards, me = lax.axis_size("frames"), lax.axis_index("frames")
    latent_count = latents.shape[0]
    rows = latent_count // shards
    stat_rows = -(-STATS * (columns // HEAD_DIM) // 16) * 16
    state_shape = shaped((rows, width), f32)
    part_shape = shaped((rows, width), bf16)
    row_shape = shaped((rows, columns), bf16)
    double_shape = shaped((rows, 2 * columns), bf16)
    packed_shape = shaped((rows + stat_rows, columns), bf16)
    state, queries, own, key_w, value_w = whole_call(
        functools.partial(latents_kernel, scale, shards),
        (
            state_shape,
            shaped((latent_count, columns), bf16),
            shaped(frames.shape, bf16),
            shaped((width, columns), bf16),
            shaped((width, columns), bf16),
        ),
        unplaced=(frames, cross_key, cross_value, latents, cross_query),
        scalars=(me,),
        scratch=[
            pltpu.VMEM((latent_count, width), bf16),
            pltpu.VMEM((width, columns), bf16),
            pltpu.VMEM((latent_count, width), bf16),
            pltpu.SemaphoreType.DMA((5,)),
        ],
        limit=LOAD_BYTES,
        cost=pl.CostEstimate(
            flops=2 * latent_count * width * columns,
            bytes_accessed=2 * latent_count * width,
            transcendentals=0,
        ),
    )
    frame_count = frames.shape[0]
    chunks = CHUNKS
    part_rows = frame_count // chunks
    count, side = lax.axis_size("heads"), lax.axis_index("heads")
    steps = range(2, count, 2)
    owners = [side, side ^ 1] + [(side - k) % count for k in steps]
    owners = owners + [((side ^ 1) - k) % count for k in steps]
    far = []
    for c in range(chunks):
        piece = lax.slice_in_dim(frames, c * part_rows, (c + 1) * part_rows, axis=0)
        far.append([shifted(piece, "heads", k) for k in steps])
    near = lax.ppermute(frames, "heads", [(i, i ^ 1) for i in range(count)])
    heads = columns // HEAD_DIM
    line_latents = latent_count // 2
    line_shape = shaped((columns + stat_rows, line_latents), bf16)
    results = [
        shaped((part_rows, width), bf16),
        shaped((part_rows, columns), bf16),
        shaped((columns, part_rows), bf16),
    ]

    def carry_of(latent_rows):
        return [shaped((columns, latent_rows), f32), shaped((2 * heads, latent_rows), f32)]

    pieces, carry = [], []
    for c in range(chunks):
        last = c + 1 == chunks
        served = line_latents if last else latent_count
        if c == 0:
            blocks, queries = pass_on(far[c], queries)
        else:
            blocks, pieces[-1] = pass_on(far[c], pieces[-1])
        made = whole_call(
            functools.partial(chunk_kernel, c, count, line_latents if last else 0, c > 0),
            results + ([line_shape] if last else carry_of(latent_count)),
            queries,
            key_w,
            value_w,
            own,
            near,
            *blocks,
            scalars=owners,
            after=carry,
            cost=pl.CostEstimate(
                flops=4 * part_rows * width * columns,
                bytes_accessed=2 * part_rows * width,
                transcendentals=heads * served * part_rows,
            ),
        )
        pieces.append(made[:3])
        if not last:
            carry = made[3:]
    other = pair_swap(made[3])
    carry = whole_call(
        own_kernel,
        carry_of(line_latents),
        queries,
        *made[1:3],
        *carry,
        cost=pl.CostEstimate(
            flops=4 * line_latents * part_rows * columns,
            bytes_accessed=4 * latent_count * columns,
            transcendentals=heads * line_latents * part_rows,
        ),
    )
    line_count = shards // 2
    first_parts = whole_call(
        functools.partial(fold_kernel, rows), [packed_shape] * line_count, *carry, other
    )
    key_values = [None] + [
        whole_call(
            functools.partial(key_value_kernel, p),
            (shaped((frame_count, columns), bf16), shaped((columns, frame_count), bf16)),
            *[piece[0] for piece in pieces],
            cross_key,
            cross_value,
            cost=pl.CostEstimate(
                flops=4 * frame_count * width * columns,
                bytes_accessed=2 * frame_count * width,
                transcendentals=0,
            ),
        )
        for p in range(1, passes)
    ]
    for p in range(passes):
        if p == 0:
            parts = line_return(first_parts)
        else:
            keys, values = key_values[p]
            results = [packed_shape] * len(queries) + [shaped((rows * len(queries), columns), bf16)]
            *parts, share = whole_call(
                functools.partial(partial_kernel, len(queries), rows),
                results,
                *queries,
                keys,
                pair_swap(keys),
                values,
                pair_swap(values),
            )
            parts = line_return(parts)
            if p == 1:
                first_share = share
        part = whole_call(functools.partial(merge_kernel, p), part_shape, *parts, cross_out)
        state, query, both = whole_call(
            functools.partial(project_kernel, p, scale),
            (state_shape, row_shape, double_shape),
            state,
            lax.all_gather(part, "heads"),
            self_query,
            self_key,
            self_value,
        )
        if shards > WIDEST:
            blocks = gathered_blocks(both, "frames")
        else:
            blocks = line_gather(both)
            blocks = blocks + [pair_swap(block) for block in blocks]
        part = whole_call(functools.partial(attend_kernel, p), part_shape, query, *blocks, self_out)
        state, part = whole_call(
            functools.partial(mlp_kernel, p),
            (state_shape, part_shape),
            state,
            lax.all_gather(part, "heads"),
            mlp_in,
            mlp_out,
        )
        part = lax.all_gather(part, "heads")
        if p + 1 < passes:
            state, message = whole_call(
                functools.partial(query_kernel, p + 1, scale),
                (state_shape, double_shape),
                state,
                part,
                cross_query,
                scalars=(lax.axis_index("heads"),),
            )
            queries = line_gather(message)
        else:
            state, midway = whole_call(
                functools.partial(final_kernel, shards),
                (state_shape, shaped((latent_count, columns), f32)),
                state,
                part,
                first_share,
                pair_swap(first_share),
                scalars=(me,),
            )
    return (state, midway)


def solution(mesh):
    columns, rows = P(None, None, "heads"), P(None, "heads", None)
    placed = (P("frames", "heads"), P(), columns, columns, columns, rows)
    placed = placed + (columns, columns, columns, rows, columns, rows)
    return jax.shard_map(
        local,
        mesh=mesh,
        in_specs=placed,
        out_specs=(P("frames", None), P(None, "heads")),
        check_vma=False,
    )
```

profile of v0, /device:TPU:0, one launch (start us, length us, event | category | flops | bytes accessed | tf_op | source)
XLA Modules:
  0.0 141.6 jit_solution(8737030229244226264)
XLA Ops:
  0.6 1.8 %fusion = (bf16[512,256]{1,0:T(8,128)(2,1)}, bf16[512,256]{1,0:T(8,128)(2,1)}) fusion(bf16[1024,256]{1,0:T(8,128)(2,1)} %frames_hbm.1), kind=kLoop, calls=%fused_computation | loop fusion | bytes 1048576 | tf_op jit(solution)/shard_map/slice | solution.py:452
  2.5 3.0 %collective-permute-start = (bf16[512,256]{1,0:T(8,128)(2,1)}, bf16[512,256]{1,0:T(8,128)(2,1)}, u32[]{:S(2)}, u32[]{:S(2)}) collective-permute-start(bf16[512,256]{1,0:T(8,128)(2,1)} %get-tuple-element.85), channel_id=1, source_target_pairs={{0,2},{1,3},{2,0},{3,1},{4,6},{5,7},{6,4},{7,5},{8,10},{9,11},{10,... | collective-permute-start | bytes 786440 | tf_op jit(solution)/shard_map/ppermute | solution.py:22
  5.5 1.0 copy-done.10
  6.5 2.3 %shard_map.131 = (f32[64,1024]{1,0:T(8,128)S(1)}, bf16[512,256]{1,0:T(8,128)(2,1)S(1)}, bf16[1024,256]{1,0:T(8,128)(2,1)S(1)}, bf16[1024,256]{1,0:T(8,128)(2,1)S(1)}, bf16[1024,256]{1,0:T(8,128)(2,1)S(1)}) custom-call(bf16[1024,256]{1,0:T(8,128)(2,1)S(1)} %copy-done.10, bf16[2,1024,256]{2,1,0:T(8,128)(2,1)} %refs_2_.1, bf16[2,1024,256]{2,1,0:T(8,128)(2,1)} %refs_3_.1, ...), custom_call_target="tpu_custom_call" | custom-call | flops 268435456 | bytes 1048576 | tf_op jit(solution)/shard_map/pallas_call | solution.py:80
  9.5 2.6 %collective-permute-done.refs_5_ = bf16[512,256]{1,0:T(8,128)(2,1)} collective-permute-done((bf16[512,256]{1,0:T(8,128)(2,1)}, bf16[512,256]{1,0:T(8,128)(2,1)}, u32[]{:S(2)}, u32[]{:S(2)}) %collective-permute-start) | collective-permute-done | bytes 262176 | tf_op jit(solution)/shard_map/ppermute | solution.py:22
  12.1 1.7 %collective-permute-start.2 = (bf16[512,256]{1,0:T(8,128)(2,1)}, bf16[512,256]{1,0:T(8,128)(2,1)}, u32[]{:S(2)}, u32[]{:S(2)}) collective-permute-start(bf16[512,256]{1,0:T(8,128)(2,1)} %get-tuple-element.84), channel_id=1, source_target_pairs={{0,2},{1,3},{2,0},{3,1},{4,6},{5,7},{6,4},{7,5},{8,10},{9,11},{10,... | collective-permute-start | bytes 786440 | tf_op jit(solution)/shard_map/ppermute | solution.py:22
  14.0 5.0 %shard_map.132 = (bf16[512,1024]{1,0:T(8,128)(2,1)S(1)}, bf16[512,256]{1,0:T(8,128)(2,1)}, bf16[256,512]{1,0:T(8,128)(2,1)}, f32[256,512]{1,0:T(8,128)S(1)}, f32[8,512]{1,0:T(8,128)S(1)}) custom-call(bf16[512,256]{1,0:T(8,128)(2,1)S(1)} %get-tuple-element.45.refs_0_.queries, bf16[1024,256]{1,0:T(8,128)(2,1)S(1)} %get-tuple-element.46.refs_1_, ...), custom_call_target="tpu_custom_call" | custom-call | flops 536870912 | bytes 1048576 | tf_op jit(solution)/shard_map/pallas_call | solution.py:80
  19.0 2.1 %collective-permute-done.2.refs_5_ = bf16[512,256]{1,0:T(8,128)(2,1)} collective-permute-done((bf16[512,256]{1,0:T(8,128)(2,1)}, bf16[512,256]{1,0:T(8,128)(2,1)}, u32[]{:S(2)}, u32[]{:S(2)}) %collective-permute-start.2) | collective-permute-done | bytes 262176 | tf_op jit(solution)/shard_map/ppermute | solution.py:22
  21.1 1.7 %collective-permute-done.4.refs_6_ = bf16[512,256]{1,0:T(8,128)(2,1)S(1)} collective-permute-done((bf16[512,256]{1,0:T(8,128)(2,1)}, bf16[512,256]{1,0:T(8,128)(2,1)S(1)}, u32[]{:S(2)}, u32[]{:S(2)}) %collective-permute-start.4) | collective-permute-done | bytes 262176 | tf_op jit(solution)/shard_map/ppermute | solution.py:72
  22.9 3.4 %shard_map.133 = (bf16[512,1024]{1,0:T(8,128)(2,1)S(1)}, bf16[512,256]{1,0:T(8,128)(2,1)S(1)}, bf16[256,512]{1,0:T(8,128)(2,1)S(1)}, bf16[272,256]{1,0:T(8,128)(2,1)S(1)}) custom-call(bf16[512,256]{1,0:T(8,128)(2,1)S(1)} %get-tuple-element.45.refs_0_.queries, bf16[1024,256]{1,0:T(8,128)(2,1)S(1)} %get-tuple-element.46.refs_1_, ...), custom_call_target="tpu_custom_call" | custom-call | flops 536870912 | bytes 1048576 | tf_op jit(solution)/shard_map/pallas_call | solution.py:80
  26.3 1.8 %collective-permute-start.5 = (bf16[272,256]{1,0:T(8,128)(2,1)S(1)}, bf16[272,256]{1,0:T(8,128)(2,1)S(1)}, u32[]{:S(2)}, u32[]{:S(2)}) collective-permute-start(bf16[272,256]{1,0:T(8,128)(2,1)S(1)} %get-tuple-element.58), channel_id=1, source_target_pairs={{0,4},{4,0},{8,12},{12,8},{16,20},{20,16},{24,28},{28,24},{1,5},{5... | collective-permute-start | bytes 417800 | tf_op jit(solution)/shard_map/ppermute | solution.py:65
  28.1 1.2 shard_map.134
  29.3 2.8 %collective-permute-done.5.other = bf16[272,256]{1,0:T(8,128)(2,1)S(1)} collective-permute-done((bf16[272,256]{1,0:T(8,128)(2,1)S(1)}, bf16[272,256]{1,0:T(8,128)(2,1)S(1)}, u32[]{:S(2)}, u32[]{:S(2)}) %collective-permute-start.5) | collective-permute-done | bytes 139296 | tf_op jit(solution)/shard_map/ppermute | solution.py:65
  32.2 3.9 %collective-permute-start.6 = (bf16[80,256]{1,0:T(8,128)(2,1)S(1)}, bf16[80,256]{1,0:T(8,128)(2,1)S(1)}, u32[]{:S(2)}, u32[]{:S(2)}) collective-permute-start(bf16[80,256]{1,0:T(8,128)(2,1)S(1)} %get-tuple-element.60), channel_id=1, source_target_pairs={{0,24},{4,28},{8,0},{12,4},{16,8},{20,12},{24,16},{28,20},{1,25},{... | collective-permute-start | bytes 122888 | tf_op jit(solution)/shard_map/ppermute | solution.py:43
  37.7 3.2 %collective-permute-done.7.refs_2_ = bf16[80,256]{1,0:T(8,128)(2,1)S(1)} collective-permute-done((bf16[80,256]{1,0:T(8,128)(2,1)S(1)}, bf16[80,256]{1,0:T(8,128)(2,1)S(1)}, u32[]{:S(2)}, u32[]{:S(2)}) %collective-permute-start.7) | collective-permute-done | bytes 40992 | tf_op jit(solution)/shard_map/ppermute | solution.py:43
  42.5 7.2 %all-gather = bf16[256,1024]{1,0:T(8,128)(2,1)S(1)} all-gather(bf16[64,1024]{1,0:T(8,128)(2,1)S(1)} %shard_map.136), channel_id=2, replica_groups=mesh['frames'=8,'heads'=4] {'heads'}, dimensions={0}, use_global_device_ids=true | all-gather | bytes 655360 | tf_op jit(solution)/shard_map/all_gather | solution.py:550
  51.6 1.9 %collective-permute-start.9 = (bf16[64,512]{1,0:T(8,128)(2,1)S(1)}, bf16[64,512]{1,0:T(8,128)(2,1)S(1)}, u32[]{:S(2)}, u32[]{:S(2)}) collective-permute-start(bf16[64,512]{1,0:T(8,128)(2,1)S(1)} %get-tuple-element.65.refs_0_), channel_id=1, source_target_pairs={{0,8},{4,12},{8,16},{12,20},{16,24},{20,28},{24,0},{28,4},{1,9},{5... | collective-permute-start | bytes 196616 | tf_op jit(solution)/shard_map/ppermute | solution.py:43
  53.5 1.5 %collective-permute-start.12 = (bf16[64,512]{1,0:T(8,128)(2,1)S(1)}, bf16[64,512]{1,0:T(8,128)(2,1)S(1)}, u32[]{:S(2)}, u32[]{:S(2)}) collective-permute-start(bf16[64,512]{1,0:T(8,128)(2,1)S(1)} %get-tuple-element.65.refs_0_), channel_id=1, source_target_pairs={{0,4},{4,0},{8,12},{12,8},{16,20},{20,16},{24,28},{28,24},{1,5},{5... | collective-permute-start | bytes 196616 | tf_op jit(solution)/shard_map/ppermute | solution.py:65
  55.4 1.5 %collective-permute-start.15 = (bf16[64,512]{1,0:T(8,128)(2,1)S(1)}, bf16[64,512]{1,0:T(8,128)(2,1)S(1)}, u32[]{:S(2)}, u32[]{:S(2)}) collective-permute-start(bf16[64,512]{1,0:T(8,128)(2,1)S(1)} %collective-permute-done.11.refs_3_), channel_id=1, source_target_pairs={{0,4},{4,0},{8,12},{12,8},{16,20},{20,16},{24,28},{28,24},{1,5},{5... | collective-permute-start | bytes 196616 | tf_op jit(solution)/shard_map/ppermute | solution.py:65
  56.9 2.0 %collective-permute-done.10.refs_2_ = bf16[64,512]{1,0:T(8,128)(2,1)S(1)} collective-permute-done((bf16[64,512]{1,0:T(8,128)(2,1)S(1)}, bf16[64,512]{1,0:T(8,128)(2,1)S(1)}, u32[]{:S(2)}, u32[]{:S(2)}) %collective-permute-start.10) | collective-permute-done | bytes 65568 | tf_op jit(solution)/shard_map/ppermute | solution.py:43
  58.9 1.5 %collective-permute-start.14 = (bf16[64,512]{1,0:T(8,128)(2,1)S(1)}, bf16[64,512]{1,0:T(8,128)(2,1)S(1)}, u32[]{:S(2)}, u32[]{:S(2)}) collective-permute-start(bf16[64,512]{1,0:T(8,128)(2,1)S(1)} %collective-permute-done.10.refs_2_), channel_id=1, source_target_pairs={{0,4},{4,0},{8,12},{12,8},{16,20},{20,16},{24,28},{28,24},{1,5},{5... | collective-permute-start | bytes 196616 | tf_op jit(solution)/shard_map/ppermute | solution.py:65
  60.9 1.3 shard_map.141
  62.3 1.6 %collective-permute-start.19 = (bf16[1024,256]{1,0:T(8,128)(2,1)S(1)}, bf16[1024,256]{1,0:T(8,128)(2,1)S(1)}, u32[]{:S(2)}, u32[]{:S(2)}) collective-permute-start(bf16[1024,256]{1,0:T(8,128)(2,1)S(1)} %get-tuple-element.72.refs_4_), channel_id=1, source_target_pairs={{0,4},{4,0},{8,12},{12,8},{16,20},{20,16},{24,28},{28,24},{1,5},{5... | collective-permute-start | bytes 1572872 | tf_op jit(solution)/shard_map/ppermute | solution.py:65
  65.4 1.0 shard_map.138
  66.4 6.7 %all-gather.1 = bf16[256,1024]{1,0:T(8,128)(2,1)S(1)} all-gather(bf16[64,1024]{1,0:T(8,128)(2,1)S(1)} %shard_map.138), channel_id=3, replica_groups=mesh['frames'=8,'heads'=4] {'heads'}, dimensions={0}, use_global_device_ids=true | all-gather | bytes 655360 | tf_op jit(solution)/shard_map/all_gather | solution.py:565
  73.1 1.1 shard_map.139
  74.2 7.3 %all-gather.2 = bf16[256,1024]{1,0:T(8,128)(2,1)S(1)} all-gather(bf16[64,1024]{1,0:T(8,128)(2,1)S(1)} %get-tuple-element.67), channel_id=4, replica_groups=mesh['frames'=8,'heads'=4] {'heads'}, dimensions={0}, use_global_device_ids=true | all-gather | bytes 655360 | tf_op jit(solution)/shard_map/all_gather | solution.py:569
  82.7 1.3 collective-permute-start.16
  84.0 2.3 %collective-permute-done.18.refs_3_ = bf16[64,512]{1,0:T(8,128)(2,1)S(1)} collective-permute-done((bf16[64,512]{1,0:T(8,128)(2,1)S(1)}, bf16[64,512]{1,0:T(8,128)(2,1)S(1)}, u32[]{:S(2)}, u32[]{:S(2)}) %collective-permute-start.18) | collective-permute-done | bytes 65568 | tf_op jit(solution)/shard_map/ppermute | solution.py:43
  86.2 4.2 %collective-permute-done.17.refs_2_ = bf16[64,512]{1,0:T(8,128)(2,1)S(1)} collective-permute-done((bf16[64,512]{1,0:T(8,128)(2,1)S(1)}, bf16[64,512]{1,0:T(8,128)(2,1)S(1)}, u32[]{:S(2)}, u32[]{:S(2)}) %collective-permute-start.17) | collective-permute-done | bytes 65568 | tf_op jit(solution)/shard_map/ppermute | solution.py:43
  90.5 3.2 %shard_map.142 = (bf16[80,256]{1,0:T(8,128)(2,1)S(1)}, bf16[80,256]{1,0:T(8,128)(2,1)S(1)}, bf16[80,256]{1,0:T(8,128)(2,1)S(1)}, bf16[80,256]{1,0:T(8,128)(2,1)S(1)}, bf16[256,256]{1,0:T(8,128)(2,1)S(1)}) custom-call(bf16[64,512]{1,0:T(8,128)(2,1)S(1)} %get-tuple-element.69.refs_0_, bf16[64,512]{1,0:T(8,128)(2,1)S(1)} %collective-permute-done.16.refs_1_, ...), custom_call_target="tpu_custom_call" | custom-call | tf_op jit(solution)/shard_map/pallas_call | solution.py:80
  93.7 1.3 collective-permute-start.21
  95.3 1.9 %collective-permute-start.23 = (bf16[80,256]{1,0:T(8,128)(2,1)S(1)}, bf16[80,256]{1,0:T(8,128)(2,1)S(1)}, u32[]{:S(2)}, u32[]{:S(2)}) collective-permute-start(bf16[80,256]{1,0:T(8,128)(2,1)S(1)} %get-tuple-element.77), channel_id=1, source_target_pairs={{0,8},{4,12},{8,16},{12,20},{16,24},{20,28},{24,0},{28,4},{1,9},{5... | collective-permute-start | bytes 122888 | tf_op jit(solution)/shard_map/ppermute | solution.py:43
  97.8 2.7 %collective-permute-done.22.refs_2_ = bf16[80,256]{1,0:T(8,128)(2,1)S(1)} collective-permute-done((bf16[80,256]{1,0:T(8,128)(2,1)S(1)}, bf16[80,256]{1,0:T(8,128)(2,1)S(1)}, u32[]{:S(2)}, u32[]{:S(2)}) %collective-permute-start.22) | collective-permute-done | bytes 40992 | tf_op jit(solution)/shard_map/ppermute | solution.py:43
  101.7 6.9 %all-gather.3 = bf16[256,1024]{1,0:T(8,128)(2,1)S(1)} all-gather(bf16[64,1024]{1,0:T(8,128)(2,1)S(1)} %shard_map.143), channel_id=5, replica_groups=mesh['frames'=8,'heads'=4] {'heads'}, dimensions={0}, use_global_device_ids=true | all-gather | bytes 655360 | tf_op jit(solution)/shard_map/all_gather | solution.py:550
  109.1 1.4 %collective-permute-start.26 = (bf16[64,512]{1,0:T(8,128)(2,1)S(1)}, bf16[64,512]{1,0:T(8,128)(2,1)S(1)}, u32[]{:S(2)}, u32[]{:S(2)}) collective-permute-start(bf16[64,512]{1,0:T(8,128)(2,1)S(1)} %get-tuple-element.80.refs_0_), channel_id=1, source_target_pairs={{0,24},{4,28},{8,0},{12,4},{16,8},{20,12},{24,16},{28,20},{1,25},{... | collective-permute-start | bytes 196616 | tf_op jit(solution)/shard_map/ppermute | solution.py:43
  110.8 1.3 collective-permute-start.24
  112.1 1.2 collective-permute-start.27
  113.5 1.3 collective-permute-start.30
  114.8 3.5 %collective-permute-done.25.refs_2_ = bf16[64,512]{1,0:T(8,128)(2,1)S(1)} collective-permute-done((bf16[64,512]{1,0:T(8,128)(2,1)S(1)}, bf16[64,512]{1,0:T(8,128)(2,1)S(1)}, u32[]{:S(2)}, u32[]{:S(2)}) %collective-permute-start.25) | collective-permute-done | bytes 65568 | tf_op jit(solution)/shard_map/ppermute | solution.py:43
  118.3 1.1 collective-permute-start.29
  120.4 1.1 collective-permute-start.31
  121.4 1.9 %collective-permute-done.29.refs_6_ = bf16[64,512]{1,0:T(8,128)(2,1)S(1)} collective-permute-done((bf16[64,512]{1,0:T(8,128)(2,1)S(1)}, bf16[64,512]{1,0:T(8,128)(2,1)S(1)}, u32[]{:S(2)}, u32[]{:S(2)}) %collective-permute-start.29) | collective-permute-done | bytes 65568 | tf_op jit(solution)/shard_map/ppermute | solution.py:65
  123.3 1.4 collective-permute-done.28.refs_5_
  124.7 1.0 shard_map.145
  125.7 6.5 %all-gather.4 = bf16[256,1024]{1,0:T(8,128)(2,1)S(1)} all-gather(bf16[64,1024]{1,0:T(8,128)(2,1)S(1)} %shard_map.145), channel_id=6, replica_groups=mesh['frames'=8,'heads'=4] {'heads'}, dimensions={0}, use_global_device_ids=true | all-gather | bytes 655360 | tf_op jit(solution)/shard_map/all_gather | solution.py:565
  132.2 1.1 shard_map.146
  133.3 7.3 %all-gather.5 = bf16[256,1024]{1,0:T(8,128)(2,1)S(1)} all-gather(bf16[64,1024]{1,0:T(8,128)(2,1)S(1)} %get-tuple-element.82), channel_id=7, replica_groups=mesh['frames'=8,'heads'=4] {'heads'}, dimensions={0}, use_global_device_ids=true | all-gather | bytes 655360 | tf_op jit(solution)/shard_map/all_gather | solution.py:569
  (66 shorter events, 14.8 us)
Async XLA Ops:
  2.5 9.6 %collective-permute-start = (bf16[512,256]{1,0:T(8,128)(2,1)}, bf16[512,256]{1,0:T(8,128)(2,1)}, u32[]{:S(2)}, u32[]{:S(2)}) collective-permute-start(bf16[512,256]{1,0:T(8,128)(2,1)} %get-tuple-element.85), channel_id=1, source_target_pairs={{0,2},{1,3},{2,0},{3,1},{4,6},{5,7},{6,4},{7,5},{8,10},{9,11},{10,... | collective-permute-start | bytes 786440 | tf_op jit(solution)/shard_map/ppermute | solution.py:22
  5.5 8.4 %collective-permute-start.1 = (bf16[1024,256]{1,0:T(8,128)(2,1)}, bf16[1024,256]{1,0:T(8,128)(2,1)S(1)}, u32[]{:S(2)}, u32[]{:S(2)}) collective-permute-start(bf16[1024,256]{1,0:T(8,128)(2,1)} %frames_hbm.1), channel_id=1, source_target_pairs={{0,1},{1,0},{2,3},{3,2},{4,5},{5,4},{6,7},{7,6},{8,9},{9,8},{10,11... | collective-permute-start | bytes 1572872 | tf_op jit(solution)/shard_map/ppermute | solution.py:454
  5.5 1.0 copy-start.10
  8.8 0.7 copy-start.11
  9.5 32.4 %copy-start.5 = (bf16[2,256,1024]{2,1,0:T(8,128)(2,1)S(1)}, bf16[2,256,1024]{2,1,0:T(8,128)(2,1)}, u32[]{:S(2)}) copy-start(bf16[2,256,1024]{2,1,0:T(8,128)(2,1)} %refs_4_.3) | copy-start | bytes 3145732
  12.1 1.9 %collective-permute-start.3 = (bf16[512,256]{1,0:T(8,128)(2,1)}, bf16[512,256]{1,0:T(8,128)(2,1)}, u32[]{:S(2)}, u32[]{:S(2)}) collective-permute-start(bf16[512,256]{1,0:T(8,128)(2,1)} %collective-permute-done.refs_5_), channel_id=1, source_target_pairs={{0,1},{1,0},{2,3},{3,2},{4,5},{5,4},{6,7},{7,6},{8,9},{9,8},{10,11... | collective-permute-start | bytes 786440 | tf_op jit(solution)/shard_map/ppermute | solution.py:72
  12.1 9.0 %collective-permute-start.2 = (bf16[512,256]{1,0:T(8,128)(2,1)}, bf16[512,256]{1,0:T(8,128)(2,1)}, u32[]{:S(2)}, u32[]{:S(2)}) collective-permute-start(bf16[512,256]{1,0:T(8,128)(2,1)} %get-tuple-element.84), channel_id=1, source_target_pairs={{0,2},{1,3},{2,0},{3,1},{4,6},{5,7},{6,4},{7,5},{8,10},{9,11},{10,... | collective-permute-start | bytes 786440 | tf_op jit(solution)/shard_map/ppermute | solution.py:22
  19.0 30.7 %copy-start.7 = (bf16[2,1024,256]{2,1,0:T(8,128)(2,1)S(1)}, bf16[2,1024,256]{2,1,0:T(8,128)(2,1)}, u32[]{:S(2)}) copy-start(bf16[2,1024,256]{2,1,0:T(8,128)(2,1)} %query_w.5) | copy-start | bytes 3145732
  19.0 30.7 %copy-start.8 = (bf16[2,1024,256]{2,1,0:T(8,128)(2,1)S(1)}, bf16[2,1024,256]{2,1,0:T(8,128)(2,1)}, u32[]{:S(2)}) copy-start(bf16[2,1024,256]{2,1,0:T(8,128)(2,1)} %key_w.3) | copy-start | bytes 3145732
  19.0 30.7 %copy-start.9 = (bf16[2,1024,256]{2,1,0:T(8,128)(2,1)S(1)}, bf16[2,1024,256]{2,1,0:T(8,128)(2,1)}, u32[]{:S(2)}) copy-start(bf16[2,1024,256]{2,1,0:T(8,128)(2,1)} %value_w.3) | copy-start | bytes 3145732
  19.0 30.7 %copy-start.12 = (f32[64,1024]{1,0:T(8,128)S(1)}, f32[64,1024]{1,0:T(8,128)}, u32[]{:S(2)}) copy-start(f32[64,1024]{1,0:T(8,128)} %copy-done.11) | copy-start | bytes 786436
  21.1 1.7 %collective-permute-start.4 = (bf16[512,256]{1,0:T(8,128)(2,1)}, bf16[512,256]{1,0:T(8,128)(2,1)S(1)}, u32[]{:S(2)}, u32[]{:S(2)}) collective-permute-start(bf16[512,256]{1,0:T(8,128)(2,1)} %collective-permute-done.2.refs_5_), channel_id=1, source_target_pairs={{0,1},{1,0},{2,3},{3,2},{4,5},{5,4},{6,7},{7,6},{8,9},{9,8},{10,11... | collective-permute-start | bytes 786440 | tf_op jit(solution)/shard_map/ppermute | solution.py:72
  26.3 34.7 %copy-start.3 = (bf16[2,1024,256]{2,1,0:T(8,128)(2,1)S(1)}, bf16[2,1024,256]{2,1,0:T(8,128)(2,1)}, u32[]{:S(2)}) copy-start(bf16[2,1024,256]{2,1,0:T(8,128)(2,1)} %refs_2_.1) | copy-start | bytes 3145732
  26.3 34.7 %copy-start.4 = (bf16[2,1024,256]{2,1,0:T(8,128)(2,1)S(1)}, bf16[2,1024,256]{2,1,0:T(8,128)(2,1)}, u32[]{:S(2)}) copy-start(bf16[2,1024,256]{2,1,0:T(8,128)(2,1)} %refs_3_.1) | copy-start | bytes 3145732
  26.3 5.8 %collective-permute-start.5 = (bf16[272,256]{1,0:T(8,128)(2,1)S(1)}, bf16[272,256]{1,0:T(8,128)(2,1)S(1)}, u32[]{:S(2)}, u32[]{:S(2)}) collective-permute-start(bf16[272,256]{1,0:T(8,128)(2,1)S(1)} %get-tuple-element.58), channel_id=1, source_target_pairs={{0,4},{4,0},{8,12},{12,8},{16,20},{20,16},{24,28},{28,24},{1,5},{5... | collective-permute-start | bytes 417800 | tf_op jit(solution)/shard_map/ppermute | solution.py:65
  32.2 5.5 %collective-permute-start.6 = (bf16[80,256]{1,0:T(8,128)(2,1)S(1)}, bf16[80,256]{1,0:T(8,128)(2,1)S(1)}, u32[]{:S(2)}, u32[]{:S(2)}) collective-permute-start(bf16[80,256]{1,0:T(8,128)(2,1)S(1)} %get-tuple-element.60), channel_id=1, source_target_pairs={{0,24},{4,28},{8,0},{12,4},{16,8},{20,12},{24,16},{28,20},{1,25},{... | collective-permute-start | bytes 122888 | tf_op jit(solution)/shard_map/ppermute | solution.py:43
  36.1 4.9 %collective-permute-start.7 = (bf16[80,256]{1,0:T(8,128)(2,1)S(1)}, bf16[80,256]{1,0:T(8,128)(2,1)S(1)}, u32[]{:S(2)}, u32[]{:S(2)}) collective-permute-start(bf16[80,256]{1,0:T(8,128)(2,1)S(1)} %get-tuple-element.61), channel_id=1, source_target_pairs={{0,16},{4,20},{8,24},{12,28},{16,0},{20,4},{24,8},{28,12},{1,17},{... | collective-permute-start | bytes 122888 | tf_op jit(solution)/shard_map/ppermute | solution.py:43
  36.1 5.8 %collective-permute-start.8 = (bf16[80,256]{1,0:T(8,128)(2,1)S(1)}, bf16[80,256]{1,0:T(8,128)(2,1)S(1)}, u32[]{:S(2)}, u32[]{:S(2)}) collective-permute-start(bf16[80,256]{1,0:T(8,128)(2,1)S(1)} %get-tuple-element.62), channel_id=1, source_target_pairs={{0,8},{4,12},{8,16},{12,20},{16,24},{20,28},{24,0},{28,4},{1,9},{5... | collective-permute-start | bytes 122888 | tf_op jit(solution)/shard_map/ppermute | solution.py:43
  49.7 15.7 %copy-start.6 = (bf16[2,256,1024]{2,1,0:T(8,128)(2,1)S(1)}, bf16[2,256,1024]{2,1,0:T(8,128)(2,1)}, u32[]{:S(2)}) copy-start(bf16[2,256,1024]{2,1,0:T(8,128)(2,1)} %refs_8_.3) | copy-start | bytes 3145732
  49.7 23.4 %copy-start.1 = (bf16[2,1024,1024]{2,1,0:T(8,128)(2,1)S(1)}, bf16[2,1024,1024]{2,1,0:T(8,128)(2,1)}, u32[]{:S(2)}) copy-start(bf16[2,1024,1024]{2,1,0:T(8,128)(2,1)} %out_w.3) | copy-start | bytes 12582916
  50.3 22.8 %copy-start = (bf16[2,1024,1024]{2,1,0:T(8,128)(2,1)S(1)}, bf16[2,1024,1024]{2,1,0:T(8,128)(2,1)}, u32[]{:S(2)}) copy-start(bf16[2,1024,1024]{2,1,0:T(8,128)(2,1)} %in_w.3) | copy-start | bytes 12582916
  50.3 5.1 %collective-permute-start.11 = (bf16[64,512]{1,0:T(8,128)(2,1)S(1)}, bf16[64,512]{1,0:T(8,128)(2,1)S(1)}, u32[]{:S(2)}, u32[]{:S(2)}) collective-permute-start(bf16[64,512]{1,0:T(8,128)(2,1)S(1)} %get-tuple-element.65.refs_0_), channel_id=1, source_target_pairs={{0,24},{4,28},{8,0},{12,4},{16,8},{20,12},{24,16},{28,20},{1,25},{... | collective-permute-start | bytes 196616 | tf_op jit(solution)/shard_map/ppermute | solution.py:43
  51.0 7.9 %collective-permute-start.10 = (bf16[64,512]{1,0:T(8,128)(2,1)S(1)}, bf16[64,512]{1,0:T(8,128)(2,1)S(1)}, u32[]{:S(2)}, u32[]{:S(2)}) collective-permute-start(bf16[64,512]{1,0:T(8,128)(2,1)S(1)} %get-tuple-element.65.refs_0_), channel_id=1, source_target_pairs={{0,16},{4,20},{8,24},{12,28},{16,0},{20,4},{24,8},{28,12},{1,17},{... | collective-permute-start | bytes 196616 | tf_op jit(solution)/shard_map/ppermute | solution.py:43
  51.6 8.8 %collective-permute-start.9 = (bf16[64,512]{1,0:T(8,128)(2,1)S(1)}, bf16[64,512]{1,0:T(8,128)(2,1)S(1)}, u32[]{:S(2)}, u32[]{:S(2)}) collective-permute-start(bf16[64,512]{1,0:T(8,128)(2,1)S(1)} %get-tuple-element.65.refs_0_), channel_id=1, source_target_pairs={{0,8},{4,12},{8,16},{12,20},{16,24},{20,28},{24,0},{28,4},{1,9},{5... | collective-permute-start | bytes 196616 | tf_op jit(solution)/shard_map/ppermute | solution.py:43
  53.5 10.3 %collective-permute-start.12 = (bf16[64,512]{1,0:T(8,128)(2,1)S(1)}, bf16[64,512]{1,0:T(8,128)(2,1)S(1)}, u32[]{:S(2)}, u32[]{:S(2)}) collective-permute-start(bf16[64,512]{1,0:T(8,128)(2,1)S(1)} %get-tuple-element.65.refs_0_), channel_id=1, source_target_pairs={{0,4},{4,0},{8,12},{12,8},{16,20},{20,16},{24,28},{28,24},{1,5},{5... | collective-permute-start | bytes 196616 | tf_op jit(solution)/shard_map/ppermute | solution.py:65
  55.4 8.9 %collective-permute-start.15 = (bf16[64,512]{1,0:T(8,128)(2,1)S(1)}, bf16[64,512]{1,0:T(8,128)(2,1)S(1)}, u32[]{:S(2)}, u32[]{:S(2)}) collective-permute-start(bf16[64,512]{1,0:T(8,128)(2,1)S(1)} %collective-permute-done.11.refs_3_), channel_id=1, source_target_pairs={{0,4},{4,0},{8,12},{12,8},{16,20},{20,16},{24,28},{28,24},{1,5},{5... | collective-permute-start | bytes 196616 | tf_op jit(solution)/shard_map/ppermute | solution.py:65
  58.9 5.5 %collective-permute-start.14 = (bf16[64,512]{1,0:T(8,128)(2,1)S(1)}, bf16[64,512]{1,0:T(8,128)(2,1)S(1)}, u32[]{:S(2)}, u32[]{:S(2)}) collective-permute-start(bf16[64,512]{1,0:T(8,128)(2,1)S(1)} %collective-permute-done.10.refs_2_), channel_id=1, source_target_pairs={{0,4},{4,0},{8,12},{12,8},{16,20},{20,16},{24,28},{28,24},{1,5},{5... | collective-permute-start | bytes 196616 | tf_op jit(solution)/shard_map/ppermute | solution.py:65
  60.4 5.0 %collective-permute-start.13 = (bf16[64,512]{1,0:T(8,128)(2,1)S(1)}, bf16[64,512]{1,0:T(8,128)(2,1)S(1)}, u32[]{:S(2)}, u32[]{:S(2)}) collective-permute-start(bf16[64,512]{1,0:T(8,128)(2,1)S(1)} %collective-permute-done.9.refs_1_), channel_id=1, source_target_pairs={{0,4},{4,0},{8,12},{12,8},{16,20},{20,16},{24,28},{28,24},{1,5},{5... | collective-permute-start | bytes 196616 | tf_op jit(solution)/shard_map/ppermute | solution.py:65
  62.3 28.2 %collective-permute-start.19 = (bf16[1024,256]{1,0:T(8,128)(2,1)S(1)}, bf16[1024,256]{1,0:T(8,128)(2,1)S(1)}, u32[]{:S(2)}, u32[]{:S(2)}) collective-permute-start(bf16[1024,256]{1,0:T(8,128)(2,1)S(1)} %get-tuple-element.72.refs_4_), channel_id=1, source_target_pairs={{0,4},{4,0},{8,12},{12,8},{16,20},{20,16},{24,28},{28,24},{1,5},{5... | collective-permute-start | bytes 1572872 | tf_op jit(solution)/shard_map/ppermute | solution.py:65
  63.8 26.7 %collective-permute-start.20 = (bf16[256,1024]{1,0:T(8,128)(2,1)S(1)}, bf16[256,1024]{1,0:T(8,128)(2,1)S(1)}, u32[]{:S(2)}, u32[]{:S(2)}) collective-permute-start(bf16[256,1024]{1,0:T(8,128)(2,1)S(1)} %get-tuple-element.73.refs_6_), channel_id=1, source_target_pairs={{0,4},{4,0},{8,12},{12,8},{16,20},{20,16},{24,28},{28,24},{1,5},{5... | collective-permute-start | bytes 1572872 | tf_op jit(solution)/shard_map/ppermute | solution.py:65
  73.1 8.3 %copy-start.2 = (bf16[2,1024,256]{2,1,0:T(8,128)(2,1)S(1)}, bf16[2,1024,256]{2,1,0:T(8,128)(2,1)}, u32[]{:S(2)}) copy-start(bf16[2,1024,256]{2,1,0:T(8,128)(2,1)} %query_w.4) | copy-start | bytes 3145732
  81.8 4.4 %collective-permute-start.18 = (bf16[64,512]{1,0:T(8,128)(2,1)S(1)}, bf16[64,512]{1,0:T(8,128)(2,1)S(1)}, u32[]{:S(2)}, u32[]{:S(2)}) collective-permute-start(bf16[64,512]{1,0:T(8,128)(2,1)S(1)} %get-tuple-element.69.refs_0_), channel_id=1, source_target_pairs={{0,24},{4,28},{8,0},{12,4},{16,8},{20,12},{24,16},{28,20},{1,25},{... | collective-permute-start | bytes 196616 | tf_op jit(solution)/shard_map/ppermute | solution.py:43
  82.7 7.8 %collective-permute-start.17 = (bf16[64,512]{1,0:T(8,128)(2,1)S(1)}, bf16[64,512]{1,0:T(8,128)(2,1)S(1)}, u32[]{:S(2)}, u32[]{:S(2)}) collective-permute-start(bf16[64,512]{1,0:T(8,128)(2,1)S(1)} %get-tuple-element.69.refs_0_), channel_id=1, source_target_pairs={{0,16},{4,20},{8,24},{12,28},{16,0},{20,4},{24,8},{28,12},{1,17},{... | collective-permute-start | bytes 196616 | tf_op jit(solution)/shard_map/ppermute | solution.py:43
  82.7 7.8 %collective-permute-start.16 = (bf16[64,512]{1,0:T(8,128)(2,1)S(1)}, bf16[64,512]{1,0:T(8,128)(2,1)S(1)}, u32[]{:S(2)}, u32[]{:S(2)}) collective-permute-start(bf16[64,512]{1,0:T(8,128)(2,1)S(1)} %get-tuple-element.69.refs_0_), channel_id=1, source_target_pairs={{0,8},{4,12},{8,16},{12,20},{16,24},{20,28},{24,0},{28,4},{1,9},{5... | collective-permute-start | bytes 196616 | tf_op jit(solution)/shard_map/ppermute | solution.py:43
  93.7 4.1 %collective-permute-start.21 = (bf16[80,256]{1,0:T(8,128)(2,1)S(1)}, bf16[80,256]{1,0:T(8,128)(2,1)S(1)}, u32[]{:S(2)}, u32[]{:S(2)}) collective-permute-start(bf16[80,256]{1,0:T(8,128)(2,1)S(1)} %get-tuple-element.75), channel_id=1, source_target_pairs={{0,24},{4,28},{8,0},{12,4},{16,8},{20,12},{24,16},{28,20},{1,25},{... | collective-permute-start | bytes 122888 | tf_op jit(solution)/shard_map/ppermute | solution.py:43
  95.0 5.4 %collective-permute-start.22 = (bf16[80,256]{1,0:T(8,128)(2,1)S(1)}, bf16[80,256]{1,0:T(8,128)(2,1)S(1)}, u32[]{:S(2)}, u32[]{:S(2)}) collective-permute-start(bf16[80,256]{1,0:T(8,128)(2,1)S(1)} %get-tuple-element.76), channel_id=1, source_target_pairs={{0,16},{4,20},{8,24},{12,28},{16,0},{20,4},{24,8},{28,12},{1,17},{... | collective-permute-start | bytes 122888 | tf_op jit(solution)/shard_map/ppermute | solution.py:43
  95.3 5.8 %collective-permute-start.23 = (bf16[80,256]{1,0:T(8,128)(2,1)S(1)}, bf16[80,256]{1,0:T(8,128)(2,1)S(1)}, u32[]{:S(2)}, u32[]{:S(2)}) collective-permute-start(bf16[80,256]{1,0:T(8,128)(2,1)S(1)} %get-tuple-element.77), channel_id=1, source_target_pairs={{0,8},{4,12},{8,16},{12,20},{16,24},{20,28},{24,0},{28,4},{1,9},{5... | collective-permute-start | bytes 122888 | tf_op jit(solution)/shard_map/ppermute | solution.py:43
  109.1 4.4 %collective-permute-start.26 = (bf16[64,512]{1,0:T(8,128)(2,1)S(1)}, bf16[64,512]{1,0:T(8,128)(2,1)S(1)}, u32[]{:S(2)}, u32[]{:S(2)}) collective-permute-start(bf16[64,512]{1,0:T(8,128)(2,1)S(1)} %get-tuple-element.80.refs_0_), channel_id=1, source_target_pairs={{0,24},{4,28},{8,0},{12,4},{16,8},{20,12},{24,16},{28,20},{1,25},{... | collective-permute-start | bytes 196616 | tf_op jit(solution)/shard_map/ppermute | solution.py:43
  110.5 7.8 %collective-permute-start.25 = (bf16[64,512]{1,0:T(8,128)(2,1)S(1)}, bf16[64,512]{1,0:T(8,128)(2,1)S(1)}, u32[]{:S(2)}, u32[]{:S(2)}) collective-permute-start(bf16[64,512]{1,0:T(8,128)(2,1)S(1)} %get-tuple-element.80.refs_0_), channel_id=1, source_target_pairs={{0,16},{4,20},{8,24},{12,28},{16,0},{20,4},{24,8},{28,12},{1,17},{... | collective-permute-start | bytes 196616 | tf_op jit(solution)/shard_map/ppermute | solution.py:43
  110.8 8.6 %collective-permute-start.24 = (bf16[64,512]{1,0:T(8,128)(2,1)S(1)}, bf16[64,512]{1,0:T(8,128)(2,1)S(1)}, u32[]{:S(2)}, u32[]{:S(2)}) collective-permute-start(bf16[64,512]{1,0:T(8,128)(2,1)S(1)} %get-tuple-element.80.refs_0_), channel_id=1, source_target_pairs={{0,8},{4,12},{8,16},{12,20},{16,24},{20,28},{24,0},{28,4},{1,9},{5... | collective-permute-start | bytes 196616 | tf_op jit(solution)/shard_map/ppermute | solution.py:43
  112.1 9.3 %collective-permute-start.27 = (bf16[64,512]{1,0:T(8,128)(2,1)S(1)}, bf16[64,512]{1,0:T(8,128)(2,1)S(1)}, u32[]{:S(2)}, u32[]{:S(2)}) collective-permute-start(bf16[64,512]{1,0:T(8,128)(2,1)S(1)} %get-tuple-element.80.refs_0_), channel_id=1, source_target_pairs={{0,4},{4,0},{8,12},{12,8},{16,20},{20,16},{24,28},{28,24},{1,5},{5... | collective-permute-start | bytes 196616 | tf_op jit(solution)/shard_map/ppermute | solution.py:65
  113.5 7.9 %collective-permute-start.30 = (bf16[64,512]{1,0:T(8,128)(2,1)S(1)}, bf16[64,512]{1,0:T(8,128)(2,1)S(1)}, u32[]{:S(2)}, u32[]{:S(2)}) collective-permute-start(bf16[64,512]{1,0:T(8,128)(2,1)S(1)} %collective-permute-done.26.refs_3_), channel_id=1, source_target_pairs={{0,4},{4,0},{8,12},{12,8},{16,20},{20,16},{24,28},{28,24},{1,5},{5... | collective-permute-start | bytes 196616 | tf_op jit(solution)/shard_map/ppermute | solution.py:65
  118.3 5.0 %collective-permute-start.29 = (bf16[64,512]{1,0:T(8,128)(2,1)S(1)}, bf16[64,512]{1,0:T(8,128)(2,1)S(1)}, u32[]{:S(2)}, u32[]{:S(2)}) collective-permute-start(bf16[64,512]{1,0:T(8,128)(2,1)S(1)} %collective-permute-done.25.refs_2_), channel_id=1, source_target_pairs={{0,4},{4,0},{8,12},{12,8},{16,20},{20,16},{24,28},{28,24},{1,5},{5... | collective-permute-start | bytes 196616 | tf_op jit(solution)/shard_map/ppermute | solution.py:65
  119.4 5.3 %collective-permute-start.28 = (bf16[64,512]{1,0:T(8,128)(2,1)S(1)}, bf16[64,512]{1,0:T(8,128)(2,1)S(1)}, u32[]{:S(2)}, u32[]{:S(2)}) collective-permute-start(bf16[64,512]{1,0:T(8,128)(2,1)S(1)} %collective-permute-done.24.refs_1_), channel_id=1, source_target_pairs={{0,4},{4,0},{8,12},{12,8},{16,20},{20,16},{24,28},{28,24},{1,5},{5... | collective-permute-start | bytes 196616 | tf_op jit(solution)/shard_map/ppermute | solution.py:65
  120.4 20.2 %collective-permute-start.31 = (bf16[256,256]{1,0:T(8,128)(2,1)S(1)}, bf16[256,256]{1,0:T(8,128)(2,1)S(1)}, u32[]{:S(2)}, u32[]{:S(2)}) collective-permute-start(bf16[256,256]{1,0:T(8,128)(2,1)S(1)} %get-tuple-element.83.share), channel_id=1, source_target_pairs={{0,4},{4,0},{8,12},{12,8},{16,20},{20,16},{24,28},{28,24},{1,5},{5... | collective-permute-start | bytes 393224 | tf_op jit(solution)/shard_map/ppermute | solution.py:65
where the time goes:
time: 142 us
  blocking collectives  41.8 us (29%)
  starting transfers between devices  35.9 us (25%)
  waiting for transfers between devices  34.9 us (25%)
  Pallas kernels  24.5 us (17%)
  local copies, waits for them, and re-layouts  3.63 us (3%)
    all_gather x4, blocking collectives, local(): lax.all_gather(part, 'heads')  27.3 us
    pallas_call x17, Pallas kernels, whole_call(): pl.pallas_call(body, out_shape=results, in_specs=specs, out_specs=jax.tre...  24.5 us
    ppermute x15, waiting for transfers between devices, line_shift(): lax.ppermute(value, 'frames', [(i, (i + 2 * step) % count) for i in range...  21.3 us
    ppermute x15, starting transfers between devices, line_shift(): lax.ppermute(value, 'frames', [(i, (i + 2 * step) % count) for i in range...  16.7 us
    all_gather x2, blocking collectives, local(): part = lax.all_gather(part, 'heads')  14.6 us
    ppermute x12, starting transfers between devices, pair_swap(): return lax.ppermute(value, 'frames', [(i, i ^ 1) for i in range(count)])  14.5 us
    ppermute x12, waiting for transfers between devices, pair_swap(): return lax.ppermute(value, 'frames', [(i, i ^ 1) for i in range(count)])  7.09 us
    ppermute x2, starting transfers between devices, shifted(): lax.ppermute(value, axis, [(i, (i + step) % count) for i in range(count)])  4.74 us
  transfers between devices with their start and end apart: 32, of which 20 were waited for; matrix products, arithmetic and copies ran while one was open for 0% of the time, Pallas kernels for 10%

commit v1 on v0

--- a/solution.py
+++ b/solution.py
@@ -116,6 +116,7 @@
     queries, key_w, value_w = refs[:3]
     blocks, owners, refs = refs[3 : 3 + count], refs[3 + count : 3 + 2 * count], refs[3 + 2 * count :]
     carry, outs = (refs[:2], refs[2:]) if carried else (None, refs)
+    outs = outs if first_half else (outs[0], outs[3], outs[4], outs[1], outs[2])
     out, keys, values = outs[:3]
     rows, width = out.shape[0], blocks[0].shape[1]
     served = queries.at[pl.ds(first_half, queries.shape[0] - first_half), :]
@@ -328,10 +329,18 @@
 
 
 def updated(state, parts):
-    return state[...] + sum(parts[h].astype(f32) for h in range(parts.shape[0]))
-
-
-def project_kernel(p, scale, state, parts, query_w, key_w, value_w, new_state, query, both):
+    terms = [part[...].astype(f32) for part in parts]
+    while len(terms) > 1:
+        terms = [first + second for first, second in zip(terms[0::2], terms[1::2])]
+    return state[...] + terms[0]
+
+
+def add_kernel(part, other, out):
+    out[...] = (part[...].astype(f32) + other[...].astype(f32)).astype(bf16)
+
+
+def project_kernel(p, scale, state, *refs):
+    parts, (query_w, key_w, value_w, new_state, query, both) = refs[:-6], refs[-6:]
     value = updated(state, parts)
     new_state[...] = value
     value = normed(value)
@@ -363,7 +372,8 @@
     out[...] = product(context.astype(bf16), weight[p]).astype(bf16)
 
 
-def mlp_kernel(p, state, parts, in_w, out_w, new_state, out):
+def mlp_kernel(p, state, *refs):
+    parts, (in_w, out_w, new_state, out) = refs[:-4], refs[-4:]
     value = updated(state, parts)
     new_state[...] = value
     hidden = product(normed(value), in_w[p])
@@ -371,7 +381,8 @@
     out[...] = product(hidden.astype(bf16), out_w[p]).astype(bf16)
 
 
-def query_kernel(p, scale, state, parts, query_w, index, new_state, message):
+def query_kernel(p, scale, state, *refs):
+    parts, (query_w, index, new_state, message) = refs[:-4], refs[-4:]
     value = updated(state, parts)
     new_state[...] = value
     columns = query_w.shape[2]
@@ -380,7 +391,8 @@
     message[:, columns:] = own.astype(bf16)
 
 
-def final_kernel(count, state, parts, share, other_share, me, new_state, midway):
+def final_kernel(count, state, *refs):
+    parts, (share, other_share, me, new_state, midway) = refs[:-5], refs[-5:]
     new_state[...] = updated(state, parts)
     rows = new_state.shape[0]
     line, side = me[0, 0] // 2, lax.rem(me[0, 0], 2)
@@ -389,6 +401,16 @@
         for block, at in ((share, place_of + side), (other_share, place_of + 1 - side)):
             start = pl.multiple_of(at * rows, rows)
             midway[pl.ds(start, rows), :] = block[k * rows : (k + 1) * rows, :].astype(f32)
+
+
+def heads_parts(part):
+    count = lax.axis_size("heads")
+
+    def from_bits(value, bits):
+        return lax.ppermute(value, "heads", [(i, i ^ bits) for i in range(count)])
+
+    both = whole_call(add_kernel, shaped(part.shape, bf16), part, from_bits(part, 1))
+    return [both] + [from_bits(both, bits) for bits in range(2, count, 2)]
 
 
 def local(
@@ -474,7 +496,7 @@
             blocks, pieces[-1] = pass_on(far[c], pieces[-1])
         made = whole_call(
             functools.partial(chunk_kernel, c, count, line_latents if last else 0, c > 0),
-            results + ([line_shape] if last else carry_of(latent_count)),
+            results + [line_shape] if last else results[:1] + carry_of(latent_count),
             queries,
             key_w,
             value_w,
@@ -483,15 +505,16 @@
             *blocks,
             scalars=owners,
             after=carry,
+            scratch=[] if last else [pltpu.VMEM(one.shape, one.dtype) for one in results[1:]],
             cost=pl.CostEstimate(
                 flops=4 * part_rows * width * columns,
                 bytes_accessed=2 * part_rows * width,
                 transcendentals=heads * served * part_rows,
             ),
         )
-        pieces.append(made[:3])
+        pieces.append(made[:1])
         if not last:
-            carry = made[3:]
+            carry = made[1:]
     other = pair_swap(made[3])
     carry = whole_call(
         own_kernel,
@@ -547,7 +570,7 @@
             functools.partial(project_kernel, p, scale),
             (state_shape, row_shape, double_shape),
             state,
-            lax.all_gather(part, "heads"),
+            *heads_parts(part),
             self_query,
             self_key,
             self_value,
@@ -562,17 +585,17 @@
             functools.partial(mlp_kernel, p),
             (state_shape, part_shape),
             state,
-            lax.all_gather(part, "heads"),
+            *heads_parts(part),
             mlp_in,
             mlp_out,
         )
-        part = lax.all_gather(part, "heads")
+        parts = heads_parts(part)
         if p + 1 < passes:
             state, message = whole_call(
                 functools.partial(query_kernel, p + 1, scale),
                 (state_shape, double_shape),
                 state,
-                part,
+                *parts,
                 cross_query,
                 scalars=(lax.axis_index("heads"),),
             )
@@ -582,7 +605,7 @@
                 functools.partial(final_kernel, shards),
                 (state_shape, shaped((latent_count, columns), f32)),
                 state,
-                part,
+                *parts,
                 first_share,
                 pair_swap(first_share),
                 scalars=(me,),

time: 142 us -> 141 us (level)
  blocking collectives: 41.8 us -> 0 us
  waiting for transfers between devices: 34.9 us -> 68.5 us
  starting transfers between devices: 35.9 us -> 43.8 us
    all_gather x6 -> x0, blocking collectives: 41.8 us -> none  [the longest x4 27.3 us: local(): lax.all_gather(part, 'heads')]
    ppermute x0 -> x12, waiting for transfers between devices: none -> 26.4 us  [from_bits(): return lax.ppermute(value, 'heads', [(i, i ^ bits) for i in range(count)])]
    ppermute x12, waiting for transfers between devices: 7.09 us -> 19.8 us  [pair_swap(): return lax.ppermute(value, 'frames', [(i, i ^ 1) for i in range(count)])]
    ppermute x0 -> x12, starting transfers between devices: none -> 9.93 us  [from_bits(): return lax.ppermute(value, 'heads', [(i, i ^ bits) for i in range(count)])]
    ppermute x15, waiting for transfers between devices: 21.3 us -> 15.3 us  [line_shift(): lax.ppermute(value, 'frames', [(i, (i + 2 * step) % count) for i in range...]
    pallas_call x17 -> x23, Pallas kernels: 24.5 us -> 24.1 us  [whole_call(): pl.pallas_call(body, out_shape=results, in_specs=specs, out_specs=jax.tre...]
  transfers between devices with their start and end apart: 32 -> 44, of which waited for: 20 -> 31; matrix products, arithmetic and copies ran while one was open for 0% -> 0% of each run, Pallas kernels for 10% -> 8%
where the time goes in v1:
time: 141 us
  waiting for transfers between devices  68.5 us (49%)
  starting transfers between devices  43.8 us (31%)
  Pallas kernels  24.1 us (17%)
  local copies, waits for them, and re-layouts  3.64 us (3%)
    ppermute x12, waiting for transfers between devices, from_bits(): return lax.ppermute(value, 'heads', [(i, i ^ bits) for i in range(count)])  26.4 us
    pallas_call x23, Pallas kernels, whole_call(): pl.pallas_call(body, out_shape=results, in_specs=specs, out_specs=jax.tre...  24.1 us
    ppermute x12, waiting for transfers between devices, pair_swap(): return lax.ppermute(value, 'frames', [(i, i ^ 1) for i in range(count)])  19.8 us
    ppermute x15, starting transfers between devices, line_shift(): lax.ppermute(value, 'frames', [(i, (i + 2 * step) % count) for i in range...  15.4 us
    ppermute x15, waiting for transfers between devices, line_shift(): lax.ppermute(value, 'frames', [(i, (i + 2 * step) % count) for i in range...  15.3 us
    ppermute x12, starting transfers between devices, pair_swap(): return lax.ppermute(value, 'frames', [(i, i ^ 1) for i in range(count)])  13.7 us
    ppermute x12, starting transfers between devices, from_bits(): return lax.ppermute(value, 'heads', [(i, i ^ bits) for i in range(count)])  9.93 us
    ppermute x2, waiting for transfers between devices, shifted(): lax.ppermute(value, axis, [(i, (i + step) % count) for i in range(count)])  5.12 us
  transfers between devices with their start and end apart: 44, of which 31 were waited for; matrix products, arithmetic and copies ran while one was open for 0% of the time, Pallas kernels for 8%

profile of v1, /device:TPU:0, one launch (start us, length us, event | category | flops | bytes accessed | tf_op | source)
XLA Modules:
  0.0 141.0 jit_solution(13588100420039347400)
XLA Ops:
  0.6 1.9 %fusion = (bf16[512,256]{1,0:T(8,128)(2,1)}, bf16[512,256]{1,0:T(8,128)(2,1)}) fusion(bf16[1024,256]{1,0:T(8,128)(2,1)} %frames_hbm.1), kind=kLoop, calls=%fused_computation | loop fusion | bytes 1048576 | tf_op jit(solution)/shard_map/slice | solution.py:474
  2.5 3.0 %collective-permute-start = (bf16[512,256]{1,0:T(8,128)(2,1)}, bf16[512,256]{1,0:T(8,128)(2,1)}, u32[]{:S(2)}, u32[]{:S(2)}) collective-permute-start(bf16[512,256]{1,0:T(8,128)(2,1)} %get-tuple-element.85), channel_id=1, source_target_pairs={{0,2},{1,3},{2,0},{3,1},{4,6},{5,7},{6,4},{7,5},{8,10},{9,11},{10,... | collective-permute-start | bytes 786440 | tf_op jit(solution)/shard_map/ppermute | solution.py:22
  6.5 2.3 %shard_map.131 = (f32[64,1024]{1,0:T(8,128)S(1)}, bf16[512,256]{1,0:T(8,128)(2,1)S(1)}, bf16[1024,256]{1,0:T(8,128)(2,1)S(1)}, bf16[1024,256]{1,0:T(8,128)(2,1)S(1)}, bf16[1024,256]{1,0:T(8,128)(2,1)S(1)}) custom-call(bf16[1024,256]{1,0:T(8,128)(2,1)S(1)} %copy-done.10, bf16[2,1024,256]{2,1,0:T(8,128)(2,1)} %refs_2_.9, bf16[2,1024,256]{2,1,0:T(8,128)(2,1)} %refs_3_.7, ...), custom_call_target="tpu_custom_call" | custom-call | flops 268435456 | bytes 1048576 | tf_op jit(solution)/shard_map/pallas_call | solution.py:80
  9.5 2.6 %collective-permute-done.refs_5_ = bf16[512,256]{1,0:T(8,128)(2,1)} collective-permute-done((bf16[512,256]{1,0:T(8,128)(2,1)}, bf16[512,256]{1,0:T(8,128)(2,1)}, u32[]{:S(2)}, u32[]{:S(2)}) %collective-permute-start) | collective-permute-done | bytes 262176 | tf_op jit(solution)/shard_map/ppermute | solution.py:22
  12.1 1.7 %collective-permute-start.2 = (bf16[512,256]{1,0:T(8,128)(2,1)}, bf16[512,256]{1,0:T(8,128)(2,1)}, u32[]{:S(2)}, u32[]{:S(2)}) collective-permute-start(bf16[512,256]{1,0:T(8,128)(2,1)} %get-tuple-element.84), channel_id=1, source_target_pairs={{0,2},{1,3},{2,0},{3,1},{4,6},{5,7},{6,4},{7,5},{8,10},{9,11},{10,... | collective-permute-start | bytes 786440 | tf_op jit(solution)/shard_map/ppermute | solution.py:22
  14.0 4.6 %shard_map.132 = (bf16[512,1024]{1,0:T(8,128)(2,1)S(1)}, f32[256,512]{1,0:T(8,128)S(1)}, f32[8,512]{1,0:T(8,128)S(1)}) custom-call(bf16[512,256]{1,0:T(8,128)(2,1)S(1)} %get-tuple-element.45.refs_0_.queries, bf16[1024,256]{1,0:T(8,128)(2,1)S(1)} %get-tuple-element.46.refs_1_, bf16[1024,256]{1,0:T(8,128)(2,1)S(1)} %get-tuple-element.47.refs_2_, ...), custom_call_target="tpu_custom_call" | custom-call | flops 536870912 | bytes 1048576 | tf_op jit(solution)/shard_map/pallas_call | solution.py:80
  18.6 2.6 %collective-permute-done.2.refs_5_ = bf16[512,256]{1,0:T(8,128)(2,1)} collective-permute-done((bf16[512,256]{1,0:T(8,128)(2,1)}, bf16[512,256]{1,0:T(8,128)(2,1)}, u32[]{:S(2)}, u32[]{:S(2)}) %collective-permute-start.2) | collective-permute-done | bytes 262176 | tf_op jit(solution)/shard_map/ppermute | solution.py:22
  21.1 1.7 %collective-permute-done.4.refs_6_ = bf16[512,256]{1,0:T(8,128)(2,1)S(1)} collective-permute-done((bf16[512,256]{1,0:T(8,128)(2,1)}, bf16[512,256]{1,0:T(8,128)(2,1)S(1)}, u32[]{:S(2)}, u32[]{:S(2)}) %collective-permute-start.4) | collective-permute-done | bytes 262176 | tf_op jit(solution)/shard_map/ppermute | solution.py:72
  22.9 3.4 %shard_map.133 = (bf16[512,1024]{1,0:T(8,128)(2,1)S(1)}, bf16[512,256]{1,0:T(8,128)(2,1)S(1)}, bf16[256,512]{1,0:T(8,128)(2,1)S(1)}, bf16[272,256]{1,0:T(8,128)(2,1)S(1)}) custom-call(bf16[512,256]{1,0:T(8,128)(2,1)S(1)} %get-tuple-element.45.refs_0_.queries, bf16[1024,256]{1,0:T(8,128)(2,1)S(1)} %get-tuple-element.46.refs_1_, ...), custom_call_target="tpu_custom_call" | custom-call | flops 536870912 | bytes 1048576 | tf_op jit(solution)/shard_map/pallas_call | solution.py:80
  26.3 1.8 %collective-permute-start.5 = (bf16[272,256]{1,0:T(8,128)(2,1)S(1)}, bf16[272,256]{1,0:T(8,128)(2,1)S(1)}, u32[]{:S(2)}, u32[]{:S(2)}) collective-permute-start(bf16[272,256]{1,0:T(8,128)(2,1)S(1)} %get-tuple-element.58), channel_id=1, source_target_pairs={{0,4},{4,0},{8,12},{12,8},{16,20},{20,16},{24,28},{28,24},{1,5},{5... | collective-permute-start | bytes 417800 | tf_op jit(solution)/shard_map/ppermute | solution.py:65
  29.3 2.8 %collective-permute-done.5.other = bf16[272,256]{1,0:T(8,128)(2,1)S(1)} collective-permute-done((bf16[272,256]{1,0:T(8,128)(2,1)S(1)}, bf16[272,256]{1,0:T(8,128)(2,1)S(1)}, u32[]{:S(2)}, u32[]{:S(2)}) %collective-permute-start.5) | collective-permute-done | bytes 139296 | tf_op jit(solution)/shard_map/ppermute | solution.py:65
  32.2 3.9 %collective-permute-start.6 = (bf16[80,256]{1,0:T(8,128)(2,1)S(1)}, bf16[80,256]{1,0:T(8,128)(2,1)S(1)}, u32[]{:S(2)}, u32[]{:S(2)}) collective-permute-start(bf16[80,256]{1,0:T(8,128)(2,1)S(1)} %get-tuple-element.60), channel_id=1, source_target_pairs={{0,24},{4,28},{8,0},{12,4},{16,8},{20,12},{24,16},{28,20},{1,25},{... | collective-permute-start | bytes 122888 | tf_op jit(solution)/shard_map/ppermute | solution.py:43
  37.7 3.2 %collective-permute-done.7.refs_2_ = bf16[80,256]{1,0:T(8,128)(2,1)S(1)} collective-permute-done((bf16[80,256]{1,0:T(8,128)(2,1)S(1)}, bf16[80,256]{1,0:T(8,128)(2,1)S(1)}, u32[]{:S(2)}, u32[]{:S(2)}) %collective-permute-start.7) | collective-permute-done | bytes 40992 | tf_op jit(solution)/shard_map/ppermute | solution.py:43
  42.6 1.3 collective-permute-done.9.other
  43.9 1.6 %collective-permute-start.10 = (bf16[64,1024]{1,0:T(8,128)(2,1)S(1)}, bf16[64,1024]{1,0:T(8,128)(2,1)S(1)}, u32[]{:S(2)}, u32[]{:S(2)}) collective-permute-start(bf16[64,1024]{1,0:T(8,128)(2,1)S(1)} %shard_map.137.refs_0_), channel_id=1, source_target_pairs={{0,2},{1,3},{2,0},{3,1},{4,6},{5,7},{6,4},{7,5},{8,10},{9,11},{10,... | collective-permute-start | bytes 393224 | tf_op jit(solution)/shard_map/ppermute | solution.py:410
  45.5 4.0 %collective-permute-done.10.refs_1_ = bf16[64,1024]{1,0:T(8,128)(2,1)S(1)} collective-permute-done((bf16[64,1024]{1,0:T(8,128)(2,1)S(1)}, bf16[64,1024]{1,0:T(8,128)(2,1)S(1)}, u32[]{:S(2)}, u32[]{:S(2)}) %collective-permute-start.10) | collective-permute-done | bytes 131104 | tf_op jit(solution)/shard_map/ppermute | solution.py:410
  51.4 1.9 %collective-permute-start.11 = (bf16[64,512]{1,0:T(8,128)(2,1)S(1)}, bf16[64,512]{1,0:T(8,128)(2,1)S(1)}, u32[]{:S(2)}, u32[]{:S(2)}) collective-permute-start(bf16[64,512]{1,0:T(8,128)(2,1)S(1)} %get-tuple-element.65.refs_0_), channel_id=1, source_target_pairs={{0,8},{4,12},{8,16},{12,20},{16,24},{20,28},{24,0},{28,4},{1,9},{5... | collective-permute-start | bytes 196616 | tf_op jit(solution)/shard_map/ppermute | solution.py:43
  53.3 1.5 %collective-permute-start.14 = (bf16[64,512]{1,0:T(8,128)(2,1)S(1)}, bf16[64,512]{1,0:T(8,128)(2,1)S(1)}, u32[]{:S(2)}, u32[]{:S(2)}) collective-permute-start(bf16[64,512]{1,0:T(8,128)(2,1)S(1)} %get-tuple-element.65.refs_0_), channel_id=1, source_target_pairs={{0,4},{4,0},{8,12},{12,8},{16,20},{20,16},{24,28},{28,24},{1,5},{5... | collective-permute-start | bytes 196616 | tf_op jit(solution)/shard_map/ppermute | solution.py:65
  55.0 1.5 %collective-permute-start.17 = (bf16[64,512]{1,0:T(8,128)(2,1)S(1)}, bf16[64,512]{1,0:T(8,128)(2,1)S(1)}, u32[]{:S(2)}, u32[]{:S(2)}) collective-permute-start(bf16[64,512]{1,0:T(8,128)(2,1)S(1)} %collective-permute-done.13.refs_3_), channel_id=1, source_target_pairs={{0,4},{4,0},{8,12},{12,8},{16,20},{20,16},{24,28},{28,24},{1,5},{5... | collective-permute-start | bytes 196616 | tf_op jit(solution)/shard_map/ppermute | solution.py:65
  56.5 1.7 %collective-permute-done.12.refs_2_ = bf16[64,512]{1,0:T(8,128)(2,1)S(1)} collective-permute-done((bf16[64,512]{1,0:T(8,128)(2,1)S(1)}, bf16[64,512]{1,0:T(8,128)(2,1)S(1)}, u32[]{:S(2)}, u32[]{:S(2)}) %collective-permute-start.12) | collective-permute-done | bytes 65568 | tf_op jit(solution)/shard_map/ppermute | solution.py:43
  58.2 1.5 %collective-permute-start.16 = (bf16[64,512]{1,0:T(8,128)(2,1)S(1)}, bf16[64,512]{1,0:T(8,128)(2,1)S(1)}, u32[]{:S(2)}, u32[]{:S(2)}) collective-permute-start(bf16[64,512]{1,0:T(8,128)(2,1)S(1)} %collective-permute-done.12.refs_2_), channel_id=1, source_target_pairs={{0,4},{4,0},{8,12},{12,8},{16,20},{20,16},{24,28},{28,24},{1,5},{5... | collective-permute-start | bytes 196616 | tf_op jit(solution)/shard_map/ppermute | solution.py:65
  60.2 2.2 %collective-permute-done.16.refs_6_ = bf16[64,512]{1,0:T(8,128)(2,1)S(1)} collective-permute-done((bf16[64,512]{1,0:T(8,128)(2,1)S(1)}, bf16[64,512]{1,0:T(8,128)(2,1)S(1)}, u32[]{:S(2)}, u32[]{:S(2)}) %collective-permute-start.16) | collective-permute-done | bytes 65568 | tf_op jit(solution)/shard_map/ppermute | solution.py:65
  62.4 1.5 %collective-permute-done.15.refs_5_ = bf16[64,512]{1,0:T(8,128)(2,1)S(1)} collective-permute-done((bf16[64,512]{1,0:T(8,128)(2,1)S(1)}, bf16[64,512]{1,0:T(8,128)(2,1)S(1)}, u32[]{:S(2)}, u32[]{:S(2)}) %collective-permute-start.15) | collective-permute-done | bytes 65568 | tf_op jit(solution)/shard_map/ppermute | solution.py:65
  65.1 1.3 shard_map.144
  67.2 1.3 collective-permute-start.26
  68.5 1.6 %collective-permute-start.19 = (bf16[64,1024]{1,0:T(8,128)(2,1)S(1)}, bf16[64,1024]{1,0:T(8,128)(2,1)S(1)}, u32[]{:S(2)}, u32[]{:S(2)}) collective-permute-start(bf16[64,1024]{1,0:T(8,128)(2,1)S(1)} %shard_map.140.refs_0_), channel_id=1, source_target_pairs={{0,2},{1,3},{2,0},{3,1},{4,6},{5,7},{6,4},{7,5},{8,10},{9,11},{10,... | collective-permute-start | bytes 393224 | tf_op jit(solution)/shard_map/ppermute | solution.py:410
  70.1 3.8 %collective-permute-done.19.refs_1_ = bf16[64,1024]{1,0:T(8,128)(2,1)S(1)} collective-permute-done((bf16[64,1024]{1,0:T(8,128)(2,1)S(1)}, bf16[64,1024]{1,0:T(8,128)(2,1)S(1)}, u32[]{:S(2)}, u32[]{:S(2)}) %collective-permute-start.19) | collective-permute-done | bytes 131104 | tf_op jit(solution)/shard_map/ppermute | solution.py:410
  75.0 1.3 collective-permute-done.20.other
  76.4 1.6 %collective-permute-start.21 = (bf16[64,1024]{1,0:T(8,128)(2,1)S(1)}, bf16[64,1024]{1,0:T(8,128)(2,1)S(1)}, u32[]{:S(2)}, u32[]{:S(2)}) collective-permute-start(bf16[64,1024]{1,0:T(8,128)(2,1)S(1)} %shard_map.142.refs_0_), channel_id=1, source_target_pairs={{0,2},{1,3},{2,0},{3,1},{4,6},{5,7},{6,4},{7,5},{8,10},{9,11},{10,... | collective-permute-start | bytes 393224 | tf_op jit(solution)/shard_map/ppermute | solution.py:410
  78.0 4.0 %collective-permute-done.21.refs_1_ = bf16[64,1024]{1,0:T(8,128)(2,1)S(1)} collective-permute-done((bf16[64,1024]{1,0:T(8,128)(2,1)S(1)}, bf16[64,1024]{1,0:T(8,128)(2,1)S(1)}, u32[]{:S(2)}, u32[]{:S(2)}) %collective-permute-start.21) | collective-permute-done | bytes 131104 | tf_op jit(solution)/shard_map/ppermute | solution.py:410
  84.5 7.5 %collective-permute-done.26.refs_7_ = bf16[256,1024]{1,0:T(8,128)(2,1)S(1)} collective-permute-done((bf16[256,1024]{1,0:T(8,128)(2,1)S(1)}, bf16[256,1024]{1,0:T(8,128)(2,1)S(1)}, u32[]{:S(2)}, u32[]{:S(2)}) %collective-permute-start.26) | collective-permute-done | bytes 524320 | tf_op jit(solution)/shard_map/ppermute | solution.py:65
  92.0 3.2 %shard_map.145 = (bf16[80,256]{1,0:T(8,128)(2,1)S(1)}, bf16[80,256]{1,0:T(8,128)(2,1)S(1)}, bf16[80,256]{1,0:T(8,128)(2,1)S(1)}, bf16[80,256]{1,0:T(8,128)(2,1)S(1)}, bf16[256,256]{1,0:T(8,128)(2,1)S(1)}) custom-call(bf16[64,512]{1,0:T(8,128)(2,1)S(1)} %get-tuple-element.69.refs_0_, bf16[64,512]{1,0:T(8,128)(2,1)S(1)} %collective-permute-done.22.refs_1_, ...), custom_call_target="tpu_custom_call" | custom-call | tf_op jit(solution)/shard_map/pallas_call | solution.py:80
  97.3 2.0 %collective-permute-done.27.refs_1_ = bf16[80,256]{1,0:T(8,128)(2,1)S(1)} collective-permute-done((bf16[80,256]{1,0:T(8,128)(2,1)S(1)}, bf16[80,256]{1,0:T(8,128)(2,1)S(1)}, u32[]{:S(2)}, u32[]{:S(2)}) %collective-permute-start.27) | collective-permute-done | bytes 40992 | tf_op jit(solution)/shard_map/ppermute | solution.py:43
  99.3 2.6 %collective-permute-done.28.refs_2_ = bf16[80,256]{1,0:T(8,128)(2,1)S(1)} collective-permute-done((bf16[80,256]{1,0:T(8,128)(2,1)S(1)}, bf16[80,256]{1,0:T(8,128)(2,1)S(1)}, u32[]{:S(2)}, u32[]{:S(2)}) %collective-permute-start.28) | collective-permute-done | bytes 40992 | tf_op jit(solution)/shard_map/ppermute | solution.py:43
  103.0 1.3 collective-permute-done.30.other
  104.4 1.6 %collective-permute-start.31 = (bf16[64,1024]{1,0:T(8,128)(2,1)S(1)}, bf16[64,1024]{1,0:T(8,128)(2,1)S(1)}, u32[]{:S(2)}, u32[]{:S(2)}) collective-permute-start(bf16[64,1024]{1,0:T(8,128)(2,1)S(1)} %shard_map.147.refs_0_), channel_id=1, source_target_pairs={{0,2},{1,3},{2,0},{3,1},{4,6},{5,7},{6,4},{7,5},{8,10},{9,11},{10,... | collective-permute-start | bytes 393224 | tf_op jit(solution)/shard_map/ppermute | solution.py:410
  105.9 4.0 %collective-permute-done.31.refs_1_ = bf16[64,1024]{1,0:T(8,128)(2,1)S(1)} collective-permute-done((bf16[64,1024]{1,0:T(8,128)(2,1)S(1)}, bf16[64,1024]{1,0:T(8,128)(2,1)S(1)}, u32[]{:S(2)}, u32[]{:S(2)}) %collective-permute-start.31) | collective-permute-done | bytes 131104 | tf_op jit(solution)/shard_map/ppermute | solution.py:410
  110.5 1.4 collective-permute-start.34
  112.0 1.7 %collective-permute-start.32 = (bf16[64,512]{1,0:T(8,128)(2,1)S(1)}, bf16[64,512]{1,0:T(8,128)(2,1)S(1)}, u32[]{:S(2)}, u32[]{:S(2)}) collective-permute-start(bf16[64,512]{1,0:T(8,128)(2,1)S(1)} %get-tuple-element.80.refs_0_), channel_id=1, source_target_pairs={{0,8},{4,12},{8,16},{12,20},{16,24},{20,28},{24,0},{28,4},{1,9},{5... | collective-permute-start | bytes 196616 | tf_op jit(solution)/shard_map/ppermute | solution.py:43
  115.9 2.9 %collective-permute-done.33.refs_2_ = bf16[64,512]{1,0:T(8,128)(2,1)S(1)} collective-permute-done((bf16[64,512]{1,0:T(8,128)(2,1)S(1)}, bf16[64,512]{1,0:T(8,128)(2,1)S(1)}, u32[]{:S(2)}, u32[]{:S(2)}) %collective-permute-start.33) | collective-permute-done | bytes 65568 | tf_op jit(solution)/shard_map/ppermute | solution.py:43
  119.5 1.3 collective-permute-start.36
  120.8 2.2 %collective-permute-done.37.refs_6_ = bf16[64,512]{1,0:T(8,128)(2,1)S(1)} collective-permute-done((bf16[64,512]{1,0:T(8,128)(2,1)S(1)}, bf16[64,512]{1,0:T(8,128)(2,1)S(1)}, u32[]{:S(2)}, u32[]{:S(2)}) %collective-permute-start.37) | collective-permute-done | bytes 65568 | tf_op jit(solution)/shard_map/ppermute | solution.py:65
  124.9 1.3 collective-permute-done.39.other
  126.2 1.6 %collective-permute-start.40 = (bf16[64,1024]{1,0:T(8,128)(2,1)S(1)}, bf16[64,1024]{1,0:T(8,128)(2,1)S(1)}, u32[]{:S(2)}, u32[]{:S(2)}) collective-permute-start(bf16[64,1024]{1,0:T(8,128)(2,1)S(1)} %shard_map.150.refs_0_), channel_id=1, source_target_pairs={{0,2},{1,3},{2,0},{3,1},{4,6},{5,7},{6,4},{7,5},{8,10},{9,11},{10,... | collective-permute-start | bytes 393224 | tf_op jit(solution)/shard_map/ppermute | solution.py:410
  127.8 4.0 %collective-permute-done.40.refs_1_ = bf16[64,1024]{1,0:T(8,128)(2,1)S(1)} collective-permute-done((bf16[64,1024]{1,0:T(8,128)(2,1)S(1)}, bf16[64,1024]{1,0:T(8,128)(2,1)S(1)}, u32[]{:S(2)}, u32[]{:S(2)}) %collective-permute-start.40) | collective-permute-done | bytes 131104 | tf_op jit(solution)/shard_map/ppermute | solution.py:410
  133.0 1.4 collective-permute-start.43
  134.4 1.6 %collective-permute-start.42 = (bf16[64,1024]{1,0:T(8,128)(2,1)S(1)}, bf16[64,1024]{1,0:T(8,128)(2,1)S(1)}, u32[]{:S(2)}, u32[]{:S(2)}) collective-permute-start(bf16[64,1024]{1,0:T(8,128)(2,1)S(1)} %shard_map.152.refs_0_), channel_id=1, source_target_pairs={{0,2},{1,3},{2,0},{3,1},{4,6},{5,7},{6,4},{7,5},{8,10},{9,11},{10,... | collective-permute-start | bytes 393224 | tf_op jit(solution)/shard_map/ppermute | solution.py:410
  136.0 2.9 %collective-permute-done.43.refs_3_ = bf16[256,256]{1,0:T(8,128)(2,1)S(1)} collective-permute-done((bf16[256,256]{1,0:T(8,128)(2,1)S(1)}, bf16[256,256]{1,0:T(8,128)(2,1)S(1)}, u32[]{:S(2)}, u32[]{:S(2)}) %collective-permute-start.43) | collective-permute-done | bytes 131104 | tf_op jit(solution)/shard_map/ppermute | solution.py:65
  (90 shorter events, 26.4 us)
Async XLA Ops:
  2.5 9.6 %collective-permute-start = (bf16[512,256]{1,0:T(8,128)(2,1)}, bf16[512,256]{1,0:T(8,128)(2,1)}, u32[]{:S(2)}, u32[]{:S(2)}) collective-permute-start(bf16[512,256]{1,0:T(8,128)(2,1)} %get-tuple-element.85), channel_id=1, source_target_pairs={{0,2},{1,3},{2,0},{3,1},{4,6},{5,7},{6,4},{7,5},{8,10},{9,11},{10,... | collective-permute-start | bytes 786440 | tf_op jit(solution)/shard_map/ppermute | solution.py:22
  5.5 8.4 %collective-permute-start.1 = (bf16[1024,256]{1,0:T(8,128)(2,1)}, bf16[1024,256]{1,0:T(8,128)(2,1)S(1)}, u32[]{:S(2)}, u32[]{:S(2)}) collective-permute-start(bf16[1024,256]{1,0:T(8,128)(2,1)} %frames_hbm.1), channel_id=1, source_target_pairs={{0,1},{1,0},{2,3},{3,2},{4,5},{5,4},{6,7},{7,6},{8,9},{9,8},{10,11... | collective-permute-start | bytes 1572872 | tf_op jit(solution)/shard_map/ppermute | solution.py:476
  12.1 1.9 %collective-permute-start.3 = (bf16[512,256]{1,0:T(8,128)(2,1)}, bf16[512,256]{1,0:T(8,128)(2,1)}, u32[]{:S(2)}, u32[]{:S(2)}) collective-permute-start(bf16[512,256]{1,0:T(8,128)(2,1)} %collective-permute-done.refs_5_), channel_id=1, source_target_pairs={{0,1},{1,0},{2,3},{3,2},{4,5},{5,4},{6,7},{7,6},{8,9},{9,8},{10,11... | collective-permute-start | bytes 786440 | tf_op jit(solution)/shard_map/ppermute | solution.py:72
  12.1 9.0 %collective-permute-start.2 = (bf16[512,256]{1,0:T(8,128)(2,1)}, bf16[512,256]{1,0:T(8,128)(2,1)}, u32[]{:S(2)}, u32[]{:S(2)}) collective-permute-start(bf16[512,256]{1,0:T(8,128)(2,1)} %get-tuple-element.84), channel_id=1, source_target_pairs={{0,2},{1,3},{2,0},{3,1},{4,6},{5,7},{6,4},{7,5},{8,10},{9,11},{10,... | collective-permute-start | bytes 786440 | tf_op jit(solution)/shard_map/ppermute | solution.py:22
  14.0 35.6 %copy-start.12 = (f32[64,1024]{1,0:T(8,128)S(1)}, f32[64,1024]{1,0:T(8,128)}, u32[]{:S(2)}) copy-start(f32[64,1024]{1,0:T(8,128)} %copy-done.11) | copy-start | bytes 786436
  21.1 1.7 %collective-permute-start.4 = (bf16[512,256]{1,0:T(8,128)(2,1)}, bf16[512,256]{1,0:T(8,128)(2,1)S(1)}, u32[]{:S(2)}, u32[]{:S(2)}) collective-permute-start(bf16[512,256]{1,0:T(8,128)(2,1)} %collective-permute-done.2.refs_5_), channel_id=1, source_target_pairs={{0,1},{1,0},{2,3},{3,2},{4,5},{5,4},{6,7},{7,6},{8,9},{9,8},{10,11... | collective-permute-start | bytes 786440 | tf_op jit(solution)/shard_map/ppermute | solution.py:72
  26.3 37.7 %copy-start.9 = (bf16[2,256,1024]{2,1,0:T(8,128)(2,1)S(1)}, bf16[2,256,1024]{2,1,0:T(8,128)(2,1)}, u32[]{:S(2)}) copy-start(bf16[2,256,1024]{2,1,0:T(8,128)(2,1)} %refs_8_.3) | copy-start | bytes 3145732
  26.3 5.8 %collective-permute-start.5 = (bf16[272,256]{1,0:T(8,128)(2,1)S(1)}, bf16[272,256]{1,0:T(8,128)(2,1)S(1)}, u32[]{:S(2)}, u32[]{:S(2)}) collective-permute-start(bf16[272,256]{1,0:T(8,128)(2,1)S(1)} %get-tuple-element.58), channel_id=1, source_target_pairs={{0,4},{4,0},{8,12},{12,8},{16,20},{20,16},{24,28},{28,24},{1,5},{5... | collective-permute-start | bytes 417800 | tf_op jit(solution)/shard_map/ppermute | solution.py:65
  28.0 37.0 %copy-start.6 = (bf16[2,1024,256]{2,1,0:T(8,128)(2,1)S(1)}, bf16[2,1024,256]{2,1,0:T(8,128)(2,1)}, u32[]{:S(2)}) copy-start(bf16[2,1024,256]{2,1,0:T(8,128)(2,1)} %refs_2_.9) | copy-start | bytes 3145732
  28.1 37.0 %copy-start.7 = (bf16[2,1024,256]{2,1,0:T(8,128)(2,1)S(1)}, bf16[2,1024,256]{2,1,0:T(8,128)(2,1)}, u32[]{:S(2)}) copy-start(bf16[2,1024,256]{2,1,0:T(8,128)(2,1)} %refs_3_.7) | copy-start | bytes 3145732
  32.2 5.5 %collective-permute-start.6 = (bf16[80,256]{1,0:T(8,128)(2,1)S(1)}, bf16[80,256]{1,0:T(8,128)(2,1)S(1)}, u32[]{:S(2)}, u32[]{:S(2)}) collective-permute-start(bf16[80,256]{1,0:T(8,128)(2,1)S(1)} %get-tuple-element.60), channel_id=1, source_target_pairs={{0,24},{4,28},{8,0},{12,4},{16,8},{20,12},{24,16},{28,20},{1,25},{... | collective-permute-start | bytes 122888 | tf_op jit(solution)/shard_map/ppermute | solution.py:43
  36.1 4.9 %collective-permute-start.7 = (bf16[80,256]{1,0:T(8,128)(2,1)S(1)}, bf16[80,256]{1,0:T(8,128)(2,1)S(1)}, u32[]{:S(2)}, u32[]{:S(2)}) collective-permute-start(bf16[80,256]{1,0:T(8,128)(2,1)S(1)} %get-tuple-element.61), channel_id=1, source_target_pairs={{0,16},{4,20},{8,24},{12,28},{16,0},{20,4},{24,8},{28,12},{1,17},{... | collective-permute-start | bytes 122888 | tf_op jit(solution)/shard_map/ppermute | solution.py:43
  36.1 5.8 %collective-permute-start.8 = (bf16[80,256]{1,0:T(8,128)(2,1)S(1)}, bf16[80,256]{1,0:T(8,128)(2,1)S(1)}, u32[]{:S(2)}, u32[]{:S(2)}) collective-permute-start(bf16[80,256]{1,0:T(8,128)(2,1)S(1)} %get-tuple-element.62), channel_id=1, source_target_pairs={{0,8},{4,12},{8,16},{12,20},{16,24},{20,28},{24,0},{28,4},{1,9},{5... | collective-permute-start | bytes 122888 | tf_op jit(solution)/shard_map/ppermute | solution.py:43
  42.5 1.4 %collective-permute-start.9 = (bf16[64,1024]{1,0:T(8,128)(2,1)S(1)}, bf16[64,1024]{1,0:T(8,128)(2,1)S(1)}, u32[]{:S(2)}, u32[]{:S(2)}) collective-permute-start(bf16[64,1024]{1,0:T(8,128)(2,1)S(1)} %shard_map.136.part), channel_id=1, source_target_pairs={{0,1},{1,0},{2,3},{3,2},{4,5},{5,4},{6,7},{7,6},{8,9},{9,8},{10,11... | collective-permute-start | bytes 393224 | tf_op jit(solution)/shard_map/ppermute | solution.py:410
  43.9 5.6 %collective-permute-start.10 = (bf16[64,1024]{1,0:T(8,128)(2,1)S(1)}, bf16[64,1024]{1,0:T(8,128)(2,1)S(1)}, u32[]{:S(2)}, u32[]{:S(2)}) collective-permute-start(bf16[64,1024]{1,0:T(8,128)(2,1)S(1)} %shard_map.137.refs_0_), channel_id=1, source_target_pairs={{0,2},{1,3},{2,0},{3,1},{4,6},{5,7},{6,4},{7,5},{8,10},{9,11},{10,... | collective-permute-start | bytes 393224 | tf_op jit(solution)/shard_map/ppermute | solution.py:410
  50.1 4.8 %collective-permute-start.13 = (bf16[64,512]{1,0:T(8,128)(2,1)S(1)}, bf16[64,512]{1,0:T(8,128)(2,1)S(1)}, u32[]{:S(2)}, u32[]{:S(2)}) collective-permute-start(bf16[64,512]{1,0:T(8,128)(2,1)S(1)} %get-tuple-element.65.refs_0_), channel_id=1, source_target_pairs={{0,24},{4,28},{8,0},{12,4},{16,8},{20,12},{24,16},{28,20},{1,25},{... | collective-permute-start | bytes 196616 | tf_op jit(solution)/shard_map/ppermute | solution.py:43
  50.9 7.3 %collective-permute-start.12 = (bf16[64,512]{1,0:T(8,128)(2,1)S(1)}, bf16[64,512]{1,0:T(8,128)(2,1)S(1)}, u32[]{:S(2)}, u32[]{:S(2)}) collective-permute-start(bf16[64,512]{1,0:T(8,128)(2,1)S(1)} %get-tuple-element.65.refs_0_), channel_id=1, source_target_pairs={{0,16},{4,20},{8,24},{12,28},{16,0},{20,4},{24,8},{28,12},{1,17},{... | collective-permute-start | bytes 196616 | tf_op jit(solution)/shard_map/ppermute | solution.py:43
  51.4 8.3 %collective-permute-start.11 = (bf16[64,512]{1,0:T(8,128)(2,1)S(1)}, bf16[64,512]{1,0:T(8,128)(2,1)S(1)}, u32[]{:S(2)}, u32[]{:S(2)}) collective-permute-start(bf16[64,512]{1,0:T(8,128)(2,1)S(1)} %get-tuple-element.65.refs_0_), channel_id=1, source_target_pairs={{0,8},{4,12},{8,16},{12,20},{16,24},{20,28},{24,0},{28,4},{1,9},{5... | collective-permute-start | bytes 196616 | tf_op jit(solution)/shard_map/ppermute | solution.py:43
  53.3 6.9 %collective-permute-start.14 = (bf16[64,512]{1,0:T(8,128)(2,1)S(1)}, bf16[64,512]{1,0:T(8,128)(2,1)S(1)}, u32[]{:S(2)}, u32[]{:S(2)}) collective-permute-start(bf16[64,512]{1,0:T(8,128)(2,1)S(1)} %get-tuple-element.65.refs_0_), channel_id=1, source_target_pairs={{0,4},{4,0},{8,12},{12,8},{16,20},{20,16},{24,28},{28,24},{1,5},{5... | collective-permute-start | bytes 196616 | tf_op jit(solution)/shard_map/ppermute | solution.py:65
  55.0 5.3 %collective-permute-start.17 = (bf16[64,512]{1,0:T(8,128)(2,1)S(1)}, bf16[64,512]{1,0:T(8,128)(2,1)S(1)}, u32[]{:S(2)}, u32[]{:S(2)}) collective-permute-start(bf16[64,512]{1,0:T(8,128)(2,1)S(1)} %collective-permute-done.13.refs_3_), channel_id=1, source_target_pairs={{0,4},{4,0},{8,12},{12,8},{16,20},{20,16},{24,28},{28,24},{1,5},{5... | collective-permute-start | bytes 196616 | tf_op jit(solution)/shard_map/ppermute | solution.py:65
  58.2 4.3 %collective-permute-start.16 = (bf16[64,512]{1,0:T(8,128)(2,1)S(1)}, bf16[64,512]{1,0:T(8,128)(2,1)S(1)}, u32[]{:S(2)}, u32[]{:S(2)}) collective-permute-start(bf16[64,512]{1,0:T(8,128)(2,1)S(1)} %collective-permute-done.12.refs_2_), channel_id=1, source_target_pairs={{0,4},{4,0},{8,12},{12,8},{16,20},{20,16},{24,28},{28,24},{1,5},{5... | collective-permute-start | bytes 196616 | tf_op jit(solution)/shard_map/ppermute | solution.py:65
  59.7 4.3 %collective-permute-start.15 = (bf16[64,512]{1,0:T(8,128)(2,1)S(1)}, bf16[64,512]{1,0:T(8,128)(2,1)S(1)}, u32[]{:S(2)}, u32[]{:S(2)}) collective-permute-start(bf16[64,512]{1,0:T(8,128)(2,1)S(1)} %collective-permute-done.11.refs_1_), channel_id=1, source_target_pairs={{0,4},{4,0},{8,12},{12,8},{16,20},{20,16},{24,28},{28,24},{1,5},{5... | collective-permute-start | bytes 196616 | tf_op jit(solution)/shard_map/ppermute | solution.py:65
  65.0 3.5 %collective-permute-start.18 = (bf16[64,1024]{1,0:T(8,128)(2,1)S(1)}, bf16[64,1024]{1,0:T(8,128)(2,1)S(1)}, u32[]{:S(2)}, u32[]{:S(2)}) collective-permute-start(bf16[64,1024]{1,0:T(8,128)(2,1)S(1)} %shard_map.139.part), channel_id=1, source_target_pairs={{0,1},{1,0},{2,3},{3,2},{4,5},{5,4},{6,7},{7,6},{8,9},{9,8},{10,11... | collective-permute-start | bytes 393224 | tf_op jit(solution)/shard_map/ppermute | solution.py:410
  66.4 18.1 %collective-permute-start.25 = (bf16[1024,256]{1,0:T(8,128)(2,1)S(1)}, bf16[1024,256]{1,0:T(8,128)(2,1)S(1)}, u32[]{:S(2)}, u32[]{:S(2)}) collective-permute-start(bf16[1024,256]{1,0:T(8,128)(2,1)S(1)} %get-tuple-element.72.refs_4_), channel_id=1, source_target_pairs={{0,4},{4,0},{8,12},{12,8},{16,20},{20,16},{24,28},{28,24},{1,5},{5... | collective-permute-start | bytes 1572872 | tf_op jit(solution)/shard_map/ppermute | solution.py:65
  67.2 24.8 %collective-permute-start.26 = (bf16[256,1024]{1,0:T(8,128)(2,1)S(1)}, bf16[256,1024]{1,0:T(8,128)(2,1)S(1)}, u32[]{:S(2)}, u32[]{:S(2)}) collective-permute-start(bf16[256,1024]{1,0:T(8,128)(2,1)S(1)} %get-tuple-element.73.refs_6_), channel_id=1, source_target_pairs={{0,4},{4,0},{8,12},{12,8},{16,20},{20,16},{24,28},{28,24},{1,5},{5... | collective-permute-start | bytes 1572872 | tf_op jit(solution)/shard_map/ppermute | solution.py:65
  68.5 5.4 %collective-permute-start.19 = (bf16[64,1024]{1,0:T(8,128)(2,1)S(1)}, bf16[64,1024]{1,0:T(8,128)(2,1)S(1)}, u32[]{:S(2)}, u32[]{:S(2)}) collective-permute-start(bf16[64,1024]{1,0:T(8,128)(2,1)S(1)} %shard_map.140.refs_0_), channel_id=1, source_target_pairs={{0,2},{1,3},{2,0},{3,1},{4,6},{5,7},{6,4},{7,5},{8,10},{9,11},{10,... | collective-permute-start | bytes 393224 | tf_op jit(solution)/shard_map/ppermute | solution.py:410
  75.0 1.4 %collective-permute-start.20 = (bf16[64,1024]{1,0:T(8,128)(2,1)S(1)}, bf16[64,1024]{1,0:T(8,128)(2,1)S(1)}, u32[]{:S(2)}, u32[]{:S(2)}) collective-permute-start(bf16[64,1024]{1,0:T(8,128)(2,1)S(1)} %get-tuple-element.67.part), channel_id=1, source_target_pairs={{0,1},{1,0},{2,3},{3,2},{4,5},{5,4},{6,7},{7,6},{8,9},{9,8},{10,11... | collective-permute-start | bytes 393224 | tf_op jit(solution)/shard_map/ppermute | solution.py:410
  76.4 5.6 %collective-permute-start.21 = (bf16[64,1024]{1,0:T(8,128)(2,1)S(1)}, bf16[64,1024]{1,0:T(8,128)(2,1)S(1)}, u32[]{:S(2)}, u32[]{:S(2)}) collective-permute-start(bf16[64,1024]{1,0:T(8,128)(2,1)S(1)} %shard_map.142.refs_0_), channel_id=1, source_target_pairs={{0,2},{1,3},{2,0},{3,1},{4,6},{5,7},{6,4},{7,5},{8,10},{9,11},{10,... | collective-permute-start | bytes 393224 | tf_op jit(solution)/shard_map/ppermute | solution.py:410
  82.4 9.6 %collective-permute-start.24 = (bf16[64,512]{1,0:T(8,128)(2,1)S(1)}, bf16[64,512]{1,0:T(8,128)(2,1)S(1)}, u32[]{:S(2)}, u32[]{:S(2)}) collective-permute-start(bf16[64,512]{1,0:T(8,128)(2,1)S(1)} %get-tuple-element.69.refs_0_), channel_id=1, source_target_pairs={{0,24},{4,28},{8,0},{12,4},{16,8},{20,12},{24,16},{28,20},{1,25},{... | collective-permute-start | bytes 196616 | tf_op jit(solution)/shard_map/ppermute | solution.py:43
  83.7 8.3 %collective-permute-start.23 = (bf16[64,512]{1,0:T(8,128)(2,1)S(1)}, bf16[64,512]{1,0:T(8,128)(2,1)S(1)}, u32[]{:S(2)}, u32[]{:S(2)}) collective-permute-start(bf16[64,512]{1,0:T(8,128)(2,1)S(1)} %get-tuple-element.69.refs_0_), channel_id=1, source_target_pairs={{0,16},{4,20},{8,24},{12,28},{16,0},{20,4},{24,8},{28,12},{1,17},{... | collective-permute-start | bytes 196616 | tf_op jit(solution)/shard_map/ppermute | solution.py:43
  83.7 8.3 %collective-permute-start.22 = (bf16[64,512]{1,0:T(8,128)(2,1)S(1)}, bf16[64,512]{1,0:T(8,128)(2,1)S(1)}, u32[]{:S(2)}, u32[]{:S(2)}) collective-permute-start(bf16[64,512]{1,0:T(8,128)(2,1)S(1)} %get-tuple-element.69.refs_0_), channel_id=1, source_target_pairs={{0,8},{4,12},{8,16},{12,20},{16,24},{20,28},{24,0},{28,4},{1,9},{5... | collective-permute-start | bytes 196616 | tf_op jit(solution)/shard_map/ppermute | solution.py:43
  95.2 4.0 %collective-permute-start.27 = (bf16[80,256]{1,0:T(8,128)(2,1)S(1)}, bf16[80,256]{1,0:T(8,128)(2,1)S(1)}, u32[]{:S(2)}, u32[]{:S(2)}) collective-permute-start(bf16[80,256]{1,0:T(8,128)(2,1)S(1)} %get-tuple-element.75), channel_id=1, source_target_pairs={{0,24},{4,28},{8,0},{12,4},{16,8},{20,12},{24,16},{28,20},{1,25},{... | collective-permute-start | bytes 122888 | tf_op jit(solution)/shard_map/ppermute | solution.py:43
  96.5 5.3 %collective-permute-start.28 = (bf16[80,256]{1,0:T(8,128)(2,1)S(1)}, bf16[80,256]{1,0:T(8,128)(2,1)S(1)}, u32[]{:S(2)}, u32[]{:S(2)}) collective-permute-start(bf16[80,256]{1,0:T(8,128)(2,1)S(1)} %get-tuple-element.76), channel_id=1, source_target_pairs={{0,16},{4,20},{8,24},{12,28},{16,0},{20,4},{24,8},{28,12},{1,17},{... | collective-permute-start | bytes 122888 | tf_op jit(solution)/shard_map/ppermute | solution.py:43
  96.5 5.8 %collective-permute-start.29 = (bf16[80,256]{1,0:T(8,128)(2,1)S(1)}, bf16[80,256]{1,0:T(8,128)(2,1)S(1)}, u32[]{:S(2)}, u32[]{:S(2)}) collective-permute-start(bf16[80,256]{1,0:T(8,128)(2,1)S(1)} %get-tuple-element.77), channel_id=1, source_target_pairs={{0,8},{4,12},{8,16},{12,20},{16,24},{20,28},{24,0},{28,4},{1,9},{5... | collective-permute-start | bytes 122888 | tf_op jit(solution)/shard_map/ppermute | solution.py:43
  102.9 1.4 %collective-permute-start.30 = (bf16[64,1024]{1,0:T(8,128)(2,1)S(1)}, bf16[64,1024]{1,0:T(8,128)(2,1)S(1)}, u32[]{:S(2)}, u32[]{:S(2)}) collective-permute-start(bf16[64,1024]{1,0:T(8,128)(2,1)S(1)} %shard_map.146.part), channel_id=1, source_target_pairs={{0,1},{1,0},{2,3},{3,2},{4,5},{5,4},{6,7},{7,6},{8,9},{9,8},{10,11... | collective-permute-start | bytes 393224 | tf_op jit(solution)/shard_map/ppermute | solution.py:410
  104.4 5.6 %collective-permute-start.31 = (bf16[64,1024]{1,0:T(8,128)(2,1)S(1)}, bf16[64,1024]{1,0:T(8,128)(2,1)S(1)}, u32[]{:S(2)}, u32[]{:S(2)}) collective-permute-start(bf16[64,1024]{1,0:T(8,128)(2,1)S(1)} %shard_map.147.refs_0_), channel_id=1, source_target_pairs={{0,2},{1,3},{2,0},{3,1},{4,6},{5,7},{6,4},{7,5},{8,10},{9,11},{10,... | collective-permute-start | bytes 393224 | tf_op jit(solution)/shard_map/ppermute | solution.py:410
  110.5 4.7 %collective-permute-start.34 = (bf16[64,512]{1,0:T(8,128)(2,1)S(1)}, bf16[64,512]{1,0:T(8,128)(2,1)S(1)}, u32[]{:S(2)}, u32[]{:S(2)}) collective-permute-start(bf16[64,512]{1,0:T(8,128)(2,1)S(1)} %get-tuple-element.80.refs_0_), channel_id=1, source_target_pairs={{0,24},{4,28},{8,0},{12,4},{16,8},{20,12},{24,16},{28,20},{1,25},{... | collective-permute-start | bytes 196616 | tf_op jit(solution)/shard_map/ppermute | solution.py:43
  111.9 6.8 %collective-permute-start.33 = (bf16[64,512]{1,0:T(8,128)(2,1)S(1)}, bf16[64,512]{1,0:T(8,128)(2,1)S(1)}, u32[]{:S(2)}, u32[]{:S(2)}) collective-permute-start(bf16[64,512]{1,0:T(8,128)(2,1)S(1)} %get-tuple-element.80.refs_0_), channel_id=1, source_target_pairs={{0,16},{4,20},{8,24},{12,28},{16,0},{20,4},{24,8},{28,12},{1,17},{... | collective-permute-start | bytes 196616 | tf_op jit(solution)/shard_map/ppermute | solution.py:43
  112.0 7.4 %collective-permute-start.32 = (bf16[64,512]{1,0:T(8,128)(2,1)S(1)}, bf16[64,512]{1,0:T(8,128)(2,1)S(1)}, u32[]{:S(2)}, u32[]{:S(2)}) collective-permute-start(bf16[64,512]{1,0:T(8,128)(2,1)S(1)} %get-tuple-element.80.refs_0_), channel_id=1, source_target_pairs={{0,8},{4,12},{8,16},{12,20},{16,24},{20,28},{24,0},{28,4},{1,9},{5... | collective-permute-start | bytes 196616 | tf_op jit(solution)/shard_map/ppermute | solution.py:43
  113.7 7.1 %collective-permute-start.35 = (bf16[64,512]{1,0:T(8,128)(2,1)S(1)}, bf16[64,512]{1,0:T(8,128)(2,1)S(1)}, u32[]{:S(2)}, u32[]{:S(2)}) collective-permute-start(bf16[64,512]{1,0:T(8,128)(2,1)S(1)} %get-tuple-element.80.refs_0_), channel_id=1, source_target_pairs={{0,4},{4,0},{8,12},{12,8},{16,20},{20,16},{24,28},{28,24},{1,5},{5... | collective-permute-start | bytes 196616 | tf_op jit(solution)/shard_map/ppermute | solution.py:65
  115.2 5.6 %collective-permute-start.38 = (bf16[64,512]{1,0:T(8,128)(2,1)S(1)}, bf16[64,512]{1,0:T(8,128)(2,1)S(1)}, u32[]{:S(2)}, u32[]{:S(2)}) collective-permute-start(bf16[64,512]{1,0:T(8,128)(2,1)S(1)} %collective-permute-done.34.refs_3_), channel_id=1, source_target_pairs={{0,4},{4,0},{8,12},{12,8},{16,20},{20,16},{24,28},{28,24},{1,5},{5... | collective-permute-start | bytes 196616 | tf_op jit(solution)/shard_map/ppermute | solution.py:65
  118.8 4.3 %collective-permute-start.37 = (bf16[64,512]{1,0:T(8,128)(2,1)S(1)}, bf16[64,512]{1,0:T(8,128)(2,1)S(1)}, u32[]{:S(2)}, u32[]{:S(2)}) collective-permute-start(bf16[64,512]{1,0:T(8,128)(2,1)S(1)} %collective-permute-done.33.refs_2_), channel_id=1, source_target_pairs={{0,4},{4,0},{8,12},{12,8},{16,20},{20,16},{24,28},{28,24},{1,5},{5... | collective-permute-start | bytes 196616 | tf_op jit(solution)/shard_map/ppermute | solution.py:65
  119.5 4.3 %collective-permute-start.36 = (bf16[64,512]{1,0:T(8,128)(2,1)S(1)}, bf16[64,512]{1,0:T(8,128)(2,1)S(1)}, u32[]{:S(2)}, u32[]{:S(2)}) collective-permute-start(bf16[64,512]{1,0:T(8,128)(2,1)S(1)} %collective-permute-done.32.refs_1_), channel_id=1, source_target_pairs={{0,4},{4,0},{8,12},{12,8},{16,20},{20,16},{24,28},{28,24},{1,5},{5... | collective-permute-start | bytes 196616 | tf_op jit(solution)/shard_map/ppermute | solution.py:65
  124.8 1.4 %collective-permute-start.39 = (bf16[64,1024]{1,0:T(8,128)(2,1)S(1)}, bf16[64,1024]{1,0:T(8,128)(2,1)S(1)}, u32[]{:S(2)}, u32[]{:S(2)}) collective-permute-start(bf16[64,1024]{1,0:T(8,128)(2,1)S(1)} %shard_map.149.part), channel_id=1, source_target_pairs={{0,1},{1,0},{2,3},{3,2},{4,5},{5,4},{6,7},{7,6},{8,9},{9,8},{10,11... | collective-permute-start | bytes 393224 | tf_op jit(solution)/shard_map/ppermute | solution.py:410
  126.2 5.6 %collective-permute-start.40 = (bf16[64,1024]{1,0:T(8,128)(2,1)S(1)}, bf16[64,1024]{1,0:T(8,128)(2,1)S(1)}, u32[]{:S(2)}, u32[]{:S(2)}) collective-permute-start(bf16[64,1024]{1,0:T(8,128)(2,1)S(1)} %shard_map.150.refs_0_), channel_id=1, source_target_pairs={{0,2},{1,3},{2,0},{3,1},{4,6},{5,7},{6,4},{7,5},{8,10},{9,11},{10,... | collective-permute-start | bytes 393224 | tf_op jit(solution)/shard_map/ppermute | solution.py:410
  132.9 1.5 %collective-permute-start.41 = (bf16[64,1024]{1,0:T(8,128)(2,1)S(1)}, bf16[64,1024]{1,0:T(8,128)(2,1)S(1)}, u32[]{:S(2)}, u32[]{:S(2)}) collective-permute-start(bf16[64,1024]{1,0:T(8,128)(2,1)S(1)} %get-tuple-element.82.part), channel_id=1, source_target_pairs={{0,1},{1,0},{2,3},{3,2},{4,5},{5,4},{6,7},{7,6},{8,9},{9,8},{10,11... | collective-permute-start | bytes 393224 | tf_op jit(solution)/shard_map/ppermute | solution.py:410
  133.0 5.9 %collective-permute-start.43 = (bf16[256,256]{1,0:T(8,128)(2,1)S(1)}, bf16[256,256]{1,0:T(8,128)(2,1)S(1)}, u32[]{:S(2)}, u32[]{:S(2)}) collective-permute-start(bf16[256,256]{1,0:T(8,128)(2,1)S(1)} %get-tuple-element.83.refs_2_), channel_id=1, source_target_pairs={{0,4},{4,0},{8,12},{12,8},{16,20},{20,16},{24,28},{28,24},{1,5},{5... | collective-permute-start | bytes 393224 | tf_op jit(solution)/shard_map/ppermute | solution.py:65
  134.4 5.6 %collective-permute-start.42 = (bf16[64,1024]{1,0:T(8,128)(2,1)S(1)}, bf16[64,1024]{1,0:T(8,128)(2,1)S(1)}, u32[]{:S(2)}, u32[]{:S(2)}) collective-permute-start(bf16[64,1024]{1,0:T(8,128)(2,1)S(1)} %shard_map.152.refs_0_), channel_id=1, source_target_pairs={{0,2},{1,3},{2,0},{3,1},{4,6},{5,7},{6,4},{7,5},{8,10},{9,11},{10,... | collective-permute-start | bytes 393224 | tf_op jit(solution)/shard_map/ppermute | solution.py:410
  (9 other events, 197.6 us)

commit v2 on v1

--- a/solution.py
+++ b/solution.py
@@ -10,7 +10,7 @@
 HEAD_DIM = 64
 STATS = 4
 VMEM_BYTES = 10 << 20
-LOAD_BYTES = 51 << 20
+LOAD_BYTES = 54 << 20
 CHUNKS = 2
 WIDEST = 8
 epsilon = 1e-05
@@ -112,11 +112,10 @@
     )
 
 
-def chunk_kernel(chunk, count, first_half, carried, *refs):
+def chunk_kernel(chunk, count, first_half, carried, last, *refs):
     queries, key_w, value_w = refs[:3]
     blocks, owners, refs = refs[3 : 3 + count], refs[3 + count : 3 + 2 * count], refs[3 + 2 * count :]
     carry, outs = (refs[:2], refs[2:]) if carried else (None, refs)
-    outs = outs if first_half else (outs[0], outs[3], outs[4], outs[1], outs[2])
     out, keys, values = outs[:3]
     rows, width = out.shape[0], blocks[0].shape[1]
     served = queries.at[pl.ds(first_half, queries.shape[0] - first_half), :]
@@ -135,16 +134,17 @@
             out[start : start + tile, lanes] = (piece * scale).astype(bf16)
     keys[...] = product(out[...], key_w[...]).astype(bf16)
     values[...] = product(out[...], value_w[...]).astype(bf16).T
-    for found in weighed(served, [keys], [values], carry, first_half):
-        if first_half:
+    for found in weighed(served, [keys], [values], carry, 0):
+        if last:
             store_terms(outs[3], *found)
         else:
             store_carry(outs[3], outs[4], *found)
 
 
-def own_kernel(queries, keys, values, carry_out, carry_stats, out, stats):
+def own_kernel(queries, keys, values, *refs):
+    carry, (out, stats) = refs[:-2] or None, refs[-2:]
     served = queries.at[pl.ds(0, out.shape[1]), :]
-    for found in weighed(served, [keys], [values], (carry_out, carry_stats), 0):
+    for found in weighed(served, [keys], [values], carry, 0):
         store_carry(out, stats, *found)
 
 
@@ -483,20 +483,20 @@
         shaped((columns, part_rows), bf16),
     ]
 
-    def carry_of(latent_rows):
-        return [shaped((columns, latent_rows), f32), shaped((2 * heads, latent_rows), f32)]
-
-    pieces, carry = [], []
+    carry_shapes = [
+        shaped((columns, line_latents), f32),
+        shaped((2 * heads, line_latents), f32),
+    ]
+    pieces, carry, own_carry = [], [], []
     for c in range(chunks):
         last = c + 1 == chunks
-        served = line_latents if last else latent_count
         if c == 0:
             blocks, queries = pass_on(far[c], queries)
         else:
             blocks, pieces[-1] = pass_on(far[c], pieces[-1])
         made = whole_call(
-            functools.partial(chunk_kernel, c, count, line_latents if last else 0, c > 0),
-            results + [line_shape] if last else results[:1] + carry_of(latent_count),
+            functools.partial(chunk_kernel, c, count, line_latents, c > 0, last),
+            results + ([line_shape] if last else carry_shapes),
             queries,
             key_w,
             value_w,
@@ -505,32 +505,31 @@
             *blocks,
             scalars=owners,
             after=carry,
-            scratch=[] if last else [pltpu.VMEM(one.shape, one.dtype) for one in results[1:]],
             cost=pl.CostEstimate(
                 flops=4 * part_rows * width * columns,
                 bytes_accessed=2 * part_rows * width,
-                transcendentals=heads * served * part_rows,
+                transcendentals=heads * line_latents * part_rows,
             ),
         )
-        pieces.append(made[:1])
-        if not last:
-            carry = made[1:]
-    other = pair_swap(made[3])
-    carry = whole_call(
-        own_kernel,
-        carry_of(line_latents),
-        queries,
-        *made[1:3],
-        *carry,
-        cost=pl.CostEstimate(
-            flops=4 * line_latents * part_rows * columns,
-            bytes_accessed=4 * latent_count * columns,
-            transcendentals=heads * line_latents * part_rows,
-        ),
-    )
+        pieces.append(made[:3])
+        carry = made[3:]
+        if last:
+            other = pair_swap(made[3])
+        own_carry = whole_call(
+            own_kernel,
+            carry_shapes,
+            queries,
+            *pieces[-1][1:3],
+            *own_carry,
+            cost=pl.CostEstimate(
+                flops=4 * line_latents * part_rows * columns,
+                bytes_accessed=4 * latent_count * columns,
+                transcendentals=heads * line_latents * part_rows,
+            ),
+        )
     line_count = shards // 2
     first_parts = whole_call(
-        functools.partial(fold_kernel, rows), [packed_shape] * line_count, *carry, other
+        functools.partial(fold_kernel, rows), [packed_shape] * line_count, *own_carry, other
     )
     key_values = [None] + [
         whole_call(
@@ -547,6 +546,10 @@
         )
         for p in range(1, passes)
     ]
+    swapped = [None]
+    for keys, values in key_values[1:]:
+        keys = pair_swap(keys)
+        swapped.append((keys, pair_swap(values)))
     for p in range(passes):
         if p == 0:
             parts = line_return(first_parts)
@@ -558,13 +561,13 @@
                 results,
                 *queries,
                 keys,
-                pair_swap(keys),
+                swapped[p][0],
                 values,
-                pair_swap(values),
+                swapped[p][1],
             )
             parts = line_return(parts)
             if p == 1:
-                first_share = share
+                shares = [share, pair_swap(share)]
         part = whole_call(functools.partial(merge_kernel, p), part_shape, *parts, cross_out)
         state, query, both = whole_call(
             functools.partial(project_kernel, p, scale),
@@ -581,11 +584,12 @@
             blocks = line_gather(both)
             blocks = blocks + [pair_swap(block) for block in blocks]
         part = whole_call(functools.partial(attend_kernel, p), part_shape, query, *blocks, self_out)
+        parts = heads_parts(part)
         state, part = whole_call(
             functools.partial(mlp_kernel, p),
             (state_shape, part_shape),
             state,
-            *heads_parts(part),
+            *parts,
             mlp_in,
             mlp_out,
         )
@@ -606,8 +610,7 @@
                 (state_shape, shaped((latent_count, columns), f32)),
                 state,
                 *parts,
-                first_share,
-                pair_swap(first_share),
+                *shares,
                 scalars=(me,),
             )
     return (state, midway)

time: 141 us -> 139 us (0.986)
  waiting for transfers between devices: 68.5 us -> 65 us
  local copies, waits for them, and re-layouts: 3.64 us -> 5.2 us
    unnamed x26 -> x30, local copies, waits for them, and re-layouts: 1.79 us -> 4.14 us
    ppermute x2, waiting for transfers between devices: 5.12 us -> 3.1 us  [shifted(): lax.ppermute(value, axis, [(i, (i + step) % count) for i in range(count)])]
    pallas_call x23 -> x24, Pallas kernels: 24.1 us -> 23.4 us  [whole_call(): pl.pallas_call(body, out_shape=results, in_specs=specs, out_specs=jax.tre...]
  transfers between devices with their start and end apart: 44 -> 44, of which waited for: 31 -> 30; matrix products, arithmetic and copies ran while one was open for 0% -> 0% of each run, Pallas kernels for 8% -> 8%
where the time goes in v2:
time: 139 us; the launch traced here: 138 us
  waiting for transfers between devices  65 us (47%)
  starting transfers between devices  43.9 us (32%)
  Pallas kernels  23.4 us (17%)
  local copies, waits for them, and re-layouts  5.2 us (4%)
    ppermute x12, waiting for transfers between devices, from_bits(): return lax.ppermute(value, 'heads', [(i, i ^ bits) for i in range(count)])  26.5 us
    pallas_call x24, Pallas kernels, whole_call(): pl.pallas_call(body, out_shape=results, in_specs=specs, out_specs=jax.tre...  23.4 us
    ppermute x12, waiting for transfers between devices, pair_swap(): return lax.ppermute(value, 'frames', [(i, i ^ 1) for i in range(count)])  18.7 us
    ppermute x15, starting transfers between devices, line_shift(): lax.ppermute(value, 'frames', [(i, (i + 2 * step) % count) for i in range...  15.5 us
    ppermute x15, waiting for transfers between devices, line_shift(): lax.ppermute(value, 'frames', [(i, (i + 2 * step) % count) for i in range...  15.2 us
    ppermute x12, starting transfers between devices, pair_swap(): return lax.ppermute(value, 'frames', [(i, i ^ 1) for i in range(count)])  13.7 us
    ppermute x12, starting transfers between devices, from_bits(): return lax.ppermute(value, 'heads', [(i, i ^ bits) for i in range(count)])  9.89 us
    ppermute x2, starting transfers between devices, shifted(): lax.ppermute(value, axis, [(i, (i + step) % count) for i in range(count)])  4.8 us
  transfers between devices with their start and end apart: 44, of which 30 were waited for; matrix products, arithmetic and copies ran while one was open for 0% of the time, Pallas kernels for 8%

profile of v2, /device:TPU:0, one launch (start us, length us, event | category | flops | bytes accessed | tf_op | source)
XLA Modules:
  0.0 138.5 jit_solution(12521401767093806958)
XLA Ops:
  1.7 3.1 %collective-permute-start = (bf16[512,256]{1,0:T(8,128)(2,1)S(1)}, bf16[512,256]{1,0:T(8,128)(2,1)S(1)}, u32[]{:S(2)}, u32[]{:S(2)}) collective-permute-start(bf16[512,256]{1,0:T(8,128)(2,1)S(1)} %get-tuple-element.93), channel_id=1, source_target_pairs={{0,2},{1,3},{2,0},{3,1},{4,6},{5,7},{6,4},{7,5},{8,10},{9,11},{10,... | collective-permute-start | bytes 786440 | tf_op jit(solution)/shard_map/ppermute | solution.py:22
  4.8 3.6 %shard_map.131 = (f32[64,1024]{1,0:T(8,128)}, bf16[512,256]{1,0:T(8,128)(2,1)}, bf16[1024,256]{1,0:T(8,128)(2,1)}, bf16[1024,256]{1,0:T(8,128)(2,1)}, bf16[1024,256]{1,0:T(8,128)(2,1)}) custom-call(bf16[1024,256]{1,0:T(8,128)(2,1)} %frames_hbm.1, bf16[2,1024,256]{2,1,0:T(8,128)(2,1)} %refs_2_.9, bf16[2,1024,256]{2,1,0:T(8,128)(2,1)} %refs_3_.7, ...), custom_call_target="tpu_custom_call" | custom-call | flops 268435456 | bytes 1048576 | tf_op jit(solution)/shard_map/pallas_call | solution.py:80
  8.4 2.7 %collective-permute-done.refs_5_ = bf16[512,256]{1,0:T(8,128)(2,1)S(1)} collective-permute-done((bf16[512,256]{1,0:T(8,128)(2,1)S(1)}, bf16[512,256]{1,0:T(8,128)(2,1)S(1)}, u32[]{:S(2)}, u32[]{:S(2)}) %collective-permute-start) | collective-permute-done | bytes 262176 | tf_op jit(solution)/shard_map/ppermute | solution.py:22
  11.1 1.7 %collective-permute-start.2 = (bf16[512,256]{1,0:T(8,128)(2,1)S(1)}, bf16[512,256]{1,0:T(8,128)(2,1)S(1)}, u32[]{:S(2)}, u32[]{:S(2)}) collective-permute-start(bf16[512,256]{1,0:T(8,128)(2,1)S(1)} %get-tuple-element.92), channel_id=1, source_target_pairs={{0,2},{1,3},{2,0},{3,1},{4,6},{5,7},{6,4},{7,5},{8,10},{9,11},{10,... | collective-permute-start | bytes 786440 | tf_op jit(solution)/shard_map/ppermute | solution.py:22
  16.9 2.4 %shard_map.132 = (bf16[512,1024]{1,0:T(8,128)(2,1)S(1)}, bf16[512,256]{1,0:T(8,128)(2,1)S(1)}, bf16[256,512]{1,0:T(8,128)(2,1)S(1)}, f32[256,256]{1,0:T(8,128)S(1)}, f32[8,256]{1,0:T(8,128)S(1)}) custom-call(bf16[512,256]{1,0:T(8,128)(2,1)S(1)} %copy-done.10, bf16[1024,256]{1,0:T(8,128)(2,1)S(1)} %copy-done.12, bf16[1024,256]{1,0:T(8,128)(2,1)S(1)} %copy-done.13, ...), custom_call_target="tpu_custom_call" | custom-call | flops 536870912 | bytes 1048576 | tf_op jit(solution)/shard_map/pallas_call | solution.py:80
  19.8 1.5 %collective-permute-done.4.refs_6_ = bf16[512,256]{1,0:T(8,128)(2,1)S(1)} collective-permute-done((bf16[512,256]{1,0:T(8,128)(2,1)S(1)}, bf16[512,256]{1,0:T(8,128)(2,1)S(1)}, u32[]{:S(2)}, u32[]{:S(2)}) %collective-permute-start.4) | collective-permute-done | bytes 262176 | tf_op jit(solution)/shard_map/ppermute | solution.py:72
  21.3 2.4 %shard_map.133 = (bf16[512,1024]{1,0:T(8,128)(2,1)S(1)}, bf16[512,256]{1,0:T(8,128)(2,1)S(1)}, bf16[256,512]{1,0:T(8,128)(2,1)S(1)}, bf16[272,256]{1,0:T(8,128)(2,1)S(1)}) custom-call(bf16[512,256]{1,0:T(8,128)(2,1)S(1)} %copy-done.10, bf16[1024,256]{1,0:T(8,128)(2,1)S(1)} %copy-done.12, bf16[1024,256]{1,0:T(8,128)(2,1)S(1)} %copy-done.13, ...), custom_call_target="tpu_custom_call" | custom-call | flops 536870912 | bytes 1048576 | tf_op jit(solution)/shard_map/pallas_call | solution.py:80
  23.8 1.8 %collective-permute-start.5 = (bf16[272,256]{1,0:T(8,128)(2,1)S(1)}, bf16[272,256]{1,0:T(8,128)(2,1)S(1)}, u32[]{:S(2)}, u32[]{:S(2)}) collective-permute-start(bf16[272,256]{1,0:T(8,128)(2,1)S(1)} %get-tuple-element.66), channel_id=1, source_target_pairs={{0,4},{4,0},{8,12},{12,8},{16,20},{20,16},{24,28},{28,24},{1,5},{5... | collective-permute-start | bytes 417800 | tf_op jit(solution)/shard_map/ppermute | solution.py:65
  27.9 1.6 %collective-permute-done.5.other = bf16[272,256]{1,0:T(8,128)(2,1)S(1)} collective-permute-done((bf16[272,256]{1,0:T(8,128)(2,1)S(1)}, bf16[272,256]{1,0:T(8,128)(2,1)S(1)}, u32[]{:S(2)}, u32[]{:S(2)}) %collective-permute-start.5) | collective-permute-done | bytes 139296 | tf_op jit(solution)/shard_map/ppermute | solution.py:65
  29.7 3.9 %collective-permute-start.6 = (bf16[80,256]{1,0:T(8,128)(2,1)S(1)}, bf16[80,256]{1,0:T(8,128)(2,1)S(1)}, u32[]{:S(2)}, u32[]{:S(2)}) collective-permute-start(bf16[80,256]{1,0:T(8,128)(2,1)S(1)} %get-tuple-element.68), channel_id=1, source_target_pairs={{0,24},{4,28},{8,0},{12,4},{16,8},{20,12},{24,16},{28,20},{1,25},{... | collective-permute-start | bytes 122888 | tf_op jit(solution)/shard_map/ppermute | solution.py:43
  35.2 3.2 %collective-permute-done.7.refs_2_ = bf16[80,256]{1,0:T(8,128)(2,1)S(1)} collective-permute-done((bf16[80,256]{1,0:T(8,128)(2,1)S(1)}, bf16[80,256]{1,0:T(8,128)(2,1)S(1)}, u32[]{:S(2)}, u32[]{:S(2)}) %collective-permute-start.7) | collective-permute-done | bytes 40992 | tf_op jit(solution)/shard_map/ppermute | solution.py:43
  40.1 1.3 collective-permute-done.9.other
  41.4 1.6 %collective-permute-start.10 = (bf16[64,1024]{1,0:T(8,128)(2,1)S(1)}, bf16[64,1024]{1,0:T(8,128)(2,1)S(1)}, u32[]{:S(2)}, u32[]{:S(2)}) collective-permute-start(bf16[64,1024]{1,0:T(8,128)(2,1)S(1)} %shard_map.138.refs_0_), channel_id=1, source_target_pairs={{0,2},{1,3},{2,0},{3,1},{4,6},{5,7},{6,4},{7,5},{8,10},{9,11},{10,... | collective-permute-start | bytes 393224 | tf_op jit(solution)/shard_map/ppermute | solution.py:410
  43.0 4.0 %collective-permute-done.10.refs_1_ = bf16[64,1024]{1,0:T(8,128)(2,1)S(1)} collective-permute-done((bf16[64,1024]{1,0:T(8,128)(2,1)S(1)}, bf16[64,1024]{1,0:T(8,128)(2,1)S(1)}, u32[]{:S(2)}, u32[]{:S(2)}) %collective-permute-start.10) | collective-permute-done | bytes 131104 | tf_op jit(solution)/shard_map/ppermute | solution.py:410
  48.9 1.9 %collective-permute-start.11 = (bf16[64,512]{1,0:T(8,128)(2,1)S(1)}, bf16[64,512]{1,0:T(8,128)(2,1)S(1)}, u32[]{:S(2)}, u32[]{:S(2)}) collective-permute-start(bf16[64,512]{1,0:T(8,128)(2,1)S(1)} %get-tuple-element.73.refs_0_), channel_id=1, source_target_pairs={{0,8},{4,12},{8,16},{12,20},{16,24},{20,28},{24,0},{28,4},{1,9},{5... | collective-permute-start | bytes 196616 | tf_op jit(solution)/shard_map/ppermute | solution.py:43
  50.9 1.5 %collective-permute-start.14 = (bf16[64,512]{1,0:T(8,128)(2,1)S(1)}, bf16[64,512]{1,0:T(8,128)(2,1)S(1)}, u32[]{:S(2)}, u32[]{:S(2)}) collective-permute-start(bf16[64,512]{1,0:T(8,128)(2,1)S(1)} %get-tuple-element.73.refs_0_), channel_id=1, source_target_pairs={{0,4},{4,0},{8,12},{12,8},{16,20},{20,16},{24,28},{28,24},{1,5},{5... | collective-permute-start | bytes 196616 | tf_op jit(solution)/shard_map/ppermute | solution.py:65
  52.5 1.5 %collective-permute-start.17 = (bf16[64,512]{1,0:T(8,128)(2,1)S(1)}, bf16[64,512]{1,0:T(8,128)(2,1)S(1)}, u32[]{:S(2)}, u32[]{:S(2)}) collective-permute-start(bf16[64,512]{1,0:T(8,128)(2,1)S(1)} %collective-permute-done.13.refs_3_), channel_id=1, source_target_pairs={{0,4},{4,0},{8,12},{12,8},{16,20},{20,16},{24,28},{28,24},{1,5},{5... | collective-permute-start | bytes 196616 | tf_op jit(solution)/shard_map/ppermute | solution.py:65
  54.0 1.7 %collective-permute-done.12.refs_2_ = bf16[64,512]{1,0:T(8,128)(2,1)S(1)} collective-permute-done((bf16[64,512]{1,0:T(8,128)(2,1)S(1)}, bf16[64,512]{1,0:T(8,128)(2,1)S(1)}, u32[]{:S(2)}, u32[]{:S(2)}) %collective-permute-start.12) | collective-permute-done | bytes 65568 | tf_op jit(solution)/shard_map/ppermute | solution.py:43
  55.7 1.5 %collective-permute-start.16 = (bf16[64,512]{1,0:T(8,128)(2,1)S(1)}, bf16[64,512]{1,0:T(8,128)(2,1)S(1)}, u32[]{:S(2)}, u32[]{:S(2)}) collective-permute-start(bf16[64,512]{1,0:T(8,128)(2,1)S(1)} %collective-permute-done.12.refs_2_), channel_id=1, source_target_pairs={{0,4},{4,0},{8,12},{12,8},{16,20},{20,16},{24,28},{28,24},{1,5},{5... | collective-permute-start | bytes 196616 | tf_op jit(solution)/shard_map/ppermute | solution.py:65
  57.7 2.2 %collective-permute-done.16.refs_6_ = bf16[64,512]{1,0:T(8,128)(2,1)S(1)} collective-permute-done((bf16[64,512]{1,0:T(8,128)(2,1)S(1)}, bf16[64,512]{1,0:T(8,128)(2,1)S(1)}, u32[]{:S(2)}, u32[]{:S(2)}) %collective-permute-start.16) | collective-permute-done | bytes 65568 | tf_op jit(solution)/shard_map/ppermute | solution.py:65
  59.9 1.5 %collective-permute-done.15.refs_5_ = bf16[64,512]{1,0:T(8,128)(2,1)S(1)} collective-permute-done((bf16[64,512]{1,0:T(8,128)(2,1)S(1)}, bf16[64,512]{1,0:T(8,128)(2,1)S(1)}, u32[]{:S(2)}, u32[]{:S(2)}) %collective-permute-start.15) | collective-permute-done | bytes 65568 | tf_op jit(solution)/shard_map/ppermute | solution.py:65
  62.6 1.3 shard_map.145
  64.7 1.3 collective-permute-start.26
  66.0 1.6 %collective-permute-start.19 = (bf16[64,1024]{1,0:T(8,128)(2,1)S(1)}, bf16[64,1024]{1,0:T(8,128)(2,1)S(1)}, u32[]{:S(2)}, u32[]{:S(2)}) collective-permute-start(bf16[64,1024]{1,0:T(8,128)(2,1)S(1)} %shard_map.141.refs_0_), channel_id=1, source_target_pairs={{0,2},{1,3},{2,0},{3,1},{4,6},{5,7},{6,4},{7,5},{8,10},{9,11},{10,... | collective-permute-start | bytes 393224 | tf_op jit(solution)/shard_map/ppermute | solution.py:410
  67.6 3.8 %collective-permute-done.19.refs_1_ = bf16[64,1024]{1,0:T(8,128)(2,1)S(1)} collective-permute-done((bf16[64,1024]{1,0:T(8,128)(2,1)S(1)}, bf16[64,1024]{1,0:T(8,128)(2,1)S(1)}, u32[]{:S(2)}, u32[]{:S(2)}) %collective-permute-start.19) | collective-permute-done | bytes 131104 | tf_op jit(solution)/shard_map/ppermute | solution.py:410
  72.5 1.3 collective-permute-done.20.other
  73.9 1.6 %collective-permute-start.21 = (bf16[64,1024]{1,0:T(8,128)(2,1)S(1)}, bf16[64,1024]{1,0:T(8,128)(2,1)S(1)}, u32[]{:S(2)}, u32[]{:S(2)}) collective-permute-start(bf16[64,1024]{1,0:T(8,128)(2,1)S(1)} %shard_map.143.refs_0_), channel_id=1, source_target_pairs={{0,2},{1,3},{2,0},{3,1},{4,6},{5,7},{6,4},{7,5},{8,10},{9,11},{10,... | collective-permute-start | bytes 393224 | tf_op jit(solution)/shard_map/ppermute | solution.py:410
  75.5 4.0 %collective-permute-done.21.refs_1_ = bf16[64,1024]{1,0:T(8,128)(2,1)S(1)} collective-permute-done((bf16[64,1024]{1,0:T(8,128)(2,1)S(1)}, bf16[64,1024]{1,0:T(8,128)(2,1)S(1)}, u32[]{:S(2)}, u32[]{:S(2)}) %collective-permute-start.21) | collective-permute-done | bytes 131104 | tf_op jit(solution)/shard_map/ppermute | solution.py:410
  79.9 1.3 collective-permute-start.24
  82.0 7.5 %collective-permute-done.26.refs_7_ = bf16[256,1024]{1,0:T(8,128)(2,1)S(1)} collective-permute-done((bf16[256,1024]{1,0:T(8,128)(2,1)S(1)}, bf16[256,1024]{1,0:T(8,128)(2,1)S(1)}, u32[]{:S(2)}, u32[]{:S(2)}) %collective-permute-start.26) | collective-permute-done | bytes 524320 | tf_op jit(solution)/shard_map/ppermute | solution.py:65
  89.5 3.2 %shard_map.146 = (bf16[80,256]{1,0:T(8,128)(2,1)S(1)}, bf16[80,256]{1,0:T(8,128)(2,1)S(1)}, bf16[80,256]{1,0:T(8,128)(2,1)S(1)}, bf16[80,256]{1,0:T(8,128)(2,1)S(1)}, bf16[256,256]{1,0:T(8,128)(2,1)S(1)}) custom-call(bf16[64,512]{1,0:T(8,128)(2,1)S(1)} %get-tuple-element.77.refs_0_, bf16[64,512]{1,0:T(8,128)(2,1)S(1)} %collective-permute-done.22.refs_1_, ...), custom_call_target="tpu_custom_call" | custom-call | tf_op jit(solution)/shard_map/pallas_call | solution.py:80
  92.7 1.3 collective-permute-start.27
  94.8 2.0 %collective-permute-done.27.refs_1_ = bf16[80,256]{1,0:T(8,128)(2,1)S(1)} collective-permute-done((bf16[80,256]{1,0:T(8,128)(2,1)S(1)}, bf16[80,256]{1,0:T(8,128)(2,1)S(1)}, u32[]{:S(2)}, u32[]{:S(2)}) %collective-permute-start.27) | collective-permute-done | bytes 40992 | tf_op jit(solution)/shard_map/ppermute | solution.py:43
  96.8 2.6 %collective-permute-done.28.refs_2_ = bf16[80,256]{1,0:T(8,128)(2,1)S(1)} collective-permute-done((bf16[80,256]{1,0:T(8,128)(2,1)S(1)}, bf16[80,256]{1,0:T(8,128)(2,1)S(1)}, u32[]{:S(2)}, u32[]{:S(2)}) %collective-permute-start.28) | collective-permute-done | bytes 40992 | tf_op jit(solution)/shard_map/ppermute | solution.py:43
  100.5 1.3 collective-permute-done.30.other
  101.9 1.6 %collective-permute-start.31 = (bf16[64,1024]{1,0:T(8,128)(2,1)S(1)}, bf16[64,1024]{1,0:T(8,128)(2,1)S(1)}, u32[]{:S(2)}, u32[]{:S(2)}) collective-permute-start(bf16[64,1024]{1,0:T(8,128)(2,1)S(1)} %shard_map.148.refs_0_), channel_id=1, source_target_pairs={{0,2},{1,3},{2,0},{3,1},{4,6},{5,7},{6,4},{7,5},{8,10},{9,11},{10,... | collective-permute-start | bytes 393224 | tf_op jit(solution)/shard_map/ppermute | solution.py:410
  103.4 4.0 %collective-permute-done.31.refs_1_ = bf16[64,1024]{1,0:T(8,128)(2,1)S(1)} collective-permute-done((bf16[64,1024]{1,0:T(8,128)(2,1)S(1)}, bf16[64,1024]{1,0:T(8,128)(2,1)S(1)}, u32[]{:S(2)}, u32[]{:S(2)}) %collective-permute-start.31) | collective-permute-done | bytes 131104 | tf_op jit(solution)/shard_map/ppermute | solution.py:410
  108.0 1.4 %collective-permute-start.34 = (bf16[64,512]{1,0:T(8,128)(2,1)S(1)}, bf16[64,512]{1,0:T(8,128)(2,1)S(1)}, u32[]{:S(2)}, u32[]{:S(2)}) collective-permute-start(bf16[64,512]{1,0:T(8,128)(2,1)S(1)} %get-tuple-element.88.refs_0_), channel_id=1, source_target_pairs={{0,24},{4,28},{8,0},{12,4},{16,8},{20,12},{24,16},{28,20},{1,25},{... | collective-permute-start | bytes 196616 | tf_op jit(solution)/shard_map/ppermute | solution.py:43
  109.6 1.7 %collective-permute-start.32 = (bf16[64,512]{1,0:T(8,128)(2,1)S(1)}, bf16[64,512]{1,0:T(8,128)(2,1)S(1)}, u32[]{:S(2)}, u32[]{:S(2)}) collective-permute-start(bf16[64,512]{1,0:T(8,128)(2,1)S(1)} %get-tuple-element.88.refs_0_), channel_id=1, source_target_pairs={{0,8},{4,12},{8,16},{12,20},{16,24},{20,28},{24,0},{28,4},{1,9},{5... | collective-permute-start | bytes 196616 | tf_op jit(solution)/shard_map/ppermute | solution.py:43
  113.4 2.8 %collective-permute-done.33.refs_2_ = bf16[64,512]{1,0:T(8,128)(2,1)S(1)} collective-permute-done((bf16[64,512]{1,0:T(8,128)(2,1)S(1)}, bf16[64,512]{1,0:T(8,128)(2,1)S(1)}, u32[]{:S(2)}, u32[]{:S(2)}) %collective-permute-start.33) | collective-permute-done | bytes 65568 | tf_op jit(solution)/shard_map/ppermute | solution.py:43
  117.0 1.3 collective-permute-start.36
  118.3 2.2 %collective-permute-done.37.refs_6_ = bf16[64,512]{1,0:T(8,128)(2,1)S(1)} collective-permute-done((bf16[64,512]{1,0:T(8,128)(2,1)S(1)}, bf16[64,512]{1,0:T(8,128)(2,1)S(1)}, u32[]{:S(2)}, u32[]{:S(2)}) %collective-permute-start.37) | collective-permute-done | bytes 65568 | tf_op jit(solution)/shard_map/ppermute | solution.py:65
  122.4 1.3 collective-permute-done.39.other
  123.7 1.6 %collective-permute-start.40 = (bf16[64,1024]{1,0:T(8,128)(2,1)S(1)}, bf16[64,1024]{1,0:T(8,128)(2,1)S(1)}, u32[]{:S(2)}, u32[]{:S(2)}) collective-permute-start(bf16[64,1024]{1,0:T(8,128)(2,1)S(1)} %shard_map.151.refs_0_), channel_id=1, source_target_pairs={{0,2},{1,3},{2,0},{3,1},{4,6},{5,7},{6,4},{7,5},{8,10},{9,11},{10,... | collective-permute-start | bytes 393224 | tf_op jit(solution)/shard_map/ppermute | solution.py:410
  125.3 4.0 %collective-permute-done.40.refs_1_ = bf16[64,1024]{1,0:T(8,128)(2,1)S(1)} collective-permute-done((bf16[64,1024]{1,0:T(8,128)(2,1)S(1)}, bf16[64,1024]{1,0:T(8,128)(2,1)S(1)}, u32[]{:S(2)}, u32[]{:S(2)}) %collective-permute-start.40) | collective-permute-done | bytes 131104 | tf_op jit(solution)/shard_map/ppermute | solution.py:410
  130.5 1.4 %collective-permute-start.43 = (bf16[256,256]{1,0:T(8,128)(2,1)S(1)}, bf16[256,256]{1,0:T(8,128)(2,1)S(1)}, u32[]{:S(2)}, u32[]{:S(2)}) collective-permute-start(bf16[256,256]{1,0:T(8,128)(2,1)S(1)} %get-tuple-element.91.refs_2_), channel_id=1, source_target_pairs={{0,4},{4,0},{8,12},{12,8},{16,20},{20,16},{24,28},{28,24},{1,5},{5... | collective-permute-start | bytes 393224 | tf_op jit(solution)/shard_map/ppermute | solution.py:65
  131.9 1.6 %collective-permute-start.42 = (bf16[64,1024]{1,0:T(8,128)(2,1)S(1)}, bf16[64,1024]{1,0:T(8,128)(2,1)S(1)}, u32[]{:S(2)}, u32[]{:S(2)}) collective-permute-start(bf16[64,1024]{1,0:T(8,128)(2,1)S(1)} %shard_map.153.refs_0_), channel_id=1, source_target_pairs={{0,2},{1,3},{2,0},{3,1},{4,6},{5,7},{6,4},{7,5},{8,10},{9,11},{10,... | collective-permute-start | bytes 393224 | tf_op jit(solution)/shard_map/ppermute | solution.py:410
  133.5 2.9 %collective-permute-done.43.refs_3_ = bf16[256,256]{1,0:T(8,128)(2,1)S(1)} collective-permute-done((bf16[256,256]{1,0:T(8,128)(2,1)S(1)}, bf16[256,256]{1,0:T(8,128)(2,1)S(1)}, u32[]{:S(2)}, u32[]{:S(2)}) %collective-permute-start.43) | collective-permute-done | bytes 131104 | tf_op jit(solution)/shard_map/ppermute | solution.py:65
  (95 shorter events, 28.7 us)
Async XLA Ops:
  1.7 9.4 %collective-permute-start = (bf16[512,256]{1,0:T(8,128)(2,1)S(1)}, bf16[512,256]{1,0:T(8,128)(2,1)S(1)}, u32[]{:S(2)}, u32[]{:S(2)}) collective-permute-start(bf16[512,256]{1,0:T(8,128)(2,1)S(1)} %get-tuple-element.93), channel_id=1, source_target_pairs={{0,2},{1,3},{2,0},{3,1},{4,6},{5,7},{6,4},{7,5},{8,10},{9,11},{10,... | collective-permute-start | bytes 786440 | tf_op jit(solution)/shard_map/ppermute | solution.py:22
  4.8 8.1 %collective-permute-start.1 = (bf16[1024,256]{1,0:T(8,128)(2,1)}, bf16[1024,256]{1,0:T(8,128)(2,1)S(1)}, u32[]{:S(2)}, u32[]{:S(2)}) collective-permute-start(bf16[1024,256]{1,0:T(8,128)(2,1)} %frames_hbm.1), channel_id=1, source_target_pairs={{0,1},{1,0},{2,3},{3,2},{4,5},{5,4},{6,7},{7,6},{8,9},{9,8},{10,11... | collective-permute-start | bytes 1572872 | tf_op jit(solution)/shard_map/ppermute | solution.py:476
  11.1 1.8 %collective-permute-start.3 = (bf16[512,256]{1,0:T(8,128)(2,1)S(1)}, bf16[512,256]{1,0:T(8,128)(2,1)S(1)}, u32[]{:S(2)}, u32[]{:S(2)}) collective-permute-start(bf16[512,256]{1,0:T(8,128)(2,1)S(1)} %collective-permute-done.refs_5_), channel_id=1, source_target_pairs={{0,1},{1,0},{2,3},{3,2},{4,5},{5,4},{6,7},{7,6},{8,9},{9,8},{10,11... | collective-permute-start | bytes 786440 | tf_op jit(solution)/shard_map/ppermute | solution.py:72
  11.1 8.7 %collective-permute-start.2 = (bf16[512,256]{1,0:T(8,128)(2,1)S(1)}, bf16[512,256]{1,0:T(8,128)(2,1)S(1)}, u32[]{:S(2)}, u32[]{:S(2)}) collective-permute-start(bf16[512,256]{1,0:T(8,128)(2,1)S(1)} %get-tuple-element.92), channel_id=1, source_target_pairs={{0,2},{1,3},{2,0},{3,1},{4,6},{5,7},{6,4},{7,5},{8,10},{9,11},{10,... | collective-permute-start | bytes 786440 | tf_op jit(solution)/shard_map/ppermute | solution.py:22
  19.3 27.7 %copy-start.2 = (bf16[2,1024,256]{2,1,0:T(8,128)(2,1)S(1)}, bf16[2,1024,256]{2,1,0:T(8,128)(2,1)}, u32[]{:S(2)}) copy-start(bf16[2,1024,256]{2,1,0:T(8,128)(2,1)} %refs_2_.10) | copy-start | bytes 3145732
  19.8 1.5 %collective-permute-start.4 = (bf16[512,256]{1,0:T(8,128)(2,1)S(1)}, bf16[512,256]{1,0:T(8,128)(2,1)S(1)}, u32[]{:S(2)}, u32[]{:S(2)}) collective-permute-start(bf16[512,256]{1,0:T(8,128)(2,1)S(1)} %collective-permute-done.2.refs_5_), channel_id=1, source_target_pairs={{0,1},{1,0},{2,3},{3,2},{4,5},{5,4},{6,7},{7,6},{8,9},{9,8},{10,11... | collective-permute-start | bytes 786440 | tf_op jit(solution)/shard_map/ppermute | solution.py:72
  23.8 37.7 %copy-start.9 = (bf16[2,256,1024]{2,1,0:T(8,128)(2,1)S(1)}, bf16[2,256,1024]{2,1,0:T(8,128)(2,1)}, u32[]{:S(2)}) copy-start(bf16[2,256,1024]{2,1,0:T(8,128)(2,1)} %refs_8_.3) | copy-start | bytes 3145732
  23.8 5.8 %collective-permute-start.5 = (bf16[272,256]{1,0:T(8,128)(2,1)S(1)}, bf16[272,256]{1,0:T(8,128)(2,1)S(1)}, u32[]{:S(2)}, u32[]{:S(2)}) collective-permute-start(bf16[272,256]{1,0:T(8,128)(2,1)S(1)} %get-tuple-element.66), channel_id=1, source_target_pairs={{0,4},{4,0},{8,12},{12,8},{16,20},{20,16},{24,28},{28,24},{1,5},{5... | collective-permute-start | bytes 417800 | tf_op jit(solution)/shard_map/ppermute | solution.py:65
  26.7 35.9 %copy-start.6 = (bf16[2,1024,256]{2,1,0:T(8,128)(2,1)S(1)}, bf16[2,1024,256]{2,1,0:T(8,128)(2,1)}, u32[]{:S(2)}) copy-start(bf16[2,1024,256]{2,1,0:T(8,128)(2,1)} %refs_2_.9) | copy-start | bytes 3145732
  26.7 35.9 %copy-start.7 = (bf16[2,1024,256]{2,1,0:T(8,128)(2,1)S(1)}, bf16[2,1024,256]{2,1,0:T(8,128)(2,1)}, u32[]{:S(2)}) copy-start(bf16[2,1024,256]{2,1,0:T(8,128)(2,1)} %refs_3_.7) | copy-start | bytes 3145732
  29.7 5.5 %collective-permute-start.6 = (bf16[80,256]{1,0:T(8,128)(2,1)S(1)}, bf16[80,256]{1,0:T(8,128)(2,1)S(1)}, u32[]{:S(2)}, u32[]{:S(2)}) collective-permute-start(bf16[80,256]{1,0:T(8,128)(2,1)S(1)} %get-tuple-element.68), channel_id=1, source_target_pairs={{0,24},{4,28},{8,0},{12,4},{16,8},{20,12},{24,16},{28,20},{1,25},{... | collective-permute-start | bytes 122888 | tf_op jit(solution)/shard_map/ppermute | solution.py:43
  33.6 4.9 %collective-permute-start.7 = (bf16[80,256]{1,0:T(8,128)(2,1)S(1)}, bf16[80,256]{1,0:T(8,128)(2,1)S(1)}, u32[]{:S(2)}, u32[]{:S(2)}) collective-permute-start(bf16[80,256]{1,0:T(8,128)(2,1)S(1)} %get-tuple-element.69), channel_id=1, source_target_pairs={{0,16},{4,20},{8,24},{12,28},{16,0},{20,4},{24,8},{28,12},{1,17},{... | collective-permute-start | bytes 122888 | tf_op jit(solution)/shard_map/ppermute | solution.py:43
  33.6 5.8 %collective-permute-start.8 = (bf16[80,256]{1,0:T(8,128)(2,1)S(1)}, bf16[80,256]{1,0:T(8,128)(2,1)S(1)}, u32[]{:S(2)}, u32[]{:S(2)}) collective-permute-start(bf16[80,256]{1,0:T(8,128)(2,1)S(1)} %get-tuple-element.70), channel_id=1, source_target_pairs={{0,8},{4,12},{8,16},{12,20},{16,24},{20,28},{24,0},{28,4},{1,9},{5... | collective-permute-start | bytes 122888 | tf_op jit(solution)/shard_map/ppermute | solution.py:43
  40.0 1.4 %collective-permute-start.9 = (bf16[64,1024]{1,0:T(8,128)(2,1)S(1)}, bf16[64,1024]{1,0:T(8,128)(2,1)S(1)}, u32[]{:S(2)}, u32[]{:S(2)}) collective-permute-start(bf16[64,1024]{1,0:T(8,128)(2,1)S(1)} %shard_map.137.part), channel_id=1, source_target_pairs={{0,1},{1,0},{2,3},{3,2},{4,5},{5,4},{6,7},{7,6},{8,9},{9,8},{10,11... | collective-permute-start | bytes 393224 | tf_op jit(solution)/shard_map/ppermute | solution.py:410
  41.4 5.6 %collective-permute-start.10 = (bf16[64,1024]{1,0:T(8,128)(2,1)S(1)}, bf16[64,1024]{1,0:T(8,128)(2,1)S(1)}, u32[]{:S(2)}, u32[]{:S(2)}) collective-permute-start(bf16[64,1024]{1,0:T(8,128)(2,1)S(1)} %shard_map.138.refs_0_), channel_id=1, source_target_pairs={{0,2},{1,3},{2,0},{3,1},{4,6},{5,7},{6,4},{7,5},{8,10},{9,11},{10,... | collective-permute-start | bytes 393224 | tf_op jit(solution)/shard_map/ppermute | solution.py:410
  47.6 4.8 %collective-permute-start.13 = (bf16[64,512]{1,0:T(8,128)(2,1)S(1)}, bf16[64,512]{1,0:T(8,128)(2,1)S(1)}, u32[]{:S(2)}, u32[]{:S(2)}) collective-permute-start(bf16[64,512]{1,0:T(8,128)(2,1)S(1)} %get-tuple-element.73.refs_0_), channel_id=1, source_target_pairs={{0,24},{4,28},{8,0},{12,4},{16,8},{20,12},{24,16},{28,20},{1,25},{... | collective-permute-start | bytes 196616 | tf_op jit(solution)/shard_map/ppermute | solution.py:43
  48.3 7.3 %collective-permute-start.12 = (bf16[64,512]{1,0:T(8,128)(2,1)S(1)}, bf16[64,512]{1,0:T(8,128)(2,1)S(1)}, u32[]{:S(2)}, u32[]{:S(2)}) collective-permute-start(bf16[64,512]{1,0:T(8,128)(2,1)S(1)} %get-tuple-element.73.refs_0_), channel_id=1, source_target_pairs={{0,16},{4,20},{8,24},{12,28},{16,0},{20,4},{24,8},{28,12},{1,17},{... | collective-permute-start | bytes 196616 | tf_op jit(solution)/shard_map/ppermute | solution.py:43
  48.9 8.3 %collective-permute-start.11 = (bf16[64,512]{1,0:T(8,128)(2,1)S(1)}, bf16[64,512]{1,0:T(8,128)(2,1)S(1)}, u32[]{:S(2)}, u32[]{:S(2)}) collective-permute-start(bf16[64,512]{1,0:T(8,128)(2,1)S(1)} %get-tuple-element.73.refs_0_), channel_id=1, source_target_pairs={{0,8},{4,12},{8,16},{12,20},{16,24},{20,28},{24,0},{28,4},{1,9},{5... | collective-permute-start | bytes 196616 | tf_op jit(solution)/shard_map/ppermute | solution.py:43
  50.9 6.8 %collective-permute-start.14 = (bf16[64,512]{1,0:T(8,128)(2,1)S(1)}, bf16[64,512]{1,0:T(8,128)(2,1)S(1)}, u32[]{:S(2)}, u32[]{:S(2)}) collective-permute-start(bf16[64,512]{1,0:T(8,128)(2,1)S(1)} %get-tuple-element.73.refs_0_), channel_id=1, source_target_pairs={{0,4},{4,0},{8,12},{12,8},{16,20},{20,16},{24,28},{28,24},{1,5},{5... | collective-permute-start | bytes 196616 | tf_op jit(solution)/shard_map/ppermute | solution.py:65
  52.5 5.2 %collective-permute-start.17 = (bf16[64,512]{1,0:T(8,128)(2,1)S(1)}, bf16[64,512]{1,0:T(8,128)(2,1)S(1)}, u32[]{:S(2)}, u32[]{:S(2)}) collective-permute-start(bf16[64,512]{1,0:T(8,128)(2,1)S(1)} %collective-permute-done.13.refs_3_), channel_id=1, source_target_pairs={{0,4},{4,0},{8,12},{12,8},{16,20},{20,16},{24,28},{28,24},{1,5},{5... | collective-permute-start | bytes 196616 | tf_op jit(solution)/shard_map/ppermute | solution.py:65
  55.7 4.3 %collective-permute-start.16 = (bf16[64,512]{1,0:T(8,128)(2,1)S(1)}, bf16[64,512]{1,0:T(8,128)(2,1)S(1)}, u32[]{:S(2)}, u32[]{:S(2)}) collective-permute-start(bf16[64,512]{1,0:T(8,128)(2,1)S(1)} %collective-permute-done.12.refs_2_), channel_id=1, source_target_pairs={{0,4},{4,0},{8,12},{12,8},{16,20},{20,16},{24,28},{28,24},{1,5},{5... | collective-permute-start | bytes 196616 | tf_op jit(solution)/shard_map/ppermute | solution.py:65
  57.2 4.3 %collective-permute-start.15 = (bf16[64,512]{1,0:T(8,128)(2,1)S(1)}, bf16[64,512]{1,0:T(8,128)(2,1)S(1)}, u32[]{:S(2)}, u32[]{:S(2)}) collective-permute-start(bf16[64,512]{1,0:T(8,128)(2,1)S(1)} %collective-permute-done.11.refs_1_), channel_id=1, source_target_pairs={{0,4},{4,0},{8,12},{12,8},{16,20},{20,16},{24,28},{28,24},{1,5},{5... | collective-permute-start | bytes 196616 | tf_op jit(solution)/shard_map/ppermute | solution.py:65
  62.5 3.5 %collective-permute-start.18 = (bf16[64,1024]{1,0:T(8,128)(2,1)S(1)}, bf16[64,1024]{1,0:T(8,128)(2,1)S(1)}, u32[]{:S(2)}, u32[]{:S(2)}) collective-permute-start(bf16[64,1024]{1,0:T(8,128)(2,1)S(1)} %shard_map.140.part), channel_id=1, source_target_pairs={{0,1},{1,0},{2,3},{3,2},{4,5},{5,4},{6,7},{7,6},{8,9},{9,8},{10,11... | collective-permute-start | bytes 393224 | tf_op jit(solution)/shard_map/ppermute | solution.py:410
  63.9 18.1 %collective-permute-start.25 = (bf16[1024,256]{1,0:T(8,128)(2,1)S(1)}, bf16[1024,256]{1,0:T(8,128)(2,1)S(1)}, u32[]{:S(2)}, u32[]{:S(2)}) collective-permute-start(bf16[1024,256]{1,0:T(8,128)(2,1)S(1)} %get-tuple-element.80.refs_4_), channel_id=1, source_target_pairs={{0,4},{4,0},{8,12},{12,8},{16,20},{20,16},{24,28},{28,24},{1,5},{5... | collective-permute-start | bytes 1572872 | tf_op jit(solution)/shard_map/ppermute | solution.py:65
  64.7 24.8 %collective-permute-start.26 = (bf16[256,1024]{1,0:T(8,128)(2,1)S(1)}, bf16[256,1024]{1,0:T(8,128)(2,1)S(1)}, u32[]{:S(2)}, u32[]{:S(2)}) collective-permute-start(bf16[256,1024]{1,0:T(8,128)(2,1)S(1)} %get-tuple-element.81.refs_6_), channel_id=1, source_target_pairs={{0,4},{4,0},{8,12},{12,8},{16,20},{20,16},{24,28},{28,24},{1,5},{5... | collective-permute-start | bytes 1572872 | tf_op jit(solution)/shard_map/ppermute | solution.py:65
  66.0 5.4 %collective-permute-start.19 = (bf16[64,1024]{1,0:T(8,128)(2,1)S(1)}, bf16[64,1024]{1,0:T(8,128)(2,1)S(1)}, u32[]{:S(2)}, u32[]{:S(2)}) collective-permute-start(bf16[64,1024]{1,0:T(8,128)(2,1)S(1)} %shard_map.141.refs_0_), channel_id=1, source_target_pairs={{0,2},{1,3},{2,0},{3,1},{4,6},{5,7},{6,4},{7,5},{8,10},{9,11},{10,... | collective-permute-start | bytes 393224 | tf_op jit(solution)/shard_map/ppermute | solution.py:410
  72.5 1.4 %collective-permute-start.20 = (bf16[64,1024]{1,0:T(8,128)(2,1)S(1)}, bf16[64,1024]{1,0:T(8,128)(2,1)S(1)}, u32[]{:S(2)}, u32[]{:S(2)}) collective-permute-start(bf16[64,1024]{1,0:T(8,128)(2,1)S(1)} %get-tuple-element.75.part), channel_id=1, source_target_pairs={{0,1},{1,0},{2,3},{3,2},{4,5},{5,4},{6,7},{7,6},{8,9},{9,8},{10,11... | collective-permute-start | bytes 393224 | tf_op jit(solution)/shard_map/ppermute | solution.py:410
  73.9 5.6 %collective-permute-start.21 = (bf16[64,1024]{1,0:T(8,128)(2,1)S(1)}, bf16[64,1024]{1,0:T(8,128)(2,1)S(1)}, u32[]{:S(2)}, u32[]{:S(2)}) collective-permute-start(bf16[64,1024]{1,0:T(8,128)(2,1)S(1)} %shard_map.143.refs_0_), channel_id=1, source_target_pairs={{0,2},{1,3},{2,0},{3,1},{4,6},{5,7},{6,4},{7,5},{8,10},{9,11},{10,... | collective-permute-start | bytes 393224 | tf_op jit(solution)/shard_map/ppermute | solution.py:410
  79.9 9.6 %collective-permute-start.24 = (bf16[64,512]{1,0:T(8,128)(2,1)S(1)}, bf16[64,512]{1,0:T(8,128)(2,1)S(1)}, u32[]{:S(2)}, u32[]{:S(2)}) collective-permute-start(bf16[64,512]{1,0:T(8,128)(2,1)S(1)} %get-tuple-element.77.refs_0_), channel_id=1, source_target_pairs={{0,24},{4,28},{8,0},{12,4},{16,8},{20,12},{24,16},{28,20},{1,25},{... | collective-permute-start | bytes 196616 | tf_op jit(solution)/shard_map/ppermute | solution.py:43
  81.2 8.3 %collective-permute-start.23 = (bf16[64,512]{1,0:T(8,128)(2,1)S(1)}, bf16[64,512]{1,0:T(8,128)(2,1)S(1)}, u32[]{:S(2)}, u32[]{:S(2)}) collective-permute-start(bf16[64,512]{1,0:T(8,128)(2,1)S(1)} %get-tuple-element.77.refs_0_), channel_id=1, source_target_pairs={{0,16},{4,20},{8,24},{12,28},{16,0},{20,4},{24,8},{28,12},{1,17},{... | collective-permute-start | bytes 196616 | tf_op jit(solution)/shard_map/ppermute | solution.py:43
  81.2 8.3 %collective-permute-start.22 = (bf16[64,512]{1,0:T(8,128)(2,1)S(1)}, bf16[64,512]{1,0:T(8,128)(2,1)S(1)}, u32[]{:S(2)}, u32[]{:S(2)}) collective-permute-start(bf16[64,512]{1,0:T(8,128)(2,1)S(1)} %get-tuple-element.77.refs_0_), channel_id=1, source_target_pairs={{0,8},{4,12},{8,16},{12,20},{16,24},{20,28},{24,0},{28,4},{1,9},{5... | collective-permute-start | bytes 196616 | tf_op jit(solution)/shard_map/ppermute | solution.py:43
  92.7 4.0 %collective-permute-start.27 = (bf16[80,256]{1,0:T(8,128)(2,1)S(1)}, bf16[80,256]{1,0:T(8,128)(2,1)S(1)}, u32[]{:S(2)}, u32[]{:S(2)}) collective-permute-start(bf16[80,256]{1,0:T(8,128)(2,1)S(1)} %get-tuple-element.83), channel_id=1, source_target_pairs={{0,24},{4,28},{8,0},{12,4},{16,8},{20,12},{24,16},{28,20},{1,25},{... | collective-permute-start | bytes 122888 | tf_op jit(solution)/shard_map/ppermute | solution.py:43
  94.0 5.3 %collective-permute-start.28 = (bf16[80,256]{1,0:T(8,128)(2,1)S(1)}, bf16[80,256]{1,0:T(8,128)(2,1)S(1)}, u32[]{:S(2)}, u32[]{:S(2)}) collective-permute-start(bf16[80,256]{1,0:T(8,128)(2,1)S(1)} %get-tuple-element.84), channel_id=1, source_target_pairs={{0,16},{4,20},{8,24},{12,28},{16,0},{20,4},{24,8},{28,12},{1,17},{... | collective-permute-start | bytes 122888 | tf_op jit(solution)/shard_map/ppermute | solution.py:43
  94.0 5.8 %collective-permute-start.29 = (bf16[80,256]{1,0:T(8,128)(2,1)S(1)}, bf16[80,256]{1,0:T(8,128)(2,1)S(1)}, u32[]{:S(2)}, u32[]{:S(2)}) collective-permute-start(bf16[80,256]{1,0:T(8,128)(2,1)S(1)} %get-tuple-element.85), channel_id=1, source_target_pairs={{0,8},{4,12},{8,16},{12,20},{16,24},{20,28},{24,0},{28,4},{1,9},{5... | collective-permute-start | bytes 122888 | tf_op jit(solution)/shard_map/ppermute | solution.py:43
  100.4 1.4 %collective-permute-start.30 = (bf16[64,1024]{1,0:T(8,128)(2,1)S(1)}, bf16[64,1024]{1,0:T(8,128)(2,1)S(1)}, u32[]{:S(2)}, u32[]{:S(2)}) collective-permute-start(bf16[64,1024]{1,0:T(8,128)(2,1)S(1)} %shard_map.147.part), channel_id=1, source_target_pairs={{0,1},{1,0},{2,3},{3,2},{4,5},{5,4},{6,7},{7,6},{8,9},{9,8},{10,11... | collective-permute-start | bytes 393224 | tf_op jit(solution)/shard_map/ppermute | solution.py:410
  101.9 5.6 %collective-permute-start.31 = (bf16[64,1024]{1,0:T(8,128)(2,1)S(1)}, bf16[64,1024]{1,0:T(8,128)(2,1)S(1)}, u32[]{:S(2)}, u32[]{:S(2)}) collective-permute-start(bf16[64,1024]{1,0:T(8,128)(2,1)S(1)} %shard_map.148.refs_0_), channel_id=1, source_target_pairs={{0,2},{1,3},{2,0},{3,1},{4,6},{5,7},{6,4},{7,5},{8,10},{9,11},{10,... | collective-permute-start | bytes 393224 | tf_op jit(solution)/shard_map/ppermute | solution.py:410
  108.0 4.7 %collective-permute-start.34 = (bf16[64,512]{1,0:T(8,128)(2,1)S(1)}, bf16[64,512]{1,0:T(8,128)(2,1)S(1)}, u32[]{:S(2)}, u32[]{:S(2)}) collective-permute-start(bf16[64,512]{1,0:T(8,128)(2,1)S(1)} %get-tuple-element.88.refs_0_), channel_id=1, source_target_pairs={{0,24},{4,28},{8,0},{12,4},{16,8},{20,12},{24,16},{28,20},{1,25},{... | collective-permute-start | bytes 196616 | tf_op jit(solution)/shard_map/ppermute | solution.py:43
  109.4 6.8 %collective-permute-start.33 = (bf16[64,512]{1,0:T(8,128)(2,1)S(1)}, bf16[64,512]{1,0:T(8,128)(2,1)S(1)}, u32[]{:S(2)}, u32[]{:S(2)}) collective-permute-start(bf16[64,512]{1,0:T(8,128)(2,1)S(1)} %get-tuple-element.88.refs_0_), channel_id=1, source_target_pairs={{0,16},{4,20},{8,24},{12,28},{16,0},{20,4},{24,8},{28,12},{1,17},{... | collective-permute-start | bytes 196616 | tf_op jit(solution)/shard_map/ppermute | solution.py:43
  109.6 7.4 %collective-permute-start.32 = (bf16[64,512]{1,0:T(8,128)(2,1)S(1)}, bf16[64,512]{1,0:T(8,128)(2,1)S(1)}, u32[]{:S(2)}, u32[]{:S(2)}) collective-permute-start(bf16[64,512]{1,0:T(8,128)(2,1)S(1)} %get-tuple-element.88.refs_0_), channel_id=1, source_target_pairs={{0,8},{4,12},{8,16},{12,20},{16,24},{20,28},{24,0},{28,4},{1,9},{5... | collective-permute-start | bytes 196616 | tf_op jit(solution)/shard_map/ppermute | solution.py:43
  111.2 7.1 %collective-permute-start.35 = (bf16[64,512]{1,0:T(8,128)(2,1)S(1)}, bf16[64,512]{1,0:T(8,128)(2,1)S(1)}, u32[]{:S(2)}, u32[]{:S(2)}) collective-permute-start(bf16[64,512]{1,0:T(8,128)(2,1)S(1)} %get-tuple-element.88.refs_0_), channel_id=1, source_target_pairs={{0,4},{4,0},{8,12},{12,8},{16,20},{20,16},{24,28},{28,24},{1,5},{5... | collective-permute-start | bytes 196616 | tf_op jit(solution)/shard_map/ppermute | solution.py:65
  112.7 5.6 %collective-permute-start.38 = (bf16[64,512]{1,0:T(8,128)(2,1)S(1)}, bf16[64,512]{1,0:T(8,128)(2,1)S(1)}, u32[]{:S(2)}, u32[]{:S(2)}) collective-permute-start(bf16[64,512]{1,0:T(8,128)(2,1)S(1)} %collective-permute-done.34.refs_3_), channel_id=1, source_target_pairs={{0,4},{4,0},{8,12},{12,8},{16,20},{20,16},{24,28},{28,24},{1,5},{5... | collective-permute-start | bytes 196616 | tf_op jit(solution)/shard_map/ppermute | solution.py:65
  116.3 4.3 %collective-permute-start.37 = (bf16[64,512]{1,0:T(8,128)(2,1)S(1)}, bf16[64,512]{1,0:T(8,128)(2,1)S(1)}, u32[]{:S(2)}, u32[]{:S(2)}) collective-permute-start(bf16[64,512]{1,0:T(8,128)(2,1)S(1)} %collective-permute-done.33.refs_2_), channel_id=1, source_target_pairs={{0,4},{4,0},{8,12},{12,8},{16,20},{20,16},{24,28},{28,24},{1,5},{5... | collective-permute-start | bytes 196616 | tf_op jit(solution)/shard_map/ppermute | solution.py:65
  117.0 4.3 %collective-permute-start.36 = (bf16[64,512]{1,0:T(8,128)(2,1)S(1)}, bf16[64,512]{1,0:T(8,128)(2,1)S(1)}, u32[]{:S(2)}, u32[]{:S(2)}) collective-permute-start(bf16[64,512]{1,0:T(8,128)(2,1)S(1)} %collective-permute-done.32.refs_1_), channel_id=1, source_target_pairs={{0,4},{4,0},{8,12},{12,8},{16,20},{20,16},{24,28},{28,24},{1,5},{5... | collective-permute-start | bytes 196616 | tf_op jit(solution)/shard_map/ppermute | solution.py:65
  122.3 1.4 %collective-permute-start.39 = (bf16[64,1024]{1,0:T(8,128)(2,1)S(1)}, bf16[64,1024]{1,0:T(8,128)(2,1)S(1)}, u32[]{:S(2)}, u32[]{:S(2)}) collective-permute-start(bf16[64,1024]{1,0:T(8,128)(2,1)S(1)} %shard_map.150.part), channel_id=1, source_target_pairs={{0,1},{1,0},{2,3},{3,2},{4,5},{5,4},{6,7},{7,6},{8,9},{9,8},{10,11... | collective-permute-start | bytes 393224 | tf_op jit(solution)/shard_map/ppermute | solution.py:410
  123.7 5.6 %collective-permute-start.40 = (bf16[64,1024]{1,0:T(8,128)(2,1)S(1)}, bf16[64,1024]{1,0:T(8,128)(2,1)S(1)}, u32[]{:S(2)}, u32[]{:S(2)}) collective-permute-start(bf16[64,1024]{1,0:T(8,128)(2,1)S(1)} %shard_map.151.refs_0_), channel_id=1, source_target_pairs={{0,2},{1,3},{2,0},{3,1},{4,6},{5,7},{6,4},{7,5},{8,10},{9,11},{10,... | collective-permute-start | bytes 393224 | tf_op jit(solution)/shard_map/ppermute | solution.py:410
  130.4 1.5 %collective-permute-start.41 = (bf16[64,1024]{1,0:T(8,128)(2,1)S(1)}, bf16[64,1024]{1,0:T(8,128)(2,1)S(1)}, u32[]{:S(2)}, u32[]{:S(2)}) collective-permute-start(bf16[64,1024]{1,0:T(8,128)(2,1)S(1)} %get-tuple-element.90.part), channel_id=1, source_target_pairs={{0,1},{1,0},{2,3},{3,2},{4,5},{5,4},{6,7},{7,6},{8,9},{9,8},{10,11... | collective-permute-start | bytes 393224 | tf_op jit(solution)/shard_map/ppermute | solution.py:410
  130.5 5.9 %collective-permute-start.43 = (bf16[256,256]{1,0:T(8,128)(2,1)S(1)}, bf16[256,256]{1,0:T(8,128)(2,1)S(1)}, u32[]{:S(2)}, u32[]{:S(2)}) collective-permute-start(bf16[256,256]{1,0:T(8,128)(2,1)S(1)} %get-tuple-element.91.refs_2_), channel_id=1, source_target_pairs={{0,4},{4,0},{8,12},{12,8},{16,20},{20,16},{24,28},{28,24},{1,5},{5... | collective-permute-start | bytes 393224 | tf_op jit(solution)/shard_map/ppermute | solution.py:65
  131.9 5.6 %collective-permute-start.42 = (bf16[64,1024]{1,0:T(8,128)(2,1)S(1)}, bf16[64,1024]{1,0:T(8,128)(2,1)S(1)}, u32[]{:S(2)}, u32[]{:S(2)}) collective-permute-start(bf16[64,1024]{1,0:T(8,128)(2,1)S(1)} %shard_map.153.refs_0_), channel_id=1, source_target_pairs={{0,2},{1,3},{2,0},{3,1},{4,6},{5,7},{6,4},{7,5},{8,10},{9,11},{10,... | collective-permute-start | bytes 393224 | tf_op jit(solution)/shard_map/ppermute | solution.py:410
  (11 other events, 166.4 us)

commit v3 on v2

--- a/solution.py
+++ b/solution.py
@@ -10,7 +10,8 @@
 HEAD_DIM = 64
 STATS = 4
 VMEM_BYTES = 10 << 20
-LOAD_BYTES = 54 << 20
+LOAD_BYTES = 53 << 20
+CHUNK_BYTES = 50 << 20
 CHUNKS = 2
 WIDEST = 8
 epsilon = 1e-05
@@ -113,13 +114,23 @@
 
 
 def chunk_kernel(chunk, count, first_half, carried, last, *refs):
-    queries, key_w, value_w = refs[:3]
-    blocks, owners, refs = refs[3 : 3 + count], refs[3 + count : 3 + 2 * count], refs[3 + 2 * count :]
-    carry, outs = (refs[:2], refs[2:]) if carried else (None, refs)
+    frames_hbm, key_hbm, value_hbm, queries = refs[:4]
+    blocks, owners, refs = refs[4 : 3 + count], refs[3 + count : 3 + 2 * count], refs[3 + 2 * count :]
+    carry, refs = (refs[:2], refs[2:]) if carried else (None, refs)
+    outs, (own, key_w, value_w, sems) = refs[:-4], refs[-4:]
     out, keys, values = outs[:3]
-    rows, width = out.shape[0], blocks[0].shape[1]
+    rows, width = own.shape
     served = queries.at[pl.ds(first_half, queries.shape[0] - first_half), :]
-    tile = min(rows, 32)
+    loads = [
+        pltpu.make_async_copy(frames_hbm.at[pl.ds(chunk * rows, rows), :], own, sems.at[0]),
+        pltpu.make_async_copy(key_hbm.at[0], key_w, sems.at[1]),
+        pltpu.make_async_copy(value_hbm.at[0], value_w, sems.at[2]),
+    ]
+    for load in loads:
+        load.start()
+    loads[0].wait()
+    blocks = [own] + list(blocks)
+    tile = min(rows, 128)
     for start in range(0, rows, tile):
         pieces = []
         for block in blocks:
@@ -132,6 +143,8 @@
         for piece, owner in zip(pieces, owners):
             lanes = pl.ds(pl.multiple_of(owner[0, 0] * width, width), width)
             out[start : start + tile, lanes] = (piece * scale).astype(bf16)
+    for load in loads[1:]:
+        load.wait()
     keys[...] = product(out[...], key_w[...]).astype(bf16)
     values[...] = product(out[...], value_w[...]).astype(bf16).T
     for found in weighed(served, [keys], [values], carry, 0):
@@ -158,15 +171,9 @@
         start = end
 
 
-def latents_kernel(scale, count, frames_hbm, key_hbm, value_hbm, latents_hbm, query_hbm, me, *refs):
-    state, queries, own, key_w, value_w, latents, query_w, rows_normed, sems = refs
-    moves = [
-        (latents_hbm, latents),
-        (query_hbm.at[0], query_w),
-        (frames_hbm, own),
-        (key_hbm.at[0], key_w),
-        (value_hbm.at[0], value_w),
-    ]
+def latents_kernel(scale, count, latents_hbm, query_hbm, me, *refs):
+    state, queries, latents, query_w, rows_normed, sems = refs
+    moves = [(latents_hbm, latents), (query_hbm.at[0], query_w)]
     loads = [pltpu.make_async_copy(*move, sems.at[i]) for i, move in enumerate(moves)]
     for load in loads:
         load.start()
@@ -181,8 +188,6 @@
     state[...] = latents[pl.ds(pl.multiple_of(me[0, 0] * rows, rows), rows), :].astype(f32)
     loads[1].wait()
     queries[...] = (product(rows_normed[...], query_w[...]) * scale).astype(bf16)
-    for load in loads[2:]:
-        load.wait()
 
 
 def split_terms(value):
@@ -438,22 +443,19 @@
     row_shape = shaped((rows, columns), bf16)
     double_shape = shaped((rows, 2 * columns), bf16)
     packed_shape = shaped((rows + stat_rows, columns), bf16)
-    state, queries, own, key_w, value_w = whole_call(
+    state, queries = whole_call(
         functools.partial(latents_kernel, scale, shards),
         (
             state_shape,
             shaped((latent_count, columns), bf16),
-            shaped(frames.shape, bf16),
-            shaped((width, columns), bf16),
-            shaped((width, columns), bf16),
         ),
-        unplaced=(frames, cross_key, cross_value, latents, cross_query),
+        unplaced=(latents, cross_query),
         scalars=(me,),
         scratch=[
             pltpu.VMEM((latent_count, width), bf16),
             pltpu.VMEM((width, columns), bf16),
             pltpu.VMEM((latent_count, width), bf16),
-            pltpu.SemaphoreType.DMA((5,)),
+            pltpu.SemaphoreType.DMA((2,)),
         ],
         limit=LOAD_BYTES,
         cost=pl.CostEstimate(
@@ -498,13 +500,18 @@
             functools.partial(chunk_kernel, c, count, line_latents, c > 0, last),
             results + ([line_shape] if last else carry_shapes),
             queries,
-            key_w,
-            value_w,
-            own,
             near,
             *blocks,
+            unplaced=(frames, cross_key, cross_value),
             scalars=owners,
             after=carry,
+            limit=CHUNK_BYTES,
+            scratch=[
+                pltpu.VMEM((part_rows, frames.shape[1]), bf16),
+                pltpu.VMEM((width, columns), bf16),
+                pltpu.VMEM((width, columns), bf16),
+                pltpu.SemaphoreType.DMA((3,)),
+            ],
             cost=pl.CostEstimate(
                 flops=4 * part_rows * width * columns,
                 bytes_accessed=2 * part_rows * width,

time: 139 us -> 139 us (level)
  waiting for transfers between devices: 65 us -> 68.8 us
  local copies, waits for them, and re-layouts: 5.2 us -> 2.16 us
    ppermute x2, waiting for transfers between devices: 3.1 us -> 6.94 us  [shifted(): lax.ppermute(value, axis, [(i, (i + step) % count) for i in range(count)])]
    unnamed x30 -> x22, local copies, waits for them, and re-layouts: 4.14 us -> 1.09 us
  transfers between devices with their start and end apart: 44 -> 44, of which waited for: 30 -> 30; matrix products, arithmetic and copies ran while one was open for 0% -> 0% of each run, Pallas kernels for 8% -> 7%
where the time goes in v3:
time: 139 us
  waiting for transfers between devices  68.8 us (49%)
  starting transfers between devices  43.9 us (32%)
  Pallas kernels  23.4 us (17%)
  local copies, waits for them, and re-layouts  2.16 us (2%)
    ppermute x12, waiting for transfers between devices, from_bits(): return lax.ppermute(value, 'heads', [(i, i ^ bits) for i in range(count)])  26.4 us
    pallas_call x24, Pallas kernels, whole_call(): pl.pallas_call(body, out_shape=results, in_specs=specs, out_specs=jax.tre...  23.4 us
    ppermute x12, waiting for transfers between devices, pair_swap(): return lax.ppermute(value, 'frames', [(i, i ^ 1) for i in range(count)])  18.6 us
    ppermute x15, starting transfers between devices, line_shift(): lax.ppermute(value, 'frames', [(i, (i + 2 * step) % count) for i in range...  15.4 us
    ppermute x15, waiting for transfers between devices, line_shift(): lax.ppermute(value, 'frames', [(i, (i + 2 * step) % count) for i in range...  15.3 us
    ppermute x12, starting transfers between devices, pair_swap(): return lax.ppermute(value, 'frames', [(i, i ^ 1) for i in range(count)])  13.7 us
    ppermute x12, starting transfers between devices, from_bits(): return lax.ppermute(value, 'heads', [(i, i ^ bits) for i in range(count)])  9.99 us
    ppermute x2, waiting for transfers between devices, shifted(): lax.ppermute(value, axis, [(i, (i + step) % count) for i in range(count)])  6.94 us
  transfers between devices with their start and end apart: 44, of which 30 were waited for; matrix products, arithmetic and copies ran while one was open for 0% of the time, Pallas kernels for 7%

profile of v3, /device:TPU:0, one launch (start us, length us, event | category | flops | bytes accessed | tf_op | source)
XLA Modules:
  0.0 139.2 jit_solution(1926442125871824386)
XLA Ops:
  1.7 3.1 %collective-permute-start = (bf16[512,256]{1,0:T(8,128)(2,1)S(1)}, bf16[512,256]{1,0:T(8,128)(2,1)S(1)}, u32[]{:S(2)}, u32[]{:S(2)}) collective-permute-start(bf16[512,256]{1,0:T(8,128)(2,1)S(1)} %get-tuple-element.87), channel_id=1, source_target_pairs={{0,2},{1,3},{2,0},{3,1},{4,6},{5,7},{6,4},{7,5},{8,10},{9,11},{10,... | collective-permute-start | bytes 786440 | tf_op jit(solution)/shard_map/ppermute | solution.py:23
  4.8 2.3 %shard_map.131 = (f32[64,1024]{1,0:T(8,128)S(1)}, bf16[512,256]{1,0:T(8,128)(2,1)S(1)}) custom-call(bf16[512,1024]{1,0:T(8,128)(2,1)} %latents_hbm.1, bf16[2,1024,256]{2,1,0:T(8,128)(2,1)} %refs_2_.12, s32[1,1]{1,0:T(1,128)} %bitcast.me.refs_4_), custom_call_target="tpu_custom_call" | custom-call | flops 268435456 | bytes 1048576 | tf_op jit(solution)/shard_map/pallas_call | solution.py:81
  7.0 4.0 %collective-permute-done.refs_5_ = bf16[512,256]{1,0:T(8,128)(2,1)S(1)} collective-permute-done((bf16[512,256]{1,0:T(8,128)(2,1)S(1)}, bf16[512,256]{1,0:T(8,128)(2,1)S(1)}, u32[]{:S(2)}, u32[]{:S(2)}) %collective-permute-start) | collective-permute-done | bytes 262176 | tf_op jit(solution)/shard_map/ppermute | solution.py:23
  11.1 1.7 %collective-permute-start.2 = (bf16[512,256]{1,0:T(8,128)(2,1)S(1)}, bf16[512,256]{1,0:T(8,128)(2,1)S(1)}, u32[]{:S(2)}, u32[]{:S(2)}) collective-permute-start(bf16[512,256]{1,0:T(8,128)(2,1)S(1)} %get-tuple-element.86), channel_id=1, source_target_pairs={{0,2},{1,3},{2,0},{3,1},{4,6},{5,7},{6,4},{7,5},{8,10},{9,11},{10,... | collective-permute-start | bytes 786440 | tf_op jit(solution)/shard_map/ppermute | solution.py:23
  13.9 3.0 %shard_map.132 = (bf16[512,1024]{1,0:T(8,128)(2,1)S(1)}, bf16[512,256]{1,0:T(8,128)(2,1)S(1)}, bf16[256,512]{1,0:T(8,128)(2,1)S(1)}, f32[256,256]{1,0:T(8,128)S(1)}, f32[8,256]{1,0:T(8,128)S(1)}) custom-call(bf16[1024,256]{1,0:T(8,128)(2,1)S(1)} %copy-done.4, bf16[2,1024,256]{2,1,0:T(8,128)(2,1)} %refs_2_.13, bf16[2,1024,256]{2,1,0:T(8,128)(2,1)} %refs_3_.7, ...), custom_call_target="tpu_custom_call" | custom-call | flops 536870912 | bytes 1048576 | tf_op jit(solution)/shard_map/pallas_call | solution.py:81
  16.9 2.9 %collective-permute-done.2.refs_5_ = bf16[512,256]{1,0:T(8,128)(2,1)S(1)} collective-permute-done((bf16[512,256]{1,0:T(8,128)(2,1)S(1)}, bf16[512,256]{1,0:T(8,128)(2,1)S(1)}, u32[]{:S(2)}, u32[]{:S(2)}) %collective-permute-start.2) | collective-permute-done | bytes 262176 | tf_op jit(solution)/shard_map/ppermute | solution.py:23
  19.8 1.5 %collective-permute-done.4.refs_6_ = bf16[512,256]{1,0:T(8,128)(2,1)S(1)} collective-permute-done((bf16[512,256]{1,0:T(8,128)(2,1)S(1)}, bf16[512,256]{1,0:T(8,128)(2,1)S(1)}, u32[]{:S(2)}, u32[]{:S(2)}) %collective-permute-start.4) | collective-permute-done | bytes 262176 | tf_op jit(solution)/shard_map/ppermute | solution.py:73
  21.3 3.2 %shard_map.133 = (bf16[512,1024]{1,0:T(8,128)(2,1)S(1)}, bf16[512,256]{1,0:T(8,128)(2,1)S(1)}, bf16[256,512]{1,0:T(8,128)(2,1)S(1)}, bf16[272,256]{1,0:T(8,128)(2,1)S(1)}) custom-call(bf16[1024,256]{1,0:T(8,128)(2,1)S(1)} %copy-done.4, bf16[2,1024,256]{2,1,0:T(8,128)(2,1)} %refs_2_.13, bf16[2,1024,256]{2,1,0:T(8,128)(2,1)} %refs_3_.7, ...), custom_call_target="tpu_custom_call" | custom-call | flops 536870912 | bytes 1048576 | tf_op jit(solution)/shard_map/pallas_call | solution.py:81
  24.5 1.8 %collective-permute-start.5 = (bf16[272,256]{1,0:T(8,128)(2,1)S(1)}, bf16[272,256]{1,0:T(8,128)(2,1)S(1)}, u32[]{:S(2)}, u32[]{:S(2)}) collective-permute-start(bf16[272,256]{1,0:T(8,128)(2,1)S(1)} %get-tuple-element.60), channel_id=1, source_target_pairs={{0,4},{4,0},{8,12},{12,8},{16,20},{20,16},{24,28},{28,24},{1,5},{5... | collective-permute-start | bytes 417800 | tf_op jit(solution)/shard_map/ppermute | solution.py:66
  28.7 1.6 %collective-permute-done.5.other = bf16[272,256]{1,0:T(8,128)(2,1)S(1)} collective-permute-done((bf16[272,256]{1,0:T(8,128)(2,1)S(1)}, bf16[272,256]{1,0:T(8,128)(2,1)S(1)}, u32[]{:S(2)}, u32[]{:S(2)}) %collective-permute-start.5) | collective-permute-done | bytes 139296 | tf_op jit(solution)/shard_map/ppermute | solution.py:66
  30.4 3.9 %collective-permute-start.6 = (bf16[80,256]{1,0:T(8,128)(2,1)S(1)}, bf16[80,256]{1,0:T(8,128)(2,1)S(1)}, u32[]{:S(2)}, u32[]{:S(2)}) collective-permute-start(bf16[80,256]{1,0:T(8,128)(2,1)S(1)} %get-tuple-element.62), channel_id=1, source_target_pairs={{0,24},{4,28},{8,0},{12,4},{16,8},{20,12},{24,16},{28,20},{1,25},{... | collective-permute-start | bytes 122888 | tf_op jit(solution)/shard_map/ppermute | solution.py:44
  36.0 3.2 %collective-permute-done.7.refs_2_ = bf16[80,256]{1,0:T(8,128)(2,1)S(1)} collective-permute-done((bf16[80,256]{1,0:T(8,128)(2,1)S(1)}, bf16[80,256]{1,0:T(8,128)(2,1)S(1)}, u32[]{:S(2)}, u32[]{:S(2)}) %collective-permute-start.7) | collective-permute-done | bytes 40992 | tf_op jit(solution)/shard_map/ppermute | solution.py:44
  40.8 1.3 collective-permute-done.9.other
  42.2 1.6 %collective-permute-start.10 = (bf16[64,1024]{1,0:T(8,128)(2,1)S(1)}, bf16[64,1024]{1,0:T(8,128)(2,1)S(1)}, u32[]{:S(2)}, u32[]{:S(2)}) collective-permute-start(bf16[64,1024]{1,0:T(8,128)(2,1)S(1)} %shard_map.138.refs_0_), channel_id=1, source_target_pairs={{0,2},{1,3},{2,0},{3,1},{4,6},{5,7},{6,4},{7,5},{8,10},{9,11},{10,... | collective-permute-start | bytes 393224 | tf_op jit(solution)/shard_map/ppermute | solution.py:415
  43.7 4.0 %collective-permute-done.10.refs_1_ = bf16[64,1024]{1,0:T(8,128)(2,1)S(1)} collective-permute-done((bf16[64,1024]{1,0:T(8,128)(2,1)S(1)}, bf16[64,1024]{1,0:T(8,128)(2,1)S(1)}, u32[]{:S(2)}, u32[]{:S(2)}) %collective-permute-start.10) | collective-permute-done | bytes 131104 | tf_op jit(solution)/shard_map/ppermute | solution.py:415
  49.6 1.9 %collective-permute-start.11 = (bf16[64,512]{1,0:T(8,128)(2,1)S(1)}, bf16[64,512]{1,0:T(8,128)(2,1)S(1)}, u32[]{:S(2)}, u32[]{:S(2)}) collective-permute-start(bf16[64,512]{1,0:T(8,128)(2,1)S(1)} %get-tuple-element.67.refs_0_), channel_id=1, source_target_pairs={{0,8},{4,12},{8,16},{12,20},{16,24},{20,28},{24,0},{28,4},{1,9},{5... | collective-permute-start | bytes 196616 | tf_op jit(solution)/shard_map/ppermute | solution.py:44
  51.6 1.5 %collective-permute-start.14 = (bf16[64,512]{1,0:T(8,128)(2,1)S(1)}, bf16[64,512]{1,0:T(8,128)(2,1)S(1)}, u32[]{:S(2)}, u32[]{:S(2)}) collective-permute-start(bf16[64,512]{1,0:T(8,128)(2,1)S(1)} %get-tuple-element.67.refs_0_), channel_id=1, source_target_pairs={{0,4},{4,0},{8,12},{12,8},{16,20},{20,16},{24,28},{28,24},{1,5},{5... | collective-permute-start | bytes 196616 | tf_op jit(solution)/shard_map/ppermute | solution.py:66
  53.2 1.5 %collective-permute-start.17 = (bf16[64,512]{1,0:T(8,128)(2,1)S(1)}, bf16[64,512]{1,0:T(8,128)(2,1)S(1)}, u32[]{:S(2)}, u32[]{:S(2)}) collective-permute-start(bf16[64,512]{1,0:T(8,128)(2,1)S(1)} %collective-permute-done.13.refs_3_), channel_id=1, source_target_pairs={{0,4},{4,0},{8,12},{12,8},{16,20},{20,16},{24,28},{28,24},{1,5},{5... | collective-permute-start | bytes 196616 | tf_op jit(solution)/shard_map/ppermute | solution.py:66
  54.7 1.7 %collective-permute-done.12.refs_2_ = bf16[64,512]{1,0:T(8,128)(2,1)S(1)} collective-permute-done((bf16[64,512]{1,0:T(8,128)(2,1)S(1)}, bf16[64,512]{1,0:T(8,128)(2,1)S(1)}, u32[]{:S(2)}, u32[]{:S(2)}) %collective-permute-start.12) | collective-permute-done | bytes 65568 | tf_op jit(solution)/shard_map/ppermute | solution.py:44
  56.4 1.5 %collective-permute-start.16 = (bf16[64,512]{1,0:T(8,128)(2,1)S(1)}, bf16[64,512]{1,0:T(8,128)(2,1)S(1)}, u32[]{:S(2)}, u32[]{:S(2)}) collective-permute-start(bf16[64,512]{1,0:T(8,128)(2,1)S(1)} %collective-permute-done.12.refs_2_), channel_id=1, source_target_pairs={{0,4},{4,0},{8,12},{12,8},{16,20},{20,16},{24,28},{28,24},{1,5},{5... | collective-permute-start | bytes 196616 | tf_op jit(solution)/shard_map/ppermute | solution.py:66
  58.4 2.2 %collective-permute-done.16.refs_6_ = bf16[64,512]{1,0:T(8,128)(2,1)S(1)} collective-permute-done((bf16[64,512]{1,0:T(8,128)(2,1)S(1)}, bf16[64,512]{1,0:T(8,128)(2,1)S(1)}, u32[]{:S(2)}, u32[]{:S(2)}) %collective-permute-start.16) | collective-permute-done | bytes 65568 | tf_op jit(solution)/shard_map/ppermute | solution.py:66
  60.7 1.5 %collective-permute-done.15.refs_5_ = bf16[64,512]{1,0:T(8,128)(2,1)S(1)} collective-permute-done((bf16[64,512]{1,0:T(8,128)(2,1)S(1)}, bf16[64,512]{1,0:T(8,128)(2,1)S(1)}, u32[]{:S(2)}, u32[]{:S(2)}) %collective-permute-start.15) | collective-permute-done | bytes 65568 | tf_op jit(solution)/shard_map/ppermute | solution.py:66
  63.3 1.3 shard_map.145
  65.4 1.3 collective-permute-start.26
  66.8 1.6 %collective-permute-start.19 = (bf16[64,1024]{1,0:T(8,128)(2,1)S(1)}, bf16[64,1024]{1,0:T(8,128)(2,1)S(1)}, u32[]{:S(2)}, u32[]{:S(2)}) collective-permute-start(bf16[64,1024]{1,0:T(8,128)(2,1)S(1)} %shard_map.141.refs_0_), channel_id=1, source_target_pairs={{0,2},{1,3},{2,0},{3,1},{4,6},{5,7},{6,4},{7,5},{8,10},{9,11},{10,... | collective-permute-start | bytes 393224 | tf_op jit(solution)/shard_map/ppermute | solution.py:415
  68.4 3.8 %collective-permute-done.19.refs_1_ = bf16[64,1024]{1,0:T(8,128)(2,1)S(1)} collective-permute-done((bf16[64,1024]{1,0:T(8,128)(2,1)S(1)}, bf16[64,1024]{1,0:T(8,128)(2,1)S(1)}, u32[]{:S(2)}, u32[]{:S(2)}) %collective-permute-start.19) | collective-permute-done | bytes 131104 | tf_op jit(solution)/shard_map/ppermute | solution.py:415
  73.3 1.3 collective-permute-done.20.other
  74.6 1.6 %collective-permute-start.21 = (bf16[64,1024]{1,0:T(8,128)(2,1)S(1)}, bf16[64,1024]{1,0:T(8,128)(2,1)S(1)}, u32[]{:S(2)}, u32[]{:S(2)}) collective-permute-start(bf16[64,1024]{1,0:T(8,128)(2,1)S(1)} %shard_map.143.refs_0_), channel_id=1, source_target_pairs={{0,2},{1,3},{2,0},{3,1},{4,6},{5,7},{6,4},{7,5},{8,10},{9,11},{10,... | collective-permute-start | bytes 393224 | tf_op jit(solution)/shard_map/ppermute | solution.py:415
  76.2 4.0 %collective-permute-done.21.refs_1_ = bf16[64,1024]{1,0:T(8,128)(2,1)S(1)} collective-permute-done((bf16[64,1024]{1,0:T(8,128)(2,1)S(1)}, bf16[64,1024]{1,0:T(8,128)(2,1)S(1)}, u32[]{:S(2)}, u32[]{:S(2)}) %collective-permute-start.21) | collective-permute-done | bytes 131104 | tf_op jit(solution)/shard_map/ppermute | solution.py:415
  80.6 1.3 collective-permute-start.24
  82.7 7.5 %collective-permute-done.26.refs_7_ = bf16[256,1024]{1,0:T(8,128)(2,1)S(1)} collective-permute-done((bf16[256,1024]{1,0:T(8,128)(2,1)S(1)}, bf16[256,1024]{1,0:T(8,128)(2,1)S(1)}, u32[]{:S(2)}, u32[]{:S(2)}) %collective-permute-start.26) | collective-permute-done | bytes 524320 | tf_op jit(solution)/shard_map/ppermute | solution.py:66
  90.2 3.2 %shard_map.146 = (bf16[80,256]{1,0:T(8,128)(2,1)S(1)}, bf16[80,256]{1,0:T(8,128)(2,1)S(1)}, bf16[80,256]{1,0:T(8,128)(2,1)S(1)}, bf16[80,256]{1,0:T(8,128)(2,1)S(1)}, bf16[256,256]{1,0:T(8,128)(2,1)S(1)}) custom-call(bf16[64,512]{1,0:T(8,128)(2,1)S(1)} %get-tuple-element.71.refs_0_, bf16[64,512]{1,0:T(8,128)(2,1)S(1)} %collective-permute-done.22.refs_1_, ...), custom_call_target="tpu_custom_call" | custom-call | tf_op jit(solution)/shard_map/pallas_call | solution.py:81
  95.5 2.0 %collective-permute-done.27.refs_1_ = bf16[80,256]{1,0:T(8,128)(2,1)S(1)} collective-permute-done((bf16[80,256]{1,0:T(8,128)(2,1)S(1)}, bf16[80,256]{1,0:T(8,128)(2,1)S(1)}, u32[]{:S(2)}, u32[]{:S(2)}) %collective-permute-start.27) | collective-permute-done | bytes 40992 | tf_op jit(solution)/shard_map/ppermute | solution.py:44
  97.5 2.6 %collective-permute-done.28.refs_2_ = bf16[80,256]{1,0:T(8,128)(2,1)S(1)} collective-permute-done((bf16[80,256]{1,0:T(8,128)(2,1)S(1)}, bf16[80,256]{1,0:T(8,128)(2,1)S(1)}, u32[]{:S(2)}, u32[]{:S(2)}) %collective-permute-start.28) | collective-permute-done | bytes 40992 | tf_op jit(solution)/shard_map/ppermute | solution.py:44
  101.2 1.3 collective-permute-done.30.other
  102.6 1.6 %collective-permute-start.31 = (bf16[64,1024]{1,0:T(8,128)(2,1)S(1)}, bf16[64,1024]{1,0:T(8,128)(2,1)S(1)}, u32[]{:S(2)}, u32[]{:S(2)}) collective-permute-start(bf16[64,1024]{1,0:T(8,128)(2,1)S(1)} %shard_map.148.refs_0_), channel_id=1, source_target_pairs={{0,2},{1,3},{2,0},{3,1},{4,6},{5,7},{6,4},{7,5},{8,10},{9,11},{10,... | collective-permute-start | bytes 393224 | tf_op jit(solution)/shard_map/ppermute | solution.py:415
  104.2 4.0 %collective-permute-done.31.refs_1_ = bf16[64,1024]{1,0:T(8,128)(2,1)S(1)} collective-permute-done((bf16[64,1024]{1,0:T(8,128)(2,1)S(1)}, bf16[64,1024]{1,0:T(8,128)(2,1)S(1)}, u32[]{:S(2)}, u32[]{:S(2)}) %collective-permute-start.31) | collective-permute-done | bytes 131104 | tf_op jit(solution)/shard_map/ppermute | solution.py:415
  108.8 1.4 %collective-permute-start.34 = (bf16[64,512]{1,0:T(8,128)(2,1)S(1)}, bf16[64,512]{1,0:T(8,128)(2,1)S(1)}, u32[]{:S(2)}, u32[]{:S(2)}) collective-permute-start(bf16[64,512]{1,0:T(8,128)(2,1)S(1)} %get-tuple-element.82.refs_0_), channel_id=1, source_target_pairs={{0,24},{4,28},{8,0},{12,4},{16,8},{20,12},{24,16},{28,20},{1,25},{... | collective-permute-start | bytes 196616 | tf_op jit(solution)/shard_map/ppermute | solution.py:44
  110.3 1.7 %collective-permute-start.32 = (bf16[64,512]{1,0:T(8,128)(2,1)S(1)}, bf16[64,512]{1,0:T(8,128)(2,1)S(1)}, u32[]{:S(2)}, u32[]{:S(2)}) collective-permute-start(bf16[64,512]{1,0:T(8,128)(2,1)S(1)} %get-tuple-element.82.refs_0_), channel_id=1, source_target_pairs={{0,8},{4,12},{8,16},{12,20},{16,24},{20,28},{24,0},{28,4},{1,9},{5... | collective-permute-start | bytes 196616 | tf_op jit(solution)/shard_map/ppermute | solution.py:44
  114.2 2.9 %collective-permute-done.33.refs_2_ = bf16[64,512]{1,0:T(8,128)(2,1)S(1)} collective-permute-done((bf16[64,512]{1,0:T(8,128)(2,1)S(1)}, bf16[64,512]{1,0:T(8,128)(2,1)S(1)}, u32[]{:S(2)}, u32[]{:S(2)}) %collective-permute-start.33) | collective-permute-done | bytes 65568 | tf_op jit(solution)/shard_map/ppermute | solution.py:44
  117.7 1.3 collective-permute-start.36
  119.0 2.2 %collective-permute-done.37.refs_6_ = bf16[64,512]{1,0:T(8,128)(2,1)S(1)} collective-permute-done((bf16[64,512]{1,0:T(8,128)(2,1)S(1)}, bf16[64,512]{1,0:T(8,128)(2,1)S(1)}, u32[]{:S(2)}, u32[]{:S(2)}) %collective-permute-start.37) | collective-permute-done | bytes 65568 | tf_op jit(solution)/shard_map/ppermute | solution.py:66
  123.1 1.3 collective-permute-done.39.other
  124.5 1.6 %collective-permute-start.40 = (bf16[64,1024]{1,0:T(8,128)(2,1)S(1)}, bf16[64,1024]{1,0:T(8,128)(2,1)S(1)}, u32[]{:S(2)}, u32[]{:S(2)}) collective-permute-start(bf16[64,1024]{1,0:T(8,128)(2,1)S(1)} %shard_map.151.refs_0_), channel_id=1, source_target_pairs={{0,2},{1,3},{2,0},{3,1},{4,6},{5,7},{6,4},{7,5},{8,10},{9,11},{10,... | collective-permute-start | bytes 393224 | tf_op jit(solution)/shard_map/ppermute | solution.py:415
  126.1 4.0 %collective-permute-done.40.refs_1_ = bf16[64,1024]{1,0:T(8,128)(2,1)S(1)} collective-permute-done((bf16[64,1024]{1,0:T(8,128)(2,1)S(1)}, bf16[64,1024]{1,0:T(8,128)(2,1)S(1)}, u32[]{:S(2)}, u32[]{:S(2)}) %collective-permute-start.40) | collective-permute-done | bytes 131104 | tf_op jit(solution)/shard_map/ppermute | solution.py:415
  131.2 1.4 %collective-permute-start.43 = (bf16[256,256]{1,0:T(8,128)(2,1)S(1)}, bf16[256,256]{1,0:T(8,128)(2,1)S(1)}, u32[]{:S(2)}, u32[]{:S(2)}) collective-permute-start(bf16[256,256]{1,0:T(8,128)(2,1)S(1)} %get-tuple-element.85.refs_2_), channel_id=1, source_target_pairs={{0,4},{4,0},{8,12},{12,8},{16,20},{20,16},{24,28},{28,24},{1,5},{5... | collective-permute-start | bytes 393224 | tf_op jit(solution)/shard_map/ppermute | solution.py:66
  132.6 1.6 %collective-permute-start.42 = (bf16[64,1024]{1,0:T(8,128)(2,1)S(1)}, bf16[64,1024]{1,0:T(8,128)(2,1)S(1)}, u32[]{:S(2)}, u32[]{:S(2)}) collective-permute-start(bf16[64,1024]{1,0:T(8,128)(2,1)S(1)} %shard_map.153.refs_0_), channel_id=1, source_target_pairs={{0,2},{1,3},{2,0},{3,1},{4,6},{5,7},{6,4},{7,5},{8,10},{9,11},{10,... | collective-permute-start | bytes 393224 | tf_op jit(solution)/shard_map/ppermute | solution.py:415
  134.2 2.9 %collective-permute-done.43.refs_3_ = bf16[256,256]{1,0:T(8,128)(2,1)S(1)} collective-permute-done((bf16[256,256]{1,0:T(8,128)(2,1)S(1)}, bf16[256,256]{1,0:T(8,128)(2,1)S(1)}, u32[]{:S(2)}, u32[]{:S(2)}) %collective-permute-start.43) | collective-permute-done | bytes 131104 | tf_op jit(solution)/shard_map/ppermute | solution.py:66
  (87 shorter events, 26.5 us)
Async XLA Ops:
  1.7 9.4 %collective-permute-start = (bf16[512,256]{1,0:T(8,128)(2,1)S(1)}, bf16[512,256]{1,0:T(8,128)(2,1)S(1)}, u32[]{:S(2)}, u32[]{:S(2)}) collective-permute-start(bf16[512,256]{1,0:T(8,128)(2,1)S(1)} %get-tuple-element.87), channel_id=1, source_target_pairs={{0,2},{1,3},{2,0},{3,1},{4,6},{5,7},{6,4},{7,5},{8,10},{9,11},{10,... | collective-permute-start | bytes 786440 | tf_op jit(solution)/shard_map/ppermute | solution.py:23
  4.8 8.1 %collective-permute-start.1 = (bf16[1024,256]{1,0:T(8,128)(2,1)}, bf16[1024,256]{1,0:T(8,128)(2,1)S(1)}, u32[]{:S(2)}, u32[]{:S(2)}) collective-permute-start(bf16[1024,256]{1,0:T(8,128)(2,1)} %refs_0_.3), channel_id=1, source_target_pairs={{0,1},{1,0},{2,3},{3,2},{4,5},{5,4},{6,7},{7,6},{8,9},{9,8},{10,11... | collective-permute-start | bytes 1572872 | tf_op jit(solution)/shard_map/ppermute | solution.py:478
  11.1 1.7 %collective-permute-start.3 = (bf16[512,256]{1,0:T(8,128)(2,1)S(1)}, bf16[512,256]{1,0:T(8,128)(2,1)S(1)}, u32[]{:S(2)}, u32[]{:S(2)}) collective-permute-start(bf16[512,256]{1,0:T(8,128)(2,1)S(1)} %collective-permute-done.refs_5_), channel_id=1, source_target_pairs={{0,1},{1,0},{2,3},{3,2},{4,5},{5,4},{6,7},{7,6},{8,9},{9,8},{10,11... | collective-permute-start | bytes 786440 | tf_op jit(solution)/shard_map/ppermute | solution.py:73
  11.1 8.7 %collective-permute-start.2 = (bf16[512,256]{1,0:T(8,128)(2,1)S(1)}, bf16[512,256]{1,0:T(8,128)(2,1)S(1)}, u32[]{:S(2)}, u32[]{:S(2)}) collective-permute-start(bf16[512,256]{1,0:T(8,128)(2,1)S(1)} %get-tuple-element.86), channel_id=1, source_target_pairs={{0,2},{1,3},{2,0},{3,1},{4,6},{5,7},{6,4},{7,5},{8,10},{9,11},{10,... | collective-permute-start | bytes 786440 | tf_op jit(solution)/shard_map/ppermute | solution.py:23
  19.8 1.5 %collective-permute-start.4 = (bf16[512,256]{1,0:T(8,128)(2,1)S(1)}, bf16[512,256]{1,0:T(8,128)(2,1)S(1)}, u32[]{:S(2)}, u32[]{:S(2)}) collective-permute-start(bf16[512,256]{1,0:T(8,128)(2,1)S(1)} %collective-permute-done.2.refs_5_), channel_id=1, source_target_pairs={{0,1},{1,0},{2,3},{3,2},{4,5},{5,4},{6,7},{7,6},{8,9},{9,8},{10,11... | collective-permute-start | bytes 786440 | tf_op jit(solution)/shard_map/ppermute | solution.py:73
  21.3 26.5 %copy-start.7 = (bf16[2,1024,256]{2,1,0:T(8,128)(2,1)S(1)}, bf16[2,1024,256]{2,1,0:T(8,128)(2,1)}, u32[]{:S(2)}) copy-start(bf16[2,1024,256]{2,1,0:T(8,128)(2,1)} %refs_4_.7) | copy-start | bytes 3145732
  24.5 37.7 %copy-start.10 = (bf16[2,256,1024]{2,1,0:T(8,128)(2,1)S(1)}, bf16[2,256,1024]{2,1,0:T(8,128)(2,1)}, u32[]{:S(2)}) copy-start(bf16[2,256,1024]{2,1,0:T(8,128)(2,1)} %refs_8_.3) | copy-start | bytes 3145732
  24.5 5.8 %collective-permute-start.5 = (bf16[272,256]{1,0:T(8,128)(2,1)S(1)}, bf16[272,256]{1,0:T(8,128)(2,1)S(1)}, u32[]{:S(2)}, u32[]{:S(2)}) collective-permute-start(bf16[272,256]{1,0:T(8,128)(2,1)S(1)} %get-tuple-element.60), channel_id=1, source_target_pairs={{0,4},{4,0},{8,12},{12,8},{16,20},{20,16},{24,28},{28,24},{1,5},{5... | collective-permute-start | bytes 417800 | tf_op jit(solution)/shard_map/ppermute | solution.py:66
  27.4 35.8 %copy-start.2 = (bf16[2,1024,256]{2,1,0:T(8,128)(2,1)S(1)}, bf16[2,1024,256]{2,1,0:T(8,128)(2,1)}, u32[]{:S(2)}) copy-start(bf16[2,1024,256]{2,1,0:T(8,128)(2,1)} %refs_2_.13) | copy-start | bytes 3145732
  27.4 35.8 %copy-start.3 = (bf16[2,1024,256]{2,1,0:T(8,128)(2,1)S(1)}, bf16[2,1024,256]{2,1,0:T(8,128)(2,1)}, u32[]{:S(2)}) copy-start(bf16[2,1024,256]{2,1,0:T(8,128)(2,1)} %refs_3_.7) | copy-start | bytes 3145732
  30.4 5.5 %collective-permute-start.6 = (bf16[80,256]{1,0:T(8,128)(2,1)S(1)}, bf16[80,256]{1,0:T(8,128)(2,1)S(1)}, u32[]{:S(2)}, u32[]{:S(2)}) collective-permute-start(bf16[80,256]{1,0:T(8,128)(2,1)S(1)} %get-tuple-element.62), channel_id=1, source_target_pairs={{0,24},{4,28},{8,0},{12,4},{16,8},{20,12},{24,16},{28,20},{1,25},{... | collective-permute-start | bytes 122888 | tf_op jit(solution)/shard_map/ppermute | solution.py:44
  34.3 4.9 %collective-permute-start.7 = (bf16[80,256]{1,0:T(8,128)(2,1)S(1)}, bf16[80,256]{1,0:T(8,128)(2,1)S(1)}, u32[]{:S(2)}, u32[]{:S(2)}) collective-permute-start(bf16[80,256]{1,0:T(8,128)(2,1)S(1)} %get-tuple-element.63), channel_id=1, source_target_pairs={{0,16},{4,20},{8,24},{12,28},{16,0},{20,4},{24,8},{28,12},{1,17},{... | collective-permute-start | bytes 122888 | tf_op jit(solution)/shard_map/ppermute | solution.py:44
  34.3 5.8 %collective-permute-start.8 = (bf16[80,256]{1,0:T(8,128)(2,1)S(1)}, bf16[80,256]{1,0:T(8,128)(2,1)S(1)}, u32[]{:S(2)}, u32[]{:S(2)}) collective-permute-start(bf16[80,256]{1,0:T(8,128)(2,1)S(1)} %get-tuple-element.64), channel_id=1, source_target_pairs={{0,8},{4,12},{8,16},{12,20},{16,24},{20,28},{24,0},{28,4},{1,9},{5... | collective-permute-start | bytes 122888 | tf_op jit(solution)/shard_map/ppermute | solution.py:44
  40.7 1.4 %collective-permute-start.9 = (bf16[64,1024]{1,0:T(8,128)(2,1)S(1)}, bf16[64,1024]{1,0:T(8,128)(2,1)S(1)}, u32[]{:S(2)}, u32[]{:S(2)}) collective-permute-start(bf16[64,1024]{1,0:T(8,128)(2,1)S(1)} %shard_map.137.part), channel_id=1, source_target_pairs={{0,1},{1,0},{2,3},{3,2},{4,5},{5,4},{6,7},{7,6},{8,9},{9,8},{10,11... | collective-permute-start | bytes 393224 | tf_op jit(solution)/shard_map/ppermute | solution.py:415
  42.2 5.6 %collective-permute-start.10 = (bf16[64,1024]{1,0:T(8,128)(2,1)S(1)}, bf16[64,1024]{1,0:T(8,128)(2,1)S(1)}, u32[]{:S(2)}, u32[]{:S(2)}) collective-permute-start(bf16[64,1024]{1,0:T(8,128)(2,1)S(1)} %shard_map.138.refs_0_), channel_id=1, source_target_pairs={{0,2},{1,3},{2,0},{3,1},{4,6},{5,7},{6,4},{7,5},{8,10},{9,11},{10,... | collective-permute-start | bytes 393224 | tf_op jit(solution)/shard_map/ppermute | solution.py:415
  48.4 4.8 %collective-permute-start.13 = (bf16[64,512]{1,0:T(8,128)(2,1)S(1)}, bf16[64,512]{1,0:T(8,128)(2,1)S(1)}, u32[]{:S(2)}, u32[]{:S(2)}) collective-permute-start(bf16[64,512]{1,0:T(8,128)(2,1)S(1)} %get-tuple-element.67.refs_0_), channel_id=1, source_target_pairs={{0,24},{4,28},{8,0},{12,4},{16,8},{20,12},{24,16},{28,20},{1,25},{... | collective-permute-start | bytes 196616 | tf_op jit(solution)/shard_map/ppermute | solution.py:44
  49.1 7.3 %collective-permute-start.12 = (bf16[64,512]{1,0:T(8,128)(2,1)S(1)}, bf16[64,512]{1,0:T(8,128)(2,1)S(1)}, u32[]{:S(2)}, u32[]{:S(2)}) collective-permute-start(bf16[64,512]{1,0:T(8,128)(2,1)S(1)} %get-tuple-element.67.refs_0_), channel_id=1, source_target_pairs={{0,16},{4,20},{8,24},{12,28},{16,0},{20,4},{24,8},{28,12},{1,17},{... | collective-permute-start | bytes 196616 | tf_op jit(solution)/shard_map/ppermute | solution.py:44
  49.6 8.2 %collective-permute-start.11 = (bf16[64,512]{1,0:T(8,128)(2,1)S(1)}, bf16[64,512]{1,0:T(8,128)(2,1)S(1)}, u32[]{:S(2)}, u32[]{:S(2)}) collective-permute-start(bf16[64,512]{1,0:T(8,128)(2,1)S(1)} %get-tuple-element.67.refs_0_), channel_id=1, source_target_pairs={{0,8},{4,12},{8,16},{12,20},{16,24},{20,28},{24,0},{28,4},{1,9},{5... | collective-permute-start | bytes 196616 | tf_op jit(solution)/shard_map/ppermute | solution.py:44
  51.6 6.8 %collective-permute-start.14 = (bf16[64,512]{1,0:T(8,128)(2,1)S(1)}, bf16[64,512]{1,0:T(8,128)(2,1)S(1)}, u32[]{:S(2)}, u32[]{:S(2)}) collective-permute-start(bf16[64,512]{1,0:T(8,128)(2,1)S(1)} %get-tuple-element.67.refs_0_), channel_id=1, source_target_pairs={{0,4},{4,0},{8,12},{12,8},{16,20},{20,16},{24,28},{28,24},{1,5},{5... | collective-permute-start | bytes 196616 | tf_op jit(solution)/shard_map/ppermute | solution.py:66
  53.2 5.2 %collective-permute-start.17 = (bf16[64,512]{1,0:T(8,128)(2,1)S(1)}, bf16[64,512]{1,0:T(8,128)(2,1)S(1)}, u32[]{:S(2)}, u32[]{:S(2)}) collective-permute-start(bf16[64,512]{1,0:T(8,128)(2,1)S(1)} %collective-permute-done.13.refs_3_), channel_id=1, source_target_pairs={{0,4},{4,0},{8,12},{12,8},{16,20},{20,16},{24,28},{28,24},{1,5},{5... | collective-permute-start | bytes 196616 | tf_op jit(solution)/shard_map/ppermute | solution.py:66
  56.4 4.3 %collective-permute-start.16 = (bf16[64,512]{1,0:T(8,128)(2,1)S(1)}, bf16[64,512]{1,0:T(8,128)(2,1)S(1)}, u32[]{:S(2)}, u32[]{:S(2)}) collective-permute-start(bf16[64,512]{1,0:T(8,128)(2,1)S(1)} %collective-permute-done.12.refs_2_), channel_id=1, source_target_pairs={{0,4},{4,0},{8,12},{12,8},{16,20},{20,16},{24,28},{28,24},{1,5},{5... | collective-permute-start | bytes 196616 | tf_op jit(solution)/shard_map/ppermute | solution.py:66
  57.9 4.3 %collective-permute-start.15 = (bf16[64,512]{1,0:T(8,128)(2,1)S(1)}, bf16[64,512]{1,0:T(8,128)(2,1)S(1)}, u32[]{:S(2)}, u32[]{:S(2)}) collective-permute-start(bf16[64,512]{1,0:T(8,128)(2,1)S(1)} %collective-permute-done.11.refs_1_), channel_id=1, source_target_pairs={{0,4},{4,0},{8,12},{12,8},{16,20},{20,16},{24,28},{28,24},{1,5},{5... | collective-permute-start | bytes 196616 | tf_op jit(solution)/shard_map/ppermute | solution.py:66
  63.2 3.5 %collective-permute-start.18 = (bf16[64,1024]{1,0:T(8,128)(2,1)S(1)}, bf16[64,1024]{1,0:T(8,128)(2,1)S(1)}, u32[]{:S(2)}, u32[]{:S(2)}) collective-permute-start(bf16[64,1024]{1,0:T(8,128)(2,1)S(1)} %shard_map.140.part), channel_id=1, source_target_pairs={{0,1},{1,0},{2,3},{3,2},{4,5},{5,4},{6,7},{7,6},{8,9},{9,8},{10,11... | collective-permute-start | bytes 393224 | tf_op jit(solution)/shard_map/ppermute | solution.py:415
  64.6 18.1 %collective-permute-start.25 = (bf16[1024,256]{1,0:T(8,128)(2,1)S(1)}, bf16[1024,256]{1,0:T(8,128)(2,1)S(1)}, u32[]{:S(2)}, u32[]{:S(2)}) collective-permute-start(bf16[1024,256]{1,0:T(8,128)(2,1)S(1)} %get-tuple-element.74.refs_4_), channel_id=1, source_target_pairs={{0,4},{4,0},{8,12},{12,8},{16,20},{20,16},{24,28},{28,24},{1,5},{5... | collective-permute-start | bytes 1572872 | tf_op jit(solution)/shard_map/ppermute | solution.py:66
  65.4 24.8 %collective-permute-start.26 = (bf16[256,1024]{1,0:T(8,128)(2,1)S(1)}, bf16[256,1024]{1,0:T(8,128)(2,1)S(1)}, u32[]{:S(2)}, u32[]{:S(2)}) collective-permute-start(bf16[256,1024]{1,0:T(8,128)(2,1)S(1)} %get-tuple-element.75.refs_6_), channel_id=1, source_target_pairs={{0,4},{4,0},{8,12},{12,8},{16,20},{20,16},{24,28},{28,24},{1,5},{5... | collective-permute-start | bytes 1572872 | tf_op jit(solution)/shard_map/ppermute | solution.py:66
  66.8 5.4 %collective-permute-start.19 = (bf16[64,1024]{1,0:T(8,128)(2,1)S(1)}, bf16[64,1024]{1,0:T(8,128)(2,1)S(1)}, u32[]{:S(2)}, u32[]{:S(2)}) collective-permute-start(bf16[64,1024]{1,0:T(8,128)(2,1)S(1)} %shard_map.141.refs_0_), channel_id=1, source_target_pairs={{0,2},{1,3},{2,0},{3,1},{4,6},{5,7},{6,4},{7,5},{8,10},{9,11},{10,... | collective-permute-start | bytes 393224 | tf_op jit(solution)/shard_map/ppermute | solution.py:415
  73.2 1.4 %collective-permute-start.20 = (bf16[64,1024]{1,0:T(8,128)(2,1)S(1)}, bf16[64,1024]{1,0:T(8,128)(2,1)S(1)}, u32[]{:S(2)}, u32[]{:S(2)}) collective-permute-start(bf16[64,1024]{1,0:T(8,128)(2,1)S(1)} %get-tuple-element.69.part), channel_id=1, source_target_pairs={{0,1},{1,0},{2,3},{3,2},{4,5},{5,4},{6,7},{7,6},{8,9},{9,8},{10,11... | collective-permute-start | bytes 393224 | tf_op jit(solution)/shard_map/ppermute | solution.py:415
  74.6 5.6 %collective-permute-start.21 = (bf16[64,1024]{1,0:T(8,128)(2,1)S(1)}, bf16[64,1024]{1,0:T(8,128)(2,1)S(1)}, u32[]{:S(2)}, u32[]{:S(2)}) collective-permute-start(bf16[64,1024]{1,0:T(8,128)(2,1)S(1)} %shard_map.143.refs_0_), channel_id=1, source_target_pairs={{0,2},{1,3},{2,0},{3,1},{4,6},{5,7},{6,4},{7,5},{8,10},{9,11},{10,... | collective-permute-start | bytes 393224 | tf_op jit(solution)/shard_map/ppermute | solution.py:415
  80.6 9.6 %collective-permute-start.24 = (bf16[64,512]{1,0:T(8,128)(2,1)S(1)}, bf16[64,512]{1,0:T(8,128)(2,1)S(1)}, u32[]{:S(2)}, u32[]{:S(2)}) collective-permute-start(bf16[64,512]{1,0:T(8,128)(2,1)S(1)} %get-tuple-element.71.refs_0_), channel_id=1, source_target_pairs={{0,24},{4,28},{8,0},{12,4},{16,8},{20,12},{24,16},{28,20},{1,25},{... | collective-permute-start | bytes 196616 | tf_op jit(solution)/shard_map/ppermute | solution.py:44
  81.9 8.3 %collective-permute-start.23 = (bf16[64,512]{1,0:T(8,128)(2,1)S(1)}, bf16[64,512]{1,0:T(8,128)(2,1)S(1)}, u32[]{:S(2)}, u32[]{:S(2)}) collective-permute-start(bf16[64,512]{1,0:T(8,128)(2,1)S(1)} %get-tuple-element.71.refs_0_), channel_id=1, source_target_pairs={{0,16},{4,20},{8,24},{12,28},{16,0},{20,4},{24,8},{28,12},{1,17},{... | collective-permute-start | bytes 196616 | tf_op jit(solution)/shard_map/ppermute | solution.py:44
  81.9 8.3 %collective-permute-start.22 = (bf16[64,512]{1,0:T(8,128)(2,1)S(1)}, bf16[64,512]{1,0:T(8,128)(2,1)S(1)}, u32[]{:S(2)}, u32[]{:S(2)}) collective-permute-start(bf16[64,512]{1,0:T(8,128)(2,1)S(1)} %get-tuple-element.71.refs_0_), channel_id=1, source_target_pairs={{0,8},{4,12},{8,16},{12,20},{16,24},{20,28},{24,0},{28,4},{1,9},{5... | collective-permute-start | bytes 196616 | tf_op jit(solution)/shard_map/ppermute | solution.py:44
  93.5 4.0 %collective-permute-start.27 = (bf16[80,256]{1,0:T(8,128)(2,1)S(1)}, bf16[80,256]{1,0:T(8,128)(2,1)S(1)}, u32[]{:S(2)}, u32[]{:S(2)}) collective-permute-start(bf16[80,256]{1,0:T(8,128)(2,1)S(1)} %get-tuple-element.77), channel_id=1, source_target_pairs={{0,24},{4,28},{8,0},{12,4},{16,8},{20,12},{24,16},{28,20},{1,25},{... | collective-permute-start | bytes 122888 | tf_op jit(solution)/shard_map/ppermute | solution.py:44
  94.7 5.3 %collective-permute-start.28 = (bf16[80,256]{1,0:T(8,128)(2,1)S(1)}, bf16[80,256]{1,0:T(8,128)(2,1)S(1)}, u32[]{:S(2)}, u32[]{:S(2)}) collective-permute-start(bf16[80,256]{1,0:T(8,128)(2,1)S(1)} %get-tuple-element.78), channel_id=1, source_target_pairs={{0,16},{4,20},{8,24},{12,28},{16,0},{20,4},{24,8},{28,12},{1,17},{... | collective-permute-start | bytes 122888 | tf_op jit(solution)/shard_map/ppermute | solution.py:44
  94.7 5.8 %collective-permute-start.29 = (bf16[80,256]{1,0:T(8,128)(2,1)S(1)}, bf16[80,256]{1,0:T(8,128)(2,1)S(1)}, u32[]{:S(2)}, u32[]{:S(2)}) collective-permute-start(bf16[80,256]{1,0:T(8,128)(2,1)S(1)} %get-tuple-element.79), channel_id=1, source_target_pairs={{0,8},{4,12},{8,16},{12,20},{16,24},{20,28},{24,0},{28,4},{1,9},{5... | collective-permute-start | bytes 122888 | tf_op jit(solution)/shard_map/ppermute | solution.py:44
  101.2 1.4 %collective-permute-start.30 = (bf16[64,1024]{1,0:T(8,128)(2,1)S(1)}, bf16[64,1024]{1,0:T(8,128)(2,1)S(1)}, u32[]{:S(2)}, u32[]{:S(2)}) collective-permute-start(bf16[64,1024]{1,0:T(8,128)(2,1)S(1)} %shard_map.147.part), channel_id=1, source_target_pairs={{0,1},{1,0},{2,3},{3,2},{4,5},{5,4},{6,7},{7,6},{8,9},{9,8},{10,11... | collective-permute-start | bytes 393224 | tf_op jit(solution)/shard_map/ppermute | solution.py:415
  102.6 5.6 %collective-permute-start.31 = (bf16[64,1024]{1,0:T(8,128)(2,1)S(1)}, bf16[64,1024]{1,0:T(8,128)(2,1)S(1)}, u32[]{:S(2)}, u32[]{:S(2)}) collective-permute-start(bf16[64,1024]{1,0:T(8,128)(2,1)S(1)} %shard_map.148.refs_0_), channel_id=1, source_target_pairs={{0,2},{1,3},{2,0},{3,1},{4,6},{5,7},{6,4},{7,5},{8,10},{9,11},{10,... | collective-permute-start | bytes 393224 | tf_op jit(solution)/shard_map/ppermute | solution.py:415
  108.8 4.7 %collective-permute-start.34 = (bf16[64,512]{1,0:T(8,128)(2,1)S(1)}, bf16[64,512]{1,0:T(8,128)(2,1)S(1)}, u32[]{:S(2)}, u32[]{:S(2)}) collective-permute-start(bf16[64,512]{1,0:T(8,128)(2,1)S(1)} %get-tuple-element.82.refs_0_), channel_id=1, source_target_pairs={{0,24},{4,28},{8,0},{12,4},{16,8},{20,12},{24,16},{28,20},{1,25},{... | collective-permute-start | bytes 196616 | tf_op jit(solution)/shard_map/ppermute | solution.py:44
  110.2 6.8 %collective-permute-start.33 = (bf16[64,512]{1,0:T(8,128)(2,1)S(1)}, bf16[64,512]{1,0:T(8,128)(2,1)S(1)}, u32[]{:S(2)}, u32[]{:S(2)}) collective-permute-start(bf16[64,512]{1,0:T(8,128)(2,1)S(1)} %get-tuple-element.82.refs_0_), channel_id=1, source_target_pairs={{0,16},{4,20},{8,24},{12,28},{16,0},{20,4},{24,8},{28,12},{1,17},{... | collective-permute-start | bytes 196616 | tf_op jit(solution)/shard_map/ppermute | solution.py:44
  110.3 7.4 %collective-permute-start.32 = (bf16[64,512]{1,0:T(8,128)(2,1)S(1)}, bf16[64,512]{1,0:T(8,128)(2,1)S(1)}, u32[]{:S(2)}, u32[]{:S(2)}) collective-permute-start(bf16[64,512]{1,0:T(8,128)(2,1)S(1)} %get-tuple-element.82.refs_0_), channel_id=1, source_target_pairs={{0,8},{4,12},{8,16},{12,20},{16,24},{20,28},{24,0},{28,4},{1,9},{5... | collective-permute-start | bytes 196616 | tf_op jit(solution)/shard_map/ppermute | solution.py:44
  112.0 7.1 %collective-permute-start.35 = (bf16[64,512]{1,0:T(8,128)(2,1)S(1)}, bf16[64,512]{1,0:T(8,128)(2,1)S(1)}, u32[]{:S(2)}, u32[]{:S(2)}) collective-permute-start(bf16[64,512]{1,0:T(8,128)(2,1)S(1)} %get-tuple-element.82.refs_0_), channel_id=1, source_target_pairs={{0,4},{4,0},{8,12},{12,8},{16,20},{20,16},{24,28},{28,24},{1,5},{5... | collective-permute-start | bytes 196616 | tf_op jit(solution)/shard_map/ppermute | solution.py:66
  113.5 5.6 %collective-permute-start.38 = (bf16[64,512]{1,0:T(8,128)(2,1)S(1)}, bf16[64,512]{1,0:T(8,128)(2,1)S(1)}, u32[]{:S(2)}, u32[]{:S(2)}) collective-permute-start(bf16[64,512]{1,0:T(8,128)(2,1)S(1)} %collective-permute-done.34.refs_3_), channel_id=1, source_target_pairs={{0,4},{4,0},{8,12},{12,8},{16,20},{20,16},{24,28},{28,24},{1,5},{5... | collective-permute-start | bytes 196616 | tf_op jit(solution)/shard_map/ppermute | solution.py:66
  117.0 4.3 %collective-permute-start.37 = (bf16[64,512]{1,0:T(8,128)(2,1)S(1)}, bf16[64,512]{1,0:T(8,128)(2,1)S(1)}, u32[]{:S(2)}, u32[]{:S(2)}) collective-permute-start(bf16[64,512]{1,0:T(8,128)(2,1)S(1)} %collective-permute-done.33.refs_2_), channel_id=1, source_target_pairs={{0,4},{4,0},{8,12},{12,8},{16,20},{20,16},{24,28},{28,24},{1,5},{5... | collective-permute-start | bytes 196616 | tf_op jit(solution)/shard_map/ppermute | solution.py:66
  117.7 4.3 %collective-permute-start.36 = (bf16[64,512]{1,0:T(8,128)(2,1)S(1)}, bf16[64,512]{1,0:T(8,128)(2,1)S(1)}, u32[]{:S(2)}, u32[]{:S(2)}) collective-permute-start(bf16[64,512]{1,0:T(8,128)(2,1)S(1)} %collective-permute-done.32.refs_1_), channel_id=1, source_target_pairs={{0,4},{4,0},{8,12},{12,8},{16,20},{20,16},{24,28},{28,24},{1,5},{5... | collective-permute-start | bytes 196616 | tf_op jit(solution)/shard_map/ppermute | solution.py:66
  123.0 1.4 %collective-permute-start.39 = (bf16[64,1024]{1,0:T(8,128)(2,1)S(1)}, bf16[64,1024]{1,0:T(8,128)(2,1)S(1)}, u32[]{:S(2)}, u32[]{:S(2)}) collective-permute-start(bf16[64,1024]{1,0:T(8,128)(2,1)S(1)} %shard_map.150.part), channel_id=1, source_target_pairs={{0,1},{1,0},{2,3},{3,2},{4,5},{5,4},{6,7},{7,6},{8,9},{9,8},{10,11... | collective-permute-start | bytes 393224 | tf_op jit(solution)/shard_map/ppermute | solution.py:415
  124.5 5.6 %collective-permute-start.40 = (bf16[64,1024]{1,0:T(8,128)(2,1)S(1)}, bf16[64,1024]{1,0:T(8,128)(2,1)S(1)}, u32[]{:S(2)}, u32[]{:S(2)}) collective-permute-start(bf16[64,1024]{1,0:T(8,128)(2,1)S(1)} %shard_map.151.refs_0_), channel_id=1, source_target_pairs={{0,2},{1,3},{2,0},{3,1},{4,6},{5,7},{6,4},{7,5},{8,10},{9,11},{10,... | collective-permute-start | bytes 393224 | tf_op jit(solution)/shard_map/ppermute | solution.py:415
  131.1 1.5 %collective-permute-start.41 = (bf16[64,1024]{1,0:T(8,128)(2,1)S(1)}, bf16[64,1024]{1,0:T(8,128)(2,1)S(1)}, u32[]{:S(2)}, u32[]{:S(2)}) collective-permute-start(bf16[64,1024]{1,0:T(8,128)(2,1)S(1)} %get-tuple-element.84.part), channel_id=1, source_target_pairs={{0,1},{1,0},{2,3},{3,2},{4,5},{5,4},{6,7},{7,6},{8,9},{9,8},{10,11... | collective-permute-start | bytes 393224 | tf_op jit(solution)/shard_map/ppermute | solution.py:415
  131.2 5.9 %collective-permute-start.43 = (bf16[256,256]{1,0:T(8,128)(2,1)S(1)}, bf16[256,256]{1,0:T(8,128)(2,1)S(1)}, u32[]{:S(2)}, u32[]{:S(2)}) collective-permute-start(bf16[256,256]{1,0:T(8,128)(2,1)S(1)} %get-tuple-element.85.refs_2_), channel_id=1, source_target_pairs={{0,4},{4,0},{8,12},{12,8},{16,20},{20,16},{24,28},{28,24},{1,5},{5... | collective-permute-start | bytes 393224 | tf_op jit(solution)/shard_map/ppermute | solution.py:66
  132.6 5.6 %collective-permute-start.42 = (bf16[64,1024]{1,0:T(8,128)(2,1)S(1)}, bf16[64,1024]{1,0:T(8,128)(2,1)S(1)}, u32[]{:S(2)}, u32[]{:S(2)}) collective-permute-start(bf16[64,1024]{1,0:T(8,128)(2,1)S(1)} %shard_map.153.refs_0_), channel_id=1, source_target_pairs={{0,2},{1,3},{2,0},{3,1},{4,6},{5,7},{6,4},{7,5},{8,10},{9,11},{10,... | collective-permute-start | bytes 393224 | tf_op jit(solution)/shard_map/ppermute | solution.py:415
  (7 other events, 134.0 us)
